TPU v7x, 768 devices: a whole 4x8x12 slice. The times are simulated.
768 devices in a mesh: grp: 48 (over z, x), intra: 16 (over y, core).
Axes of the slice: x: 4, y: 8, z: 12, core: 2. Of those that a mesh axis runs over, the one named last changes fastest.
Arguments:
- normed: bfloat16 [98304, 4096], P(('grp', 'intra')), may hold values from -6 to 6
- cotangent: bfloat16 [98304, 1024], P(('grp', 'intra')), may hold values from -0.01953125 to 0.01953125
- norm_gain: float32 [4096], replicated, may hold values from 0.25 to 4
- weights: bfloat16 [4096, 1024], P('intra'), may hold values from -6 to 6
- row_state: float32 [48, 16, 4, 16], P('grp', 'intra'), may hold values from 0.05 to 20
- col_state: float32 [8, 128], replicated, may hold values from 0.3 to 10
- owner_table: int32 [128, 1], replicated, may hold values from 0 to 47; in each aligned block of 128 rows (0 to 127, 128 to 255, ...) at most 4 rows name the same one
Outputs:
- new_weights: bfloat16 [4096, 1024], P('intra')
- row_moments: float32 [48, 16, 4, 16], P('grp', 'intra')
- col_moments: float32 [8, 128], replicated
Inputs may be any that keep to these rules, and one draw needn't show every extreme that they name: `owner_table`: each group owns at most 4 units, some group exactly 4, and every group owns at least one.
All inputs are finite; a program needn't handle non-finite values.
Results may differ from a plain program's by a relative error of at most 0.013.
Values may be sent and summed in bfloat16 or wider, within the bound.
No kernel may reach another device: no remote copies, remote signals or barrier semaphores. Data moves between devices by JAX's collectives and lax.ppermute only.
A program may use at most 32 MiB of HBM per device.

v0:
```python
import functools

import jax
import jax.numpy as jnp
from jax import lax
from jax.experimental import pallas as pl
from jax.experimental.pallas import tpu as pltpu
from jax.sharding import PartitionSpec as P


decay_rate = 0.8
step_size = 0.5
epsilon = 1e-06

N_X = 4
CORES = 2


def arrange_kernel(slab, x_ref, gain_ref, mine_ref, theirs_ref):
    me = lax.axis_index("intra")
    my_y, my_core = me // CORES, me % CORES
    half = x_ref.shape[1] // (CORES * slab)
    n_y = 2 * half // CORES
    ahead = [n_y] + [2 * k + h for k in range(n_y // 2 - 1, 0, -1) for h in (0, 1)] + [1]
    behind = [n_y + 1] + [2 * k + h for k in range(n_y // 2 + 1, n_y) for h in (1, 0)] + [0]
    for out, up, down in ((theirs_ref, behind, ahead), (mine_ref, ahead, behind)):
        for u in range(half):
            piece = lax.rem(jnp.where(my_core == 0, up[u], down[u]) + 2 * my_y, 2 * half)
            column = pl.multiple_of(piece * slab, slab)
            block = x_ref[:, pl.ds(column, slab)].astype(jnp.float32)
            scaled = block * gain_ref[:, pl.ds(column, slab)]
            out[:, u * slab : (u + 1) * slab] = scaled.astype(out.dtype)


def arrange(x, gain, slab):
    tokens, d_model = x.shape
    half = jax.ShapeDtypeStruct((tokens, d_model // CORES), x.dtype)
    vmem = pl.BlockSpec(memory_space=pltpu.VMEM)
    return pl.pallas_call(
        functools.partial(arrange_kernel, slab),
        out_shape=(half, half),
        in_specs=[vmem, vmem],
        out_specs=(vmem, vmem),
        cost_estimate=pl.CostEstimate(
            flops=tokens * d_model, bytes_accessed=4 * tokens * d_model, transcendentals=0
        ),
        compiler_params=pltpu.CompilerParams(vmem_limit_bytes=12 << 20),
        name="arrange",
    )(x, gain)


def products_kernel(slab, begin, after, x_ref, xg_ref, c_ref, cg_ref, *outs):
    dims = (((0,), (0,)), ((), ()))
    for u, out in enumerate(outs[after:], begin):
        cols = slice(u * slab, (u + 1) * slab)
        total = lax.dot_general(
            x_ref[:, cols], c_ref[...], dims, preferred_element_type=jnp.float32
        ) + lax.dot_general(
            xg_ref[:, cols], cg_ref[...], dims, preferred_element_type=jnp.float32
        )
        out[...] = total.astype(out.dtype)


def products(mine, got, cot, cot_got, slab, begin, end, *after):
    tokens, _ = mine.shape
    width = cot.shape[1]
    count = end - begin
    vmem = pl.BlockSpec(memory_space=pltpu.VMEM)
    return pl.pallas_call(
        functools.partial(products_kernel, slab, begin, len(after)),
        out_shape=tuple(jax.ShapeDtypeStruct((slab, width), cot.dtype) for _ in range(count)),
        in_specs=[vmem] * 4 + [pl.BlockSpec(memory_space=pl.ANY)] * len(after),
        out_specs=tuple([vmem] * count),
        cost_estimate=pl.CostEstimate(
            flops=4 * tokens * count * slab * width,
            bytes_accessed=4 * count * slab * width,
            transcendentals=0,
        ),
        compiler_params=pltpu.CompilerParams(vmem_limit_bytes=16 << 20),
        name="products",
    )(mine, got, cot, cot_got, *after)


def finish_kernel(a_ref, b_ref, out_ref):
    head = out_ref.shape[2]
    slab = a_ref.shape[0]
    for t in range(a_ref.shape[1] // head):
        cols = slice(t * head, (t + 1) * head)
        total = a_ref[:, cols].astype(jnp.float32) + b_ref[:, cols].astype(jnp.float32)
        x, row = divmod(t * slab, out_ref.shape[1])
        out_ref[x, row : row + slab, :] = total.astype(out_ref.dtype)


def finish(a, b, head):
    vmem = pl.BlockSpec(memory_space=pltpu.VMEM)
    return pl.pallas_call(
        finish_kernel,
        out_shape=jax.ShapeDtypeStruct((N_X, a.size // (N_X * head), head), a.dtype),
        in_specs=[vmem, vmem],
        out_specs=vmem,
        cost_estimate=pl.CostEstimate(
            flops=a.size, bytes_accessed=6 * a.size, transcendentals=0
        ),
        compiler_params=pltpu.CompilerParams(vmem_limit_bytes=8 << 20),
        name="finish",
    )(a, b)


def on_device(normed, cotangent, norm_gain, weights, row_state, col_state, owner_table):
    bf16, f32 = jnp.bfloat16, jnp.float32
    groups = lax.axis_size("grp")
    intra = lax.axis_size("intra")
    n_y = intra // CORES
    n_z = groups // N_X
    _, d_model = normed.shape
    tensors, head = col_state.shape
    width = tensors * head
    capacity, unit_rows = row_state.shape[2:]
    slab = weights.shape[0]
    blocks = slab // unit_rows
    units = tensors * blocks

    x_groups = [[z * N_X + x for x in range(N_X)] for z in range(n_z)]
    z_groups = [[z * N_X + x for z in range(n_z)] for x in range(N_X)]

    my_group = lax.axis_index("grp")

    swap = [(i, i ^ 1) for i in range(intra)]
    cot_got = lax.ppermute(cotangent, "intra", swap)
    mine, theirs = arrange(normed, norm_gain[None, :], slab)
    got = lax.ppermute(theirs, "intra", swap)
    inputs = (mine, got, cotangent, cot_got, slab)
    parts = products(*inputs, 0, 1)
    parts = parts + products(*inputs, 1, mine.shape[1] // slab, parts[0])

    ring = [
        (y * CORES + c, ((y + 1 - 2 * c) % n_y) * CORES + c) for y in range(n_y) for c in range(CORES)
    ]

    def add(*terms):
        return sum(t.astype(f32) for t in terms)

    def hop(a):
        return lax.ppermute(a, "intra", ring)

    first, second = parts[0], parts[2]
    for k in range(1, len(parts) - 2, 2):
        first = add(hop(first), parts[k]).astype(bf16)
        if k > 1:
            second = add(hop(second), parts[k + 1]).astype(bf16)
    last = hop(first)
    give = add(hop(second), parts[-1]).astype(bf16)
    own = finish(last, lax.ppermute(give, "intra", swap), head)

    def to_units(a):
        return (
            a.reshape(blocks, unit_rows, tensors, head)
            .transpose(2, 0, 1, 3)
            .reshape(units, unit_rows, head)
        )

    per_x = units // N_X
    per_z = -(-per_x // n_z)
    got = lax.all_to_all(own, "grp", 0, 0, axis_index_groups=x_groups, tiled=True)
    summed = jnp.sum(got.astype(f32), axis=0).astype(bf16)
    summed = jnp.pad(summed, ((0, (per_z * n_z - per_x) * unit_rows), (0, 0)))
    got = lax.all_to_all(
        summed.reshape(n_z, per_z * unit_rows, head),
        "grp", 0, 0, axis_index_groups=z_groups, tiled=True,
    )
    chunk = jnp.sum(got.astype(f32), axis=0).astype(bf16)

    flat_state = row_state.reshape(1, capacity * unit_rows)
    high = flat_state.astype(bf16)
    low = (flat_state - high.astype(f32)).astype(bf16)
    state_row = jnp.concatenate([high, low], axis=1)
    state_width = state_row.shape[1]
    state_row = jnp.pad(state_row, ((0, unit_rows - 1), (0, head - state_width)))
    chunk = jnp.concatenate([chunk, state_row], axis=0)
    got = lax.all_to_all(
        jnp.broadcast_to(chunk[None], (n_z,) + chunk.shape),
        "grp", 0, 0, axis_index_groups=z_groups, tiled=True,
    )
    grads = got[:, : per_z * unit_rows].reshape(-1, head)[: per_x * unit_rows]
    states = got[:, per_z * unit_rows]
    pad = -n_z % unit_rows
    packed = jnp.concatenate([grads, jnp.pad(states, ((0, pad), (0, 0)))], axis=0)
    got = lax.all_to_all(
        jnp.broadcast_to(packed[None], (N_X,) + packed.shape),
        "grp", 0, 0, axis_index_groups=x_groups, tiled=True,
    )
    grad_units = got[:, : per_x * unit_rows].reshape(units, unit_rows, head).astype(f32)
    states = got[:, per_x * unit_rows : per_x * unit_rows + n_z]
    states = states.transpose(1, 0, 2).reshape(groups, head)
    half = capacity * unit_rows
    state_high = states[:, :half].reshape(groups * capacity, unit_rows)
    state_low = states[:, half : 2 * half].reshape(groups * capacity, unit_rows)

    owner = owner_table[:, 0]
    onehot = (owner[:, None] == jnp.arange(groups, dtype=jnp.int32)[None, :]).astype(jnp.int32)
    before = jnp.cumsum(onehot, axis=0) - onehot
    slot = jnp.sum(before * onehot, axis=1)
    place = owner * capacity + slot
    pick = (place[:, None] == jnp.arange(groups * capacity, dtype=jnp.int32)[None, :]).astype(bf16)
    prev = jnp.dot(pick, state_high, preferred_element_type=f32) + jnp.dot(
        pick, state_low, preferred_element_type=f32
    )

    squares = grad_units * grad_units
    row_mean = jnp.mean(squares, axis=2) + epsilon
    row_new = decay_rate * prev + (1.0 - decay_rate) * row_mean
    col_part = jnp.sum(squares.reshape(tensors, blocks * unit_rows, head), axis=1)
    row_part = jnp.sum(row_new.reshape(tensors, blocks * unit_rows), axis=1)
    stats = jnp.concatenate(
        [col_part, jnp.broadcast_to(row_part[:, None], (tensors, head))], axis=0
    )
    stats = lax.all_to_all(
        jnp.broadcast_to(stats[None], (intra,) + stats.shape), "intra", 0, 0, tiled=True
    )
    total = jnp.sum(stats, axis=0)
    col_total, row_total = total[:tensors], total[tensors:]
    col_new = decay_rate * col_state + (1.0 - decay_rate) * (col_total / d_model + epsilon)
    row_avg = row_total / d_model
    col_factor = col_new / row_avg
    variance = row_new.reshape(tensors, blocks * unit_rows, 1) * col_factor[:, None, :]
    weight_units = to_units(weights).reshape(tensors, blocks * unit_rows, head)
    updated = weight_units.astype(f32) - step_size * grad_units.reshape(
        tensors, blocks * unit_rows, head
    ) / jnp.sqrt(variance)
    new_weights = (
        updated.astype(bf16).transpose(1, 0, 2).reshape(slab, width)
    )

    mine = (
        place[None, :] == my_group * capacity + jnp.arange(capacity, dtype=jnp.int32)[:, None]
    )
    filled = jnp.any(mine, axis=1)
    own_mean = jnp.dot(mine.astype(f32), row_mean, precision=lax.Precision.HIGHEST)
    row_moments = jnp.where(
        filled[:, None], decay_rate * row_state[0, 0] + (1.0 - decay_rate) * own_mean, 0.0
    )
    return (new_weights, row_moments[None, None], col_new)


def solution(mesh):
    placed = (
        P(("grp", "intra"), None),
        P(("grp", "intra"), None),
        P(),
        P("intra", None),
        P("grp", "intra", None, None),
        P(),
        P(),
    )
    return jax.shard_map(
        on_device,
        mesh=mesh,
        in_specs=placed,
        out_specs=(P("intra", None), P("grp", "intra", None, None), P()),
        check_vma=False,
    )
```

profile of v0, /device:TPU:1, one launch (start us, length us, event | category | flops | bytes accessed | tf_op | source)
XLA Modules:
  0.0 161.0 jit_solution(5253132915747242033)
XLA Ops:
  2.8 12.4 %collective-permute-start = (bf16[128,2048]{1,0:T(8,128)(2,1)S(1)}, bf16[128,2048]{1,0:T(8,128)(2,1)S(1)}, u32[]{:S(2)}, u32[]{:S(2)}) collective-permute-start(bf16[128,2048]{1,0:T(8,128)(2,1)S(1)} %get-tuple-element.13), channel_id=1, source_target_pairs={{0,1},{1,0},{2,3},{3,2},{4,5},{5,4},{6,7},{7,6},{8,9},{9,8},{10,11... | collective-permute-start | bytes 1572872 | tf_op jit(solution)/shard_map/ppermute | solution.py:131
  15.2 1.9 %collective-permute-start.1 = (bf16[128,1024]{1,0:T(8,128)(2,1)S(1)}, bf16[128,1024]{1,0:T(8,128)(2,1)S(1)}, u32[]{:S(2)}, u32[]{:S(2)}) collective-permute-start(bf16[128,1024]{1,0:T(8,128)(2,1)S(1)} %copy-done.1), channel_id=1, source_target_pairs={{0,1},{1,0},{2,3},{3,2},{4,5},{5,4},{6,7},{7,6},{8,9},{9,8},{10,11... | collective-permute-start | bytes 786440 | tf_op jit(solution)/shard_map/ppermute | solution.py:129
  19.1 2.1 %products.3 = (bf16[256,1024]{1,0:T(8,128)(2,1)S(1)}, bf16[256,1024]{1,0:T(8,128)(2,1)S(1)}, bf16[256,1024]{1,0:T(8,128)(2,1)S(1)}, bf16[256,1024]{1,0:T(8,128)(...) custom-call(bf16[128,2048]{1,0:T(8,128)(2,1)S(1)} %get-tuple-element.12.x_ref,, ...), custom_call_target="tpu_custom_call" | custom-call | flops 939524096 | bytes 7340032 | tf_op jit(solution)/shard_map/products/pallas_call | solution.py:69
  25.0 6.4 %collective-permute-done.6 = bf16[256,1024]{1,0:T(8,128)(2,1)S(1)} collective-permute-done((bf16[256,1024]{1,0:T(8,128)(2,1)S(1)}, bf16[256,1024]{1,0:T(8,128)(2,1)S(1)}, u32[]{:S(2)}, u32[]{:S(2)}) %collective-permute-start.6) | collective-permute-done | bytes 524320 | tf_op jit(solution)/shard_map/ppermute | solution.py:144
  31.6 2.8 %collective-permute-start.7 = (bf16[256,1024]{1,0:T(8,128)(2,1)S(1)}, bf16[256,1024]{1,0:T(8,128)(2,1)S(1)}, u32[]{:S(2)}, u32[]{:S(2)}) collective-permute-start(bf16[256,1024]{1,0:T(8,128)(2,1)S(1)} %add_convert_fusion.2), channel_id=1, source_target_pairs={{0,2},{1,15},{2,4},{3,1},{4,6},{5,3},{6,8},{7,5},{8,10},{9,7},{10,... | collective-permute-start | bytes 1572872 | tf_op jit(solution)/shard_map/ppermute | solution.py:144
  34.4 2.6 %collective-permute-done.2 = bf16[256,1024]{1,0:T(8,128)(2,1)S(1)} collective-permute-done((bf16[256,1024]{1,0:T(8,128)(2,1)S(1)}, bf16[256,1024]{1,0:T(8,128)(2,1)S(1)}, u32[]{:S(2)}, u32[]{:S(2)}) %collective-permute-start.2) | collective-permute-done | bytes 524320 | tf_op jit(solution)/shard_map/ppermute | solution.py:144
  37.2 2.8 %collective-permute-start.3 = (bf16[256,1024]{1,0:T(8,128)(2,1)S(1)}, bf16[256,1024]{1,0:T(8,128)(2,1)S(1)}, u32[]{:S(2)}, u32[]{:S(2)}) collective-permute-start(bf16[256,1024]{1,0:T(8,128)(2,1)S(1)} %add_convert_fusion.5), channel_id=1, source_target_pairs={{0,2},{1,15},{2,4},{3,1},{4,6},{5,3},{6,8},{7,5},{8,10},{9,7},{10,... | collective-permute-start | bytes 1572872 | tf_op jit(solution)/shard_map/ppermute | solution.py:144
  40.0 2.6 %collective-permute-done.7 = bf16[256,1024]{1,0:T(8,128)(2,1)S(1)} collective-permute-done((bf16[256,1024]{1,0:T(8,128)(2,1)S(1)}, bf16[256,1024]{1,0:T(8,128)(2,1)S(1)}, u32[]{:S(2)}, u32[]{:S(2)}) %collective-permute-start.7) | collective-permute-done | bytes 524320 | tf_op jit(solution)/shard_map/ppermute | solution.py:144
  42.8 2.9 %collective-permute-start.8 = (bf16[256,1024]{1,0:T(8,128)(2,1)S(1)}, bf16[256,1024]{1,0:T(8,128)(2,1)S(1)}, u32[]{:S(2)}, u32[]{:S(2)}) collective-permute-start(bf16[256,1024]{1,0:T(8,128)(2,1)S(1)} %add_convert_fusion.1), channel_id=1, source_target_pairs={{0,2},{1,15},{2,4},{3,1},{4,6},{5,3},{6,8},{7,5},{8,10},{9,7},{10,... | collective-permute-start | bytes 1572872 | tf_op jit(solution)/shard_map/ppermute | solution.py:144
  45.7 2.5 %collective-permute-done.3 = bf16[256,1024]{1,0:T(8,128)(2,1)S(1)} collective-permute-done((bf16[256,1024]{1,0:T(8,128)(2,1)S(1)}, bf16[256,1024]{1,0:T(8,128)(2,1)S(1)}, u32[]{:S(2)}, u32[]{:S(2)}) %collective-permute-start.3) | collective-permute-done | bytes 524320 | tf_op jit(solution)/shard_map/ppermute | solution.py:144
  48.4 2.9 %collective-permute-start.4 = (bf16[256,1024]{1,0:T(8,128)(2,1)S(1)}, bf16[256,1024]{1,0:T(8,128)(2,1)S(1)}, u32[]{:S(2)}, u32[]{:S(2)}) collective-permute-start(bf16[256,1024]{1,0:T(8,128)(2,1)S(1)} %add_convert_fusion.4), channel_id=1, source_target_pairs={{0,2},{1,15},{2,4},{3,1},{4,6},{5,3},{6,8},{7,5},{8,10},{9,7},{10,... | collective-permute-start | bytes 1572872 | tf_op jit(solution)/shard_map/ppermute | solution.py:144
  51.4 2.5 %collective-permute-done.8 = bf16[256,1024]{1,0:T(8,128)(2,1)S(1)} collective-permute-done((bf16[256,1024]{1,0:T(8,128)(2,1)S(1)}, bf16[256,1024]{1,0:T(8,128)(2,1)S(1)}, u32[]{:S(2)}, u32[]{:S(2)}) %collective-permute-start.8) | collective-permute-done | bytes 524320 | tf_op jit(solution)/shard_map/ppermute | solution.py:144
  54.0 6.6 %collective-permute-start.9 = (bf16[256,1024]{1,0:T(8,128)(2,1)S(1)}, bf16[256,1024]{1,0:T(8,128)(2,1)S(1)}, u32[]{:S(2)}, u32[]{:S(2)}) collective-permute-start(bf16[256,1024]{1,0:T(8,128)(2,1)S(1)} %add_convert_fusion), channel_id=1, source_target_pairs={{0,1},{1,0},{2,3},{3,2},{4,5},{5,4},{6,7},{7,6},{8,9},{9,8},{10,11... | collective-permute-start | bytes 1572872 | tf_op jit(solution)/shard_map/ppermute | solution.py:153
  60.9 1.9 %collective-permute-start.5 = (bf16[256,1024]{1,0:T(8,128)(2,1)S(1)}, bf16[256,1024]{1,0:T(8,128)(2,1)S(1)}, u32[]{:S(2)}, u32[]{:S(2)}) collective-permute-start(bf16[256,1024]{1,0:T(8,128)(2,1)S(1)} %add_convert_fusion.3), channel_id=1, source_target_pairs={{0,2},{1,15},{2,4},{3,1},{4,6},{5,3},{6,8},{7,5},{8,10},{9,7},{10,... | collective-permute-start | bytes 1572872 | tf_op jit(solution)/shard_map/ppermute | solution.py:144
  62.8 8.3 %collective-permute-done.5.a_ref = bf16[256,1024]{1,0:T(8,128)(2,1)S(1)} collective-permute-done((bf16[256,1024]{1,0:T(8,128)(2,1)S(1)}, bf16[256,1024]{1,0:T(8,128)(2,1)S(1)}, u32[]{:S(2)}, u32[]{:S(2)}) %collective-permute-start.5) | collective-permute-done | bytes 524320 | tf_op jit(solution)/shard_map/ppermute | solution.py:144
  71.3 9.3 %all_to_all.25 = bf16[4,512,128]{2,1,0:T(8,128)(2,1)S(1)} all-to-all(bf16[4,512,128]{2,1,0:T(8,128)(2,1)S(1)} %finish.1), channel_id=1, replica_groups={{0,16,32,48},{64,80,96,112},{128,144,160,176},{192,208,224,240},{256,27..., dimensions={0} | all-to-all | bytes 1048576 | tf_op jit(solution)/shard_map/all_to_all | solution.py:164
  81.3 8.3 %all-to-all-start.1 = ((bf16[12,48,128]{2,1,0:T(8,128)(2,1)}), bf16[12,48,128]{2,1,0:T(8,128)(2,1)S(1)}, u32[]{:S(2)}, u32[]{:S(2)}) async-start(bf16[12,48,128]{2,1,0:T(8,128)(2,1)} %bitcast.3), calls=%async_computation.1 | async-start | bytes 294912 | tf_op jit(solution)/shard_map/all_to_all | solution.py:167
  89.9 10.6 %all-to-all-done.1 = bf16[12,48,128]{2,1,0:T(8,128)(2,1)S(1)} async-done(((bf16[12,48,128]{2,1,0:T(8,128)(2,1)}), bf16[12,48,128]{2,1,0:T(8,128)(2,1)S(1)}, u32[]{:S(2)}, u32[]{:S(2)}) %all-to-all-start.1) | async-done | bytes 147488 | tf_op jit(solution)/shard_map/all_to_all | solution.py:167
  101.2 3.5 %all-to-all-start.2 = ((bf16[12,64,128]{2,1,0:T(8,128)(2,1)}), bf16[12,64,128]{2,1,0:T(8,128)(2,1)S(1)}, u32[]{:S(2)}, u32[]{:S(2)}) async-start(bf16[12,64,128]{2,1,0:T(8,128)(2,1)} %broadcast_in_dim.21), calls=%async_computation.2 | async-start | bytes 393216 | tf_op jit(solution)/shard_map/all_to_all | solution.py:180
  105.8 10.9 %all-to-all-done.2 = bf16[12,64,128]{2,1,0:T(8,128)(2,1)S(1)} async-done(((bf16[12,64,128]{2,1,0:T(8,128)(2,1)}), bf16[12,64,128]{2,1,0:T(8,128)(2,1)S(1)}, u32[]{:S(2)}, u32[]{:S(2)}) %all-to-all-start.2) | async-done | bytes 196640 | tf_op jit(solution)/shard_map/all_to_all | solution.py:180
  117.6 4.3 %all-to-all-start.3 = ((bf16[4,528,128]{2,1,0:T(8,128)(2,1)}), bf16[4,528,128]{2,1,0:T(8,128)(2,1)}, u32[]{:S(2)}, u32[]{:S(2)}) async-start(bf16[4,528,128]{2,1,0:T(8,128)(2,1)} %broadcast_in_dim.22), calls=%async_computation.3 | async-start | bytes 1081344 | tf_op jit(solution)/shard_map/all_to_all | solution.py:188
  122.1 6.9 %all-to-all-done.3 = bf16[4,528,128]{2,1,0:T(8,128)(2,1)} async-done(((bf16[4,528,128]{2,1,0:T(8,128)(2,1)}), bf16[4,528,128]{2,1,0:T(8,128)(2,1)}, u32[]{:S(2)}, u32[]{:S(2)}) %all-to-all-start.3) | async-done | bytes 540704 | tf_op jit(solution)/shard_map/all_to_all | solution.py:188
  133.1 16.8 %all-to-all-start.4 = ((f32[16,16,128]{2,1,0:T(8,128)}), f32[16,16,128]{2,1,0:T(8,128)S(1)}, u32[]{:S(2)}, u32[]{:S(2)}) async-start(f32[16,16,128]{2,1,0:T(8,128)} %broadcast_in_dim.24), calls=%async_computation.4 | async-start | bytes 262144 | tf_op jit(solution)/shard_map/all_to_all | solution.py:217
  151.5 7.3 %all-to-all-done.4 = f32[16,16,128]{2,1,0:T(8,128)S(1)} async-done(((f32[16,16,128]{2,1,0:T(8,128)}), f32[16,16,128]{2,1,0:T(8,128)S(1)}, u32[]{:S(2)}, u32[]{:S(2)}) %all-to-all-start.4) | async-done | bytes 131104 | tf_op jit(solution)/shard_map/all_to_all | solution.py:217
  (78 shorter events, 20.8 us)
Async XLA Ops:
  0.6 1.2 copy-start
  1.9 0.7 copy-start.2
  2.6 12.6 %copy-start.1 = (bf16[128,1024]{1,0:T(8,128)(2,1)S(1)}, bf16[128,1024]{1,0:T(8,128)(2,1)}, u32[]{:S(2)}) copy-start(bf16[128,1024]{1,0:T(8,128)(2,1)} %c_ref.3) | copy-start | bytes 786436
  2.8 15.8 %collective-permute-start = (bf16[128,2048]{1,0:T(8,128)(2,1)S(1)}, bf16[128,2048]{1,0:T(8,128)(2,1)S(1)}, u32[]{:S(2)}, u32[]{:S(2)}) collective-permute-start(bf16[128,2048]{1,0:T(8,128)(2,1)S(1)} %get-tuple-element.13), channel_id=1, source_target_pairs={{0,1},{1,0},{2,3},{3,2},{4,5},{5,4},{6,7},{7,6},{8,9},{9,8},{10,11... | collective-permute-start | bytes 1572872 | tf_op jit(solution)/shard_map/ppermute | solution.py:131
  15.2 3.4 %collective-permute-start.1 = (bf16[128,1024]{1,0:T(8,128)(2,1)S(1)}, bf16[128,1024]{1,0:T(8,128)(2,1)S(1)}, u32[]{:S(2)}, u32[]{:S(2)}) collective-permute-start(bf16[128,1024]{1,0:T(8,128)(2,1)S(1)} %copy-done.1), channel_id=1, source_target_pairs={{0,1},{1,0},{2,3},{3,2},{4,5},{5,4},{6,7},{7,6},{8,9},{9,8},{10,11... | collective-permute-start | bytes 786440 | tf_op jit(solution)/shard_map/ppermute | solution.py:129
  21.1 10.2 %collective-permute-start.6 = (bf16[256,1024]{1,0:T(8,128)(2,1)S(1)}, bf16[256,1024]{1,0:T(8,128)(2,1)S(1)}, u32[]{:S(2)}, u32[]{:S(2)}) collective-permute-start(bf16[256,1024]{1,0:T(8,128)(2,1)S(1)} %get-tuple-element.17), channel_id=1, source_target_pairs={{0,2},{1,15},{2,4},{3,1},{4,6},{5,3},{6,8},{7,5},{8,10},{9,7},{10,... | collective-permute-start | bytes 1572872 | tf_op jit(solution)/shard_map/ppermute | solution.py:144
  23.1 13.9 %collective-permute-start.2 = (bf16[256,1024]{1,0:T(8,128)(2,1)S(1)}, bf16[256,1024]{1,0:T(8,128)(2,1)S(1)}, u32[]{:S(2)}, u32[]{:S(2)}) collective-permute-start(bf16[256,1024]{1,0:T(8,128)(2,1)S(1)} %products.2.outs_0_), channel_id=1, source_target_pairs={{0,2},{1,15},{2,4},{3,1},{4,6},{5,3},{6,8},{7,5},{8,10},{9,7},{10,... | collective-permute-start | bytes 1572872 | tf_op jit(solution)/shard_map/ppermute | solution.py:144
  31.6 11.0 %collective-permute-start.7 = (bf16[256,1024]{1,0:T(8,128)(2,1)S(1)}, bf16[256,1024]{1,0:T(8,128)(2,1)S(1)}, u32[]{:S(2)}, u32[]{:S(2)}) collective-permute-start(bf16[256,1024]{1,0:T(8,128)(2,1)S(1)} %add_convert_fusion.2), channel_id=1, source_target_pairs={{0,2},{1,15},{2,4},{3,1},{4,6},{5,3},{6,8},{7,5},{8,10},{9,7},{10,... | collective-permute-start | bytes 1572872 | tf_op jit(solution)/shard_map/ppermute | solution.py:144
  37.2 11.0 %collective-permute-start.3 = (bf16[256,1024]{1,0:T(8,128)(2,1)S(1)}, bf16[256,1024]{1,0:T(8,128)(2,1)S(1)}, u32[]{:S(2)}, u32[]{:S(2)}) collective-permute-start(bf16[256,1024]{1,0:T(8,128)(2,1)S(1)} %add_convert_fusion.5), channel_id=1, source_target_pairs={{0,2},{1,15},{2,4},{3,1},{4,6},{5,3},{6,8},{7,5},{8,10},{9,7},{10,... | collective-permute-start | bytes 1572872 | tf_op jit(solution)/shard_map/ppermute | solution.py:144
  42.8 11.0 %collective-permute-start.8 = (bf16[256,1024]{1,0:T(8,128)(2,1)S(1)}, bf16[256,1024]{1,0:T(8,128)(2,1)S(1)}, u32[]{:S(2)}, u32[]{:S(2)}) collective-permute-start(bf16[256,1024]{1,0:T(8,128)(2,1)S(1)} %add_convert_fusion.1), channel_id=1, source_target_pairs={{0,2},{1,15},{2,4},{3,1},{4,6},{5,3},{6,8},{7,5},{8,10},{9,7},{10,... | collective-permute-start | bytes 1572872 | tf_op jit(solution)/shard_map/ppermute | solution.py:144
  48.4 12.2 %collective-permute-start.4 = (bf16[256,1024]{1,0:T(8,128)(2,1)S(1)}, bf16[256,1024]{1,0:T(8,128)(2,1)S(1)}, u32[]{:S(2)}, u32[]{:S(2)}) collective-permute-start(bf16[256,1024]{1,0:T(8,128)(2,1)S(1)} %add_convert_fusion.4), channel_id=1, source_target_pairs={{0,2},{1,15},{2,4},{3,1},{4,6},{5,3},{6,8},{7,5},{8,10},{9,7},{10,... | collective-permute-start | bytes 1572872 | tf_op jit(solution)/shard_map/ppermute | solution.py:144
  54.0 8.8 %collective-permute-start.9 = (bf16[256,1024]{1,0:T(8,128)(2,1)S(1)}, bf16[256,1024]{1,0:T(8,128)(2,1)S(1)}, u32[]{:S(2)}, u32[]{:S(2)}) collective-permute-start(bf16[256,1024]{1,0:T(8,128)(2,1)S(1)} %add_convert_fusion), channel_id=1, source_target_pairs={{0,1},{1,0},{2,3},{3,2},{4,5},{5,4},{6,7},{7,6},{8,9},{9,8},{10,11... | collective-permute-start | bytes 1572872 | tf_op jit(solution)/shard_map/ppermute | solution.py:153
  60.9 10.2 %collective-permute-start.5 = (bf16[256,1024]{1,0:T(8,128)(2,1)S(1)}, bf16[256,1024]{1,0:T(8,128)(2,1)S(1)}, u32[]{:S(2)}, u32[]{:S(2)}) collective-permute-start(bf16[256,1024]{1,0:T(8,128)(2,1)S(1)} %add_convert_fusion.3), channel_id=1, source_target_pairs={{0,2},{1,15},{2,4},{3,1},{4,6},{5,3},{6,8},{7,5},{8,10},{9,7},{10,... | collective-permute-start | bytes 1572872 | tf_op jit(solution)/shard_map/ppermute | solution.py:144
  81.3 8.4 %copy-start.6 = (f32[1,1,4,16]{3,2,1,0:T(4,128)S(1)}, f32[1,1,4,16]{3,2,1,0:T(4,128)}, u32[]{:S(2)}) copy-start(f32[1,1,4,16]{3,2,1,0:T(4,128)} %param.11) | copy-start | bytes 772
  81.3 19.1 %all-to-all-start.1 = ((bf16[12,48,128]{2,1,0:T(8,128)(2,1)}), bf16[12,48,128]{2,1,0:T(8,128)(2,1)S(1)}, u32[]{:S(2)}, u32[]{:S(2)}) async-start(bf16[12,48,128]{2,1,0:T(8,128)(2,1)} %bitcast.3), calls=%async_computation.1 | async-start | bytes 294912 | tf_op jit(solution)/shard_map/all_to_all | solution.py:167
  101.2 15.5 %all-to-all-start.2 = ((bf16[12,64,128]{2,1,0:T(8,128)(2,1)}), bf16[12,64,128]{2,1,0:T(8,128)(2,1)S(1)}, u32[]{:S(2)}, u32[]{:S(2)}) async-start(bf16[12,64,128]{2,1,0:T(8,128)(2,1)} %broadcast_in_dim.21), calls=%async_computation.2 | async-start | bytes 393216 | tf_op jit(solution)/shard_map/all_to_all | solution.py:180
  104.7 0.7 copy-start.5
  117.6 4.3 %copy-start.3 = (bf16[256,1024]{1,0:T(8,128)(2,1)S(1)}, bf16[256,1024]{1,0:T(8,128)(2,1)}, u32[]{:S(2)}) copy-start(bf16[256,1024]{1,0:T(8,128)(2,1)} %param.10) | copy-start | bytes 1572868
  117.6 11.4 %all-to-all-start.3 = ((bf16[4,528,128]{2,1,0:T(8,128)(2,1)}), bf16[4,528,128]{2,1,0:T(8,128)(2,1)}, u32[]{:S(2)}, u32[]{:S(2)}) async-start(bf16[4,528,128]{2,1,0:T(8,128)(2,1)} %broadcast_in_dim.22), calls=%async_computation.3 | async-start | bytes 1081344 | tf_op jit(solution)/shard_map/all_to_all | solution.py:188
  133.1 25.7 %all-to-all-start.4 = ((f32[16,16,128]{2,1,0:T(8,128)}), f32[16,16,128]{2,1,0:T(8,128)S(1)}, u32[]{:S(2)}, u32[]{:S(2)}) async-start(f32[16,16,128]{2,1,0:T(8,128)} %broadcast_in_dim.24), calls=%async_computation.4 | async-start | bytes 262144 | tf_op jit(solution)/shard_map/all_to_all | solution.py:217
  151.5 7.3 %copy-start.4 = (f32[8,128]{1,0:T(8,128)S(1)}, f32[8,128]{1,0:T(8,128)}, u32[]{:S(2)}) copy-start(f32[8,128]{1,0:T(8,128)} %param.12) | copy-start | bytes 12292
where the time goes:
time: 162 us; the launch traced here: 161 us
  starting transfers between devices  71.1 us (44%)
  waiting for transfers between devices  61.9 us (38%)
  blocking collectives  9.33 us (6%)
  local copies, waits for them, and re-layouts  8.74 us (5%)
  other arithmetic  4.69 us (3%)
  Pallas kernels  2.89 us (2%)
    ppermute x7, waiting for transfers between devices, hop(): return lax.ppermute(a, 'intra', ring)  24.8 us
    ppermute x7, starting transfers between devices, hop(): return lax.ppermute(a, 'intra', ring)  17.3 us
    all_to_all x1, starting transfers between devices, on_device(): lax.all_to_all(jnp.broadcast_to(stats[None], (intra,) + stats.shape), 'in...  16.8 us
    ppermute x1, starting transfers between devices, on_device(): got = lax.ppermute(theirs, 'intra', swap)  12.4 us
    all_to_all x1, waiting for transfers between devices, on_device(): lax.all_to_all(jnp.broadcast_to(chunk[None], (n_z,) + chunk.shape), 'grp'...  10.9 us
    all_to_all x1, waiting for transfers between devices, on_device(): lax.all_to_all(summed.reshape(n_z, per_z * unit_rows, head), 'grp', 0, 0,...  10.6 us
    all_to_all x1, blocking collectives, on_device(): lax.all_to_all(own, 'grp', 0, 0, axis_index_groups=x_groups, tiled=True)  9.33 us
    all_to_all x1, starting transfers between devices, on_device(): lax.all_to_all(summed.reshape(n_z, per_z * unit_rows, head), 'grp', 0, 0,...  8.34 us
  transfers between devices with their start and end apart: 14, of which 11 were waited for; matrix products, arithmetic and copies ran while one was open for 2% of the time, Pallas kernels for 0%

commit v1 on v0

--- a/solution.py
+++ b/solution.py
@@ -106,6 +106,62 @@
     )(a, b)
 
 
+def small_kernel(body, out_shape, *operands):
+    vmem = pl.BlockSpec(memory_space=pltpu.VMEM)
+    size = sum(a.size for a in operands)
+    return pl.pallas_call(
+        body,
+        out_shape=out_shape,
+        in_specs=[vmem] * len(operands),
+        out_specs=jax.tree.map(lambda _: vmem, out_shape),
+        cost_estimate=pl.CostEstimate(flops=size, bytes_accessed=4 * size, transcendentals=0),
+        compiler_params=pltpu.CompilerParams(vmem_limit_bytes=8 << 20),
+    )(*operands)
+
+
+def total_of(ref, rows=slice(None)):
+    return sum(ref[j, rows, :].astype(jnp.float32) for j in range(ref.shape[0]))
+
+
+def sum_x_kernel(got_ref, out_ref):
+    rows = out_ref.shape[1]
+    for j in range(out_ref.shape[0]):
+        begin = min(j * rows, got_ref.shape[1])
+        end = min(begin + rows, got_ref.shape[1])
+        if end > begin:
+            out_ref[j, : end - begin, :] = total_of(got_ref, slice(begin, end)).astype(out_ref.dtype)
+        if end - begin < rows:
+            out_ref[j, end - begin :, :] = jnp.zeros(
+                (rows - end + begin, out_ref.shape[2]), out_ref.dtype
+            )
+
+
+def sum_z_kernel(got_ref, extra_ref, out_ref):
+    rows = got_ref.shape[1]
+    total = total_of(got_ref).astype(out_ref.dtype)
+    for j in range(out_ref.shape[0]):
+        out_ref[j, :rows, :] = total
+        out_ref[j, rows:, :] = extra_ref[...]
+
+
+def pack_kernel(rows, got_ref, out_ref):
+    count = got_ref.shape[0]
+    full = out_ref.shape[1] - (count + (-count) % 16)
+    for x in range(out_ref.shape[0]):
+        for j in range(count):
+            begin = min(j * rows, full)
+            end = min(begin + rows, full)
+            if end > begin:
+                out_ref[x, begin:end, :] = got_ref[j, : end - begin, :]
+    tail = jnp.concatenate(
+        [got_ref[j, rows : rows + 1, :].astype(jnp.float32) for j in range(count)]
+        + [jnp.zeros(((-count) % 16, got_ref.shape[2]), jnp.float32)],
+        axis=0,
+    ).astype(out_ref.dtype)
+    for x in range(out_ref.shape[0]):
+        out_ref[x, full:, :] = tail
+
+
 def on_device(normed, cotangent, norm_gain, weights, row_state, col_state, owner_table):
     bf16, f32 = jnp.bfloat16, jnp.float32
     groups = lax.axis_size("grp")
@@ -150,7 +206,8 @@
             second = add(hop(second), parts[k + 1]).astype(bf16)
     last = hop(first)
     give = add(hop(second), parts[-1]).astype(bf16)
-    own = finish(last, lax.ppermute(give, "intra", swap), head)
+    other = lax.ppermute(give, "intra", swap)
+    own = finish(last, other, head)
 
     def to_units(a):
         return (
@@ -162,13 +219,9 @@
     per_x = units // N_X
     per_z = -(-per_x // n_z)
     got = lax.all_to_all(own, "grp", 0, 0, axis_index_groups=x_groups, tiled=True)
-    summed = jnp.sum(got.astype(f32), axis=0).astype(bf16)
-    summed = jnp.pad(summed, ((0, (per_z * n_z - per_x) * unit_rows), (0, 0)))
-    got = lax.all_to_all(
-        summed.reshape(n_z, per_z * unit_rows, head),
-        "grp", 0, 0, axis_index_groups=z_groups, tiled=True,
-    )
-    chunk = jnp.sum(got.astype(f32), axis=0).astype(bf16)
+    sent = jax.ShapeDtypeStruct((n_z, per_z * unit_rows, head), bf16)
+    sent = small_kernel(sum_x_kernel, sent, got)
+    got = lax.all_to_all(sent, "grp", 0, 0, axis_index_groups=z_groups, tiled=True)
 
     flat_state = row_state.reshape(1, capacity * unit_rows)
     high = flat_state.astype(bf16)
@@ -176,19 +229,13 @@
     state_row = jnp.concatenate([high, low], axis=1)
     state_width = state_row.shape[1]
     state_row = jnp.pad(state_row, ((0, unit_rows - 1), (0, head - state_width)))
-    chunk = jnp.concatenate([chunk, state_row], axis=0)
-    got = lax.all_to_all(
-        jnp.broadcast_to(chunk[None], (n_z,) + chunk.shape),
-        "grp", 0, 0, axis_index_groups=z_groups, tiled=True,
-    )
-    grads = got[:, : per_z * unit_rows].reshape(-1, head)[: per_x * unit_rows]
-    states = got[:, per_z * unit_rows]
-    pad = -n_z % unit_rows
-    packed = jnp.concatenate([grads, jnp.pad(states, ((0, pad), (0, 0)))], axis=0)
-    got = lax.all_to_all(
-        jnp.broadcast_to(packed[None], (N_X,) + packed.shape),
-        "grp", 0, 0, axis_index_groups=x_groups, tiled=True,
-    )
+    sent = jax.ShapeDtypeStruct((n_z, got.shape[1] + unit_rows, head), bf16)
+    sent = small_kernel(sum_z_kernel, sent, got, state_row)
+    got = lax.all_to_all(sent, "grp", 0, 0, axis_index_groups=z_groups, tiled=True)
+    sent = jax.ShapeDtypeStruct((N_X, per_x * unit_rows + n_z + -n_z % unit_rows, head), bf16)
+    body = functools.partial(pack_kernel, per_z * unit_rows)
+    sent = small_kernel(body, sent, got)
+    got = lax.all_to_all(sent, "grp", 0, 0, axis_index_groups=x_groups, tiled=True)
     grad_units = got[:, : per_x * unit_rows].reshape(units, unit_rows, head).astype(f32)
     states = got[:, per_x * unit_rows : per_x * unit_rows + n_z]
     states = states.transpose(1, 0, 2).reshape(groups, head)

time: 162 us -> 161 us (level)
  Pallas kernels: 2.89 us -> 5.18 us
  local copies, waits for them, and re-layouts: 8.74 us -> 6.75 us
    pallas_call x0 -> x3, Pallas kernels: none -> 2.29 us  [small_kernel(): pl.pallas_call(body, out_shape=out_shape, in_specs=[vmem] * len(operands)...]
    unnamed x17 -> x15, local copies, waits for them, and re-layouts: 3.81 us -> 3.35 us
where the time goes in v1:
time: 161 us; the launch traced here: 160 us
  starting transfers between devices  70.9 us (44%)
  waiting for transfers between devices  61.3 us (38%)
  blocking collectives  9.33 us (6%)
  local copies, waits for them, and re-layouts  6.75 us (4%)
  Pallas kernels  5.18 us (3%)
  other arithmetic  4.57 us (3%)
    ppermute x7, waiting for transfers between devices, hop(): return lax.ppermute(a, 'intra', ring)  24.8 us
    all_to_all x2, waiting for transfers between devices, on_device(): lax.all_to_all(sent, 'grp', 0, 0, axis_index_groups=z_groups, tiled=True)  20.5 us
    ppermute x7, starting transfers between devices, hop(): return lax.ppermute(a, 'intra', ring)  17.3 us
    all_to_all x1, starting transfers between devices, on_device(): lax.all_to_all(jnp.broadcast_to(stats[None], (intra,) + stats.shape), 'in...  16.8 us
    ppermute x1, starting transfers between devices, on_device(): got = lax.ppermute(theirs, 'intra', swap)  12.4 us
    all_to_all x2, starting transfers between devices, on_device(): lax.all_to_all(sent, 'grp', 0, 0, axis_index_groups=z_groups, tiled=True)  11.7 us
    all_to_all x1, blocking collectives, on_device(): lax.all_to_all(own, 'grp', 0, 0, axis_index_groups=x_groups, tiled=True)  9.33 us
    all_to_all x1, waiting for transfers between devices, on_device(): lax.all_to_all(jnp.broadcast_to(stats[None], (intra,) + stats.shape), 'in...  7.5 us
  transfers between devices with their start and end apart: 14, of which 11 were waited for; matrix products, arithmetic and copies ran while one was open for 2% of the time, Pallas kernels for 0%

profile of v1, /device:TPU:1, one launch (start us, length us, event | category | flops | bytes accessed | tf_op | source)
XLA Modules:
  0.0 160.2 jit_solution(1967777691094859285)
XLA Ops:
  2.8 12.4 %collective-permute-start = (bf16[128,2048]{1,0:T(8,128)(2,1)S(1)}, bf16[128,2048]{1,0:T(8,128)(2,1)S(1)}, u32[]{:S(2)}, u32[]{:S(2)}) collective-permute-start(bf16[128,2048]{1,0:T(8,128)(2,1)S(1)} %get-tuple-element.13), channel_id=1, source_target_pairs={{0,1},{1,0},{2,3},{3,2},{4,5},{5,4},{6,7},{7,6},{8,9},{9,8},{10,11... | collective-permute-start | bytes 1572872 | tf_op jit(solution)/shard_map/ppermute | solution.py:187
  15.2 1.9 %collective-permute-start.1 = (bf16[128,1024]{1,0:T(8,128)(2,1)S(1)}, bf16[128,1024]{1,0:T(8,128)(2,1)S(1)}, u32[]{:S(2)}, u32[]{:S(2)}) collective-permute-start(bf16[128,1024]{1,0:T(8,128)(2,1)S(1)} %copy-done.1), channel_id=1, source_target_pairs={{0,1},{1,0},{2,3},{3,2},{4,5},{5,4},{6,7},{7,6},{8,9},{9,8},{10,11... | collective-permute-start | bytes 786440 | tf_op jit(solution)/shard_map/ppermute | solution.py:185
  19.1 2.1 %products.3 = (bf16[256,1024]{1,0:T(8,128)(2,1)S(1)}, bf16[256,1024]{1,0:T(8,128)(2,1)S(1)}, bf16[256,1024]{1,0:T(8,128)(2,1)S(1)}, bf16[256,1024]{1,0:T(8,128)(...) custom-call(bf16[128,2048]{1,0:T(8,128)(2,1)S(1)} %get-tuple-element.12.x_ref,, ...), custom_call_target="tpu_custom_call" | custom-call | flops 939524096 | bytes 7340032 | tf_op jit(solution)/shard_map/products/pallas_call | solution.py:69
  25.0 6.4 %collective-permute-done.6 = bf16[256,1024]{1,0:T(8,128)(2,1)S(1)} collective-permute-done((bf16[256,1024]{1,0:T(8,128)(2,1)S(1)}, bf16[256,1024]{1,0:T(8,128)(2,1)S(1)}, u32[]{:S(2)}, u32[]{:S(2)}) %collective-permute-start.6) | collective-permute-done | bytes 524320 | tf_op jit(solution)/shard_map/ppermute | solution.py:200
  31.6 2.8 %collective-permute-start.7 = (bf16[256,1024]{1,0:T(8,128)(2,1)S(1)}, bf16[256,1024]{1,0:T(8,128)(2,1)S(1)}, u32[]{:S(2)}, u32[]{:S(2)}) collective-permute-start(bf16[256,1024]{1,0:T(8,128)(2,1)S(1)} %add_convert_fusion.2), channel_id=1, source_target_pairs={{0,2},{1,15},{2,4},{3,1},{4,6},{5,3},{6,8},{7,5},{8,10},{9,7},{10,... | collective-permute-start | bytes 1572872 | tf_op jit(solution)/shard_map/ppermute | solution.py:200
  34.4 2.6 %collective-permute-done.2 = bf16[256,1024]{1,0:T(8,128)(2,1)S(1)} collective-permute-done((bf16[256,1024]{1,0:T(8,128)(2,1)S(1)}, bf16[256,1024]{1,0:T(8,128)(2,1)S(1)}, u32[]{:S(2)}, u32[]{:S(2)}) %collective-permute-start.2) | collective-permute-done | bytes 524320 | tf_op jit(solution)/shard_map/ppermute | solution.py:200
  37.2 2.8 %collective-permute-start.3 = (bf16[256,1024]{1,0:T(8,128)(2,1)S(1)}, bf16[256,1024]{1,0:T(8,128)(2,1)S(1)}, u32[]{:S(2)}, u32[]{:S(2)}) collective-permute-start(bf16[256,1024]{1,0:T(8,128)(2,1)S(1)} %add_convert_fusion.5), channel_id=1, source_target_pairs={{0,2},{1,15},{2,4},{3,1},{4,6},{5,3},{6,8},{7,5},{8,10},{9,7},{10,... | collective-permute-start | bytes 1572872 | tf_op jit(solution)/shard_map/ppermute | solution.py:200
  40.0 2.6 %collective-permute-done.7 = bf16[256,1024]{1,0:T(8,128)(2,1)S(1)} collective-permute-done((bf16[256,1024]{1,0:T(8,128)(2,1)S(1)}, bf16[256,1024]{1,0:T(8,128)(2,1)S(1)}, u32[]{:S(2)}, u32[]{:S(2)}) %collective-permute-start.7) | collective-permute-done | bytes 524320 | tf_op jit(solution)/shard_map/ppermute | solution.py:200
  42.8 2.9 %collective-permute-start.8 = (bf16[256,1024]{1,0:T(8,128)(2,1)S(1)}, bf16[256,1024]{1,0:T(8,128)(2,1)S(1)}, u32[]{:S(2)}, u32[]{:S(2)}) collective-permute-start(bf16[256,1024]{1,0:T(8,128)(2,1)S(1)} %add_convert_fusion.1), channel_id=1, source_target_pairs={{0,2},{1,15},{2,4},{3,1},{4,6},{5,3},{6,8},{7,5},{8,10},{9,7},{10,... | collective-permute-start | bytes 1572872 | tf_op jit(solution)/shard_map/ppermute | solution.py:200
  45.7 2.5 %collective-permute-done.3 = bf16[256,1024]{1,0:T(8,128)(2,1)S(1)} collective-permute-done((bf16[256,1024]{1,0:T(8,128)(2,1)S(1)}, bf16[256,1024]{1,0:T(8,128)(2,1)S(1)}, u32[]{:S(2)}, u32[]{:S(2)}) %collective-permute-start.3) | collective-permute-done | bytes 524320 | tf_op jit(solution)/shard_map/ppermute | solution.py:200
  48.4 2.9 %collective-permute-start.4 = (bf16[256,1024]{1,0:T(8,128)(2,1)S(1)}, bf16[256,1024]{1,0:T(8,128)(2,1)S(1)}, u32[]{:S(2)}, u32[]{:S(2)}) collective-permute-start(bf16[256,1024]{1,0:T(8,128)(2,1)S(1)} %add_convert_fusion.4), channel_id=1, source_target_pairs={{0,2},{1,15},{2,4},{3,1},{4,6},{5,3},{6,8},{7,5},{8,10},{9,7},{10,... | collective-permute-start | bytes 1572872 | tf_op jit(solution)/shard_map/ppermute | solution.py:200
  51.4 2.5 %collective-permute-done.8 = bf16[256,1024]{1,0:T(8,128)(2,1)S(1)} collective-permute-done((bf16[256,1024]{1,0:T(8,128)(2,1)S(1)}, bf16[256,1024]{1,0:T(8,128)(2,1)S(1)}, u32[]{:S(2)}, u32[]{:S(2)}) %collective-permute-start.8) | collective-permute-done | bytes 524320 | tf_op jit(solution)/shard_map/ppermute | solution.py:200
  54.0 6.6 %collective-permute-start.9 = (bf16[256,1024]{1,0:T(8,128)(2,1)S(1)}, bf16[256,1024]{1,0:T(8,128)(2,1)S(1)}, u32[]{:S(2)}, u32[]{:S(2)}) collective-permute-start(bf16[256,1024]{1,0:T(8,128)(2,1)S(1)} %add_convert_fusion), channel_id=1, source_target_pairs={{0,1},{1,0},{2,3},{3,2},{4,5},{5,4},{6,7},{7,6},{8,9},{9,8},{10,11... | collective-permute-start | bytes 1572872 | tf_op jit(solution)/shard_map/ppermute | solution.py:209
  60.9 1.9 %collective-permute-start.5 = (bf16[256,1024]{1,0:T(8,128)(2,1)S(1)}, bf16[256,1024]{1,0:T(8,128)(2,1)S(1)}, u32[]{:S(2)}, u32[]{:S(2)}) collective-permute-start(bf16[256,1024]{1,0:T(8,128)(2,1)S(1)} %add_convert_fusion.3), channel_id=1, source_target_pairs={{0,2},{1,15},{2,4},{3,1},{4,6},{5,3},{6,8},{7,5},{8,10},{9,7},{10,... | collective-permute-start | bytes 1572872 | tf_op jit(solution)/shard_map/ppermute | solution.py:200
  62.8 8.3 %collective-permute-done.5.a_ref = bf16[256,1024]{1,0:T(8,128)(2,1)S(1)} collective-permute-done((bf16[256,1024]{1,0:T(8,128)(2,1)S(1)}, bf16[256,1024]{1,0:T(8,128)(2,1)S(1)}, u32[]{:S(2)}, u32[]{:S(2)}) %collective-permute-start.5) | collective-permute-done | bytes 524320 | tf_op jit(solution)/shard_map/ppermute | solution.py:200
  71.3 9.3 %all_to_all.25.got_ref = bf16[4,512,128]{2,1,0:T(8,128)(2,1)S(1)} all-to-all(bf16[4,512,128]{2,1,0:T(8,128)(2,1)S(1)} %finish.1), channel_id=1, replica_groups={{0,16,32,48},{64,80,96,112},{128,144,160,176},{192,208,224,240},{256,27..., dimensions={0} | all-to-all | bytes 1048576 | tf_op jit(solution)/shard_map/all_to_all | solution.py:221
  81.3 8.2 %all-to-all-start.1 = ((bf16[12,48,128]{2,1,0:T(8,128)(2,1)}), bf16[12,48,128]{2,1,0:T(8,128)(2,1)S(1)}, u32[]{:S(2)}, u32[]{:S(2)}) async-start(bf16[12,48,128]{2,1,0:T(8,128)(2,1)} %shard_map.94), calls=%async_computation.1 | async-start | bytes 294912 | tf_op jit(solution)/shard_map/all_to_all | solution.py:224
  90.6 9.7 %all-to-all-done.1.got_ref = bf16[12,48,128]{2,1,0:T(8,128)(2,1)S(1)} async-done(((bf16[12,48,128]{2,1,0:T(8,128)(2,1)}), bf16[12,48,128]{2,1,0:T(8,128)(2,1)S(1)}, u32[]{:S(2)}, u32[]{:S(2)}) %all-to-all-start.1) | async-done | bytes 147488 | tf_op jit(solution)/shard_map/all_to_all | solution.py:224
  101.0 3.5 %all-to-all-start.2 = ((bf16[12,64,128]{2,1,0:T(8,128)(2,1)}), bf16[12,64,128]{2,1,0:T(8,128)(2,1)S(1)}, u32[]{:S(2)}, u32[]{:S(2)}) async-start(bf16[12,64,128]{2,1,0:T(8,128)(2,1)} %shard_map.95), calls=%async_computation.2 | async-start | bytes 393216 | tf_op jit(solution)/shard_map/all_to_all | solution.py:234
  105.6 10.9 %all-to-all-done.2.got_ref = bf16[12,64,128]{2,1,0:T(8,128)(2,1)S(1)} async-done(((bf16[12,64,128]{2,1,0:T(8,128)(2,1)}), bf16[12,64,128]{2,1,0:T(8,128)(2,1)S(1)}, u32[]{:S(2)}, u32[]{:S(2)}) %all-to-all-start.2) | async-done | bytes 196640 | tf_op jit(solution)/shard_map/all_to_all | solution.py:234
  117.3 4.1 %all-to-all-start.3 = ((bf16[4,528,128]{2,1,0:T(8,128)(2,1)}), bf16[4,528,128]{2,1,0:T(8,128)(2,1)}, u32[]{:S(2)}, u32[]{:S(2)}) async-start(bf16[4,528,128]{2,1,0:T(8,128)(2,1)} %shard_map.96), calls=%async_computation.3 | async-start | bytes 1081344 | tf_op jit(solution)/shard_map/all_to_all | solution.py:238
  121.6 7.0 %all-to-all-done.3 = bf16[4,528,128]{2,1,0:T(8,128)(2,1)} async-done(((bf16[4,528,128]{2,1,0:T(8,128)(2,1)}), bf16[4,528,128]{2,1,0:T(8,128)(2,1)}, u32[]{:S(2)}, u32[]{:S(2)}) %all-to-all-start.3) | async-done | bytes 540704 | tf_op jit(solution)/shard_map/all_to_all | solution.py:238
  132.7 16.8 %all-to-all-start.4 = ((f32[16,16,128]{2,1,0:T(8,128)}), f32[16,16,128]{2,1,0:T(8,128)S(1)}, u32[]{:S(2)}, u32[]{:S(2)}) async-start(f32[16,16,128]{2,1,0:T(8,128)} %broadcast_in_dim.18), calls=%async_computation.4 | async-start | bytes 262144 | tf_op jit(solution)/shard_map/all_to_all | solution.py:264
  150.8 7.5 %all-to-all-done.4 = f32[16,16,128]{2,1,0:T(8,128)S(1)} async-done(((f32[16,16,128]{2,1,0:T(8,128)}), f32[16,16,128]{2,1,0:T(8,128)S(1)}, u32[]{:S(2)}, u32[]{:S(2)}) %all-to-all-start.4) | async-done | bytes 131104 | tf_op jit(solution)/shard_map/all_to_all | solution.py:264
  (70 shorter events, 21.0 us)
Async XLA Ops:
  0.6 1.2 copy-start
  1.9 0.7 copy-start.2
  2.6 12.6 %copy-start.1 = (bf16[128,1024]{1,0:T(8,128)(2,1)S(1)}, bf16[128,1024]{1,0:T(8,128)(2,1)}, u32[]{:S(2)}) copy-start(bf16[128,1024]{1,0:T(8,128)(2,1)} %c_ref.3) | copy-start | bytes 786436
  2.8 15.8 %collective-permute-start = (bf16[128,2048]{1,0:T(8,128)(2,1)S(1)}, bf16[128,2048]{1,0:T(8,128)(2,1)S(1)}, u32[]{:S(2)}, u32[]{:S(2)}) collective-permute-start(bf16[128,2048]{1,0:T(8,128)(2,1)S(1)} %get-tuple-element.13), channel_id=1, source_target_pairs={{0,1},{1,0},{2,3},{3,2},{4,5},{5,4},{6,7},{7,6},{8,9},{9,8},{10,11... | collective-permute-start | bytes 1572872 | tf_op jit(solution)/shard_map/ppermute | solution.py:187
  15.2 3.4 %collective-permute-start.1 = (bf16[128,1024]{1,0:T(8,128)(2,1)S(1)}, bf16[128,1024]{1,0:T(8,128)(2,1)S(1)}, u32[]{:S(2)}, u32[]{:S(2)}) collective-permute-start(bf16[128,1024]{1,0:T(8,128)(2,1)S(1)} %copy-done.1), channel_id=1, source_target_pairs={{0,1},{1,0},{2,3},{3,2},{4,5},{5,4},{6,7},{7,6},{8,9},{9,8},{10,11... | collective-permute-start | bytes 786440 | tf_op jit(solution)/shard_map/ppermute | solution.py:185
  21.1 10.2 %collective-permute-start.6 = (bf16[256,1024]{1,0:T(8,128)(2,1)S(1)}, bf16[256,1024]{1,0:T(8,128)(2,1)S(1)}, u32[]{:S(2)}, u32[]{:S(2)}) collective-permute-start(bf16[256,1024]{1,0:T(8,128)(2,1)S(1)} %get-tuple-element.17), channel_id=1, source_target_pairs={{0,2},{1,15},{2,4},{3,1},{4,6},{5,3},{6,8},{7,5},{8,10},{9,7},{10,... | collective-permute-start | bytes 1572872 | tf_op jit(solution)/shard_map/ppermute | solution.py:200
  23.1 13.9 %collective-permute-start.2 = (bf16[256,1024]{1,0:T(8,128)(2,1)S(1)}, bf16[256,1024]{1,0:T(8,128)(2,1)S(1)}, u32[]{:S(2)}, u32[]{:S(2)}) collective-permute-start(bf16[256,1024]{1,0:T(8,128)(2,1)S(1)} %products.2.outs_0_), channel_id=1, source_target_pairs={{0,2},{1,15},{2,4},{3,1},{4,6},{5,3},{6,8},{7,5},{8,10},{9,7},{10,... | collective-permute-start | bytes 1572872 | tf_op jit(solution)/shard_map/ppermute | solution.py:200
  31.6 11.0 %collective-permute-start.7 = (bf16[256,1024]{1,0:T(8,128)(2,1)S(1)}, bf16[256,1024]{1,0:T(8,128)(2,1)S(1)}, u32[]{:S(2)}, u32[]{:S(2)}) collective-permute-start(bf16[256,1024]{1,0:T(8,128)(2,1)S(1)} %add_convert_fusion.2), channel_id=1, source_target_pairs={{0,2},{1,15},{2,4},{3,1},{4,6},{5,3},{6,8},{7,5},{8,10},{9,7},{10,... | collective-permute-start | bytes 1572872 | tf_op jit(solution)/shard_map/ppermute | solution.py:200
  37.2 11.0 %collective-permute-start.3 = (bf16[256,1024]{1,0:T(8,128)(2,1)S(1)}, bf16[256,1024]{1,0:T(8,128)(2,1)S(1)}, u32[]{:S(2)}, u32[]{:S(2)}) collective-permute-start(bf16[256,1024]{1,0:T(8,128)(2,1)S(1)} %add_convert_fusion.5), channel_id=1, source_target_pairs={{0,2},{1,15},{2,4},{3,1},{4,6},{5,3},{6,8},{7,5},{8,10},{9,7},{10,... | collective-permute-start | bytes 1572872 | tf_op jit(solution)/shard_map/ppermute | solution.py:200
  42.8 11.0 %collective-permute-start.8 = (bf16[256,1024]{1,0:T(8,128)(2,1)S(1)}, bf16[256,1024]{1,0:T(8,128)(2,1)S(1)}, u32[]{:S(2)}, u32[]{:S(2)}) collective-permute-start(bf16[256,1024]{1,0:T(8,128)(2,1)S(1)} %add_convert_fusion.1), channel_id=1, source_target_pairs={{0,2},{1,15},{2,4},{3,1},{4,6},{5,3},{6,8},{7,5},{8,10},{9,7},{10,... | collective-permute-start | bytes 1572872 | tf_op jit(solution)/shard_map/ppermute | solution.py:200
  48.4 12.2 %collective-permute-start.4 = (bf16[256,1024]{1,0:T(8,128)(2,1)S(1)}, bf16[256,1024]{1,0:T(8,128)(2,1)S(1)}, u32[]{:S(2)}, u32[]{:S(2)}) collective-permute-start(bf16[256,1024]{1,0:T(8,128)(2,1)S(1)} %add_convert_fusion.4), channel_id=1, source_target_pairs={{0,2},{1,15},{2,4},{3,1},{4,6},{5,3},{6,8},{7,5},{8,10},{9,7},{10,... | collective-permute-start | bytes 1572872 | tf_op jit(solution)/shard_map/ppermute | solution.py:200
  54.0 8.8 %collective-permute-start.9 = (bf16[256,1024]{1,0:T(8,128)(2,1)S(1)}, bf16[256,1024]{1,0:T(8,128)(2,1)S(1)}, u32[]{:S(2)}, u32[]{:S(2)}) collective-permute-start(bf16[256,1024]{1,0:T(8,128)(2,1)S(1)} %add_convert_fusion), channel_id=1, source_target_pairs={{0,1},{1,0},{2,3},{3,2},{4,5},{5,4},{6,7},{7,6},{8,9},{9,8},{10,11... | collective-permute-start | bytes 1572872 | tf_op jit(solution)/shard_map/ppermute | solution.py:209
  60.9 10.2 %collective-permute-start.5 = (bf16[256,1024]{1,0:T(8,128)(2,1)S(1)}, bf16[256,1024]{1,0:T(8,128)(2,1)S(1)}, u32[]{:S(2)}, u32[]{:S(2)}) collective-permute-start(bf16[256,1024]{1,0:T(8,128)(2,1)S(1)} %add_convert_fusion.3), channel_id=1, source_target_pairs={{0,2},{1,15},{2,4},{3,1},{4,6},{5,3},{6,8},{7,5},{8,10},{9,7},{10,... | collective-permute-start | bytes 1572872 | tf_op jit(solution)/shard_map/ppermute | solution.py:200
  80.6 8.9 %copy-start.3 = (bf16[256,1024]{1,0:T(8,128)(2,1)S(1)}, bf16[256,1024]{1,0:T(8,128)(2,1)}, u32[]{:S(2)}) copy-start(bf16[256,1024]{1,0:T(8,128)(2,1)} %param.10) | copy-start | bytes 1572868
  81.3 19.0 %all-to-all-start.1 = ((bf16[12,48,128]{2,1,0:T(8,128)(2,1)}), bf16[12,48,128]{2,1,0:T(8,128)(2,1)S(1)}, u32[]{:S(2)}, u32[]{:S(2)}) async-start(bf16[12,48,128]{2,1,0:T(8,128)(2,1)} %shard_map.94), calls=%async_computation.1 | async-start | bytes 294912 | tf_op jit(solution)/shard_map/all_to_all | solution.py:224
  89.5 0.7 copy-start.6
  101.0 15.5 %all-to-all-start.2 = ((bf16[12,64,128]{2,1,0:T(8,128)(2,1)}), bf16[12,64,128]{2,1,0:T(8,128)(2,1)S(1)}, u32[]{:S(2)}, u32[]{:S(2)}) async-start(bf16[12,64,128]{2,1,0:T(8,128)(2,1)} %shard_map.95), calls=%async_computation.2 | async-start | bytes 393216 | tf_op jit(solution)/shard_map/all_to_all | solution.py:234
  104.5 0.7 copy-start.5
  117.3 11.2 %all-to-all-start.3 = ((bf16[4,528,128]{2,1,0:T(8,128)(2,1)}), bf16[4,528,128]{2,1,0:T(8,128)(2,1)}, u32[]{:S(2)}, u32[]{:S(2)}) async-start(bf16[4,528,128]{2,1,0:T(8,128)(2,1)} %shard_map.96), calls=%async_computation.3 | async-start | bytes 1081344 | tf_op jit(solution)/shard_map/all_to_all | solution.py:238
  132.7 25.7 %all-to-all-start.4 = ((f32[16,16,128]{2,1,0:T(8,128)}), f32[16,16,128]{2,1,0:T(8,128)S(1)}, u32[]{:S(2)}, u32[]{:S(2)}) async-start(f32[16,16,128]{2,1,0:T(8,128)} %broadcast_in_dim.18), calls=%async_computation.4 | async-start | bytes 262144 | tf_op jit(solution)/shard_map/all_to_all | solution.py:264
  150.8 7.5 %copy-start.4 = (f32[8,128]{1,0:T(8,128)S(1)}, f32[8,128]{1,0:T(8,128)}, u32[]{:S(2)}) copy-start(f32[8,128]{1,0:T(8,128)} %param.12) | copy-start | bytes 12292

commit v2 on v1

--- a/solution.py
+++ b/solution.py
@@ -144,22 +144,69 @@
         out_ref[j, rows:, :] = extra_ref[...]
 
 
-def pack_kernel(rows, got_ref, out_ref):
-    count = got_ref.shape[0]
-    full = out_ref.shape[1] - (count + (-count) % 16)
-    for x in range(out_ref.shape[0]):
-        for j in range(count):
-            begin = min(j * rows, full)
-            end = min(begin + rows, full)
-            if end > begin:
-                out_ref[x, begin:end, :] = got_ref[j, : end - begin, :]
-    tail = jnp.concatenate(
-        [got_ref[j, rows : rows + 1, :].astype(jnp.float32) for j in range(count)]
-        + [jnp.zeros(((-count) % 16, got_ref.shape[2]), jnp.float32)],
-        axis=0,
-    ).astype(out_ref.dtype)
-    for x in range(out_ref.shape[0]):
-        out_ref[x, full:, :] = tail
+def pack_kernel(rows, got_ref, out_ref, stats_ref):
+    count, _, head = got_ref.shape
+    pad = -count % 16
+    full = out_ref.shape[0] - count - pad
+    cols = [jnp.zeros((1, head), jnp.float32)] * 2
+    for j in range(count):
+        begin = min(j * rows, full)
+        end = min(begin + rows, full)
+        if end > begin:
+            out_ref[begin:end, :] = got_ref[j, : end - begin, :]
+        for t in range(2):
+            low, high = max(begin, t * full // 2), min(end, (t + 1) * full // 2)
+            if high > low:
+                part = got_ref[j, low - begin : high - begin, :].astype(jnp.float32)
+                cols[t] = cols[t] + jnp.sum(part * part, axis=0, keepdims=True)
+    extra = [got_ref[j, rows : rows + 16, :].astype(jnp.float32) for j in range(count)]
+    tail = [e[:1] for e in extra] + [jnp.zeros((pad, head), jnp.float32)]
+    tail = jnp.concatenate(tail, axis=0).astype(out_ref.dtype)
+    out_ref[full:, :] = tail
+    sums = sum(e[1:2] for e in extra)
+    stats = cols + [sums, jnp.zeros((stats_ref.shape[1] - 3, head), jnp.float32)]
+    stats = jnp.concatenate(stats, axis=0)
+    for j in range(stats_ref.shape[0]):
+        stats_ref[j] = stats
+
+
+def rows_kernel(pick_ref, lane_ref, *refs):
+    *got, out_ref, mean_ref = refs
+    my_x = lax.axis_index("grp") % N_X
+    head = out_ref.shape[1]
+    full = out_ref.shape[0] // N_X
+    slab = full // 2
+    states = jnp.concatenate([ref[full:, :] for ref in got], axis=0)
+    for k, ref in enumerate(got):
+        for t in range(2):
+            begin = ((my_x + k) % N_X) * full + t * slab
+            where = pl.ds(pl.multiple_of(begin, slab), slab)
+            grad = ref[t * slab : (t + 1) * slab, :].astype(jnp.float32)
+            state = jnp.dot(pick_ref[where, :], states, preferred_element_type=jnp.float32)
+            prev = jnp.sum(state * lane_ref[where, :].astype(jnp.float32), axis=1, keepdims=True)
+            mean = jnp.sum(grad * grad, axis=1, keepdims=True) / head + epsilon
+            mean_ref[where, :] = jnp.broadcast_to(mean, (slab, mean_ref.shape[1]))
+            out_ref[where, :] = grad * lax.rsqrt(decay_rate * prev + (1.0 - decay_rate) * mean)
+
+
+def update_kernel(stats_ref, grad_ref, weight_ref, state_ref, out_ref, col_ref):
+    tensors, head = state_ref.shape
+    slab = weight_ref.shape[0]
+    d_model = slab * stats_ref.shape[0] // N_X
+    plane = stats_ref.shape[0] // N_X
+    sums = jnp.sum(stats_ref[:, 2, :], axis=0, keepdims=True)
+    for t in range(tensors):
+        x = t // 2
+        col = jnp.sum(stats_ref[x * plane : (x + 1) * plane, t % 2, :], axis=0, keepdims=True)
+        col = col / d_model + epsilon
+        col_new = decay_rate * state_ref[t : t + 1, :] + (1.0 - decay_rate) * col
+        col_ref[t : t + 1, :] = col_new
+        prev = (sums[:, t : t + 1] + sums[:, tensors + t : tensors + t + 1]) / d_model
+        average = decay_rate * prev + (1.0 - decay_rate) * jnp.mean(col, axis=1, keepdims=True)
+        factor = step_size * lax.rsqrt(col_new / average)
+        cols = slice(t * head, (t + 1) * head)
+        change = grad_ref[t * slab : (t + 1) * slab, :] * factor
+        out_ref[:, cols] = (weight_ref[:, cols].astype(jnp.float32) - change).astype(out_ref.dtype)
 
 
 def on_device(normed, cotangent, norm_gain, weights, row_state, col_state, owner_table):
@@ -168,9 +215,7 @@
     intra = lax.axis_size("intra")
     n_y = intra // CORES
     n_z = groups // N_X
-    _, d_model = normed.shape
     tensors, head = col_state.shape
-    width = tensors * head
     capacity, unit_rows = row_state.shape[2:]
     slab = weights.shape[0]
     blocks = slab // unit_rows
@@ -209,13 +254,6 @@
     other = lax.ppermute(give, "intra", swap)
     own = finish(last, other, head)
 
-    def to_units(a):
-        return (
-            a.reshape(blocks, unit_rows, tensors, head)
-            .transpose(2, 0, 1, 3)
-            .reshape(units, unit_rows, head)
-        )
-
     per_x = units // N_X
     per_z = -(-per_x // n_z)
     got = lax.all_to_all(own, "grp", 0, 0, axis_index_groups=x_groups, tiled=True)
@@ -223,65 +261,69 @@
     sent = small_kernel(sum_x_kernel, sent, got)
     got = lax.all_to_all(sent, "grp", 0, 0, axis_index_groups=z_groups, tiled=True)
 
-    flat_state = row_state.reshape(1, capacity * unit_rows)
-    high = flat_state.astype(bf16)
-    low = (flat_state - high.astype(f32)).astype(bf16)
-    state_row = jnp.concatenate([high, low], axis=1)
-    state_width = state_row.shape[1]
-    state_row = jnp.pad(state_row, ((0, unit_rows - 1), (0, head - state_width)))
-    sent = jax.ShapeDtypeStruct((n_z, got.shape[1] + unit_rows, head), bf16)
-    sent = small_kernel(sum_z_kernel, sent, got, state_row)
-    got = lax.all_to_all(sent, "grp", 0, 0, axis_index_groups=z_groups, tiled=True)
-    sent = jax.ShapeDtypeStruct((N_X, per_x * unit_rows + n_z + -n_z % unit_rows, head), bf16)
-    body = functools.partial(pack_kernel, per_z * unit_rows)
-    sent = small_kernel(body, sent, got)
-    got = lax.all_to_all(sent, "grp", 0, 0, axis_index_groups=x_groups, tiled=True)
-    grad_units = got[:, : per_x * unit_rows].reshape(units, unit_rows, head).astype(f32)
-    states = got[:, per_x * unit_rows : per_x * unit_rows + n_z]
-    states = states.transpose(1, 0, 2).reshape(groups, head)
-    half = capacity * unit_rows
-    state_high = states[:, :half].reshape(groups * capacity, unit_rows)
-    state_low = states[:, half : 2 * half].reshape(groups * capacity, unit_rows)
-
     owner = owner_table[:, 0]
     onehot = (owner[:, None] == jnp.arange(groups, dtype=jnp.int32)[None, :]).astype(jnp.int32)
     before = jnp.cumsum(onehot, axis=0) - onehot
     slot = jnp.sum(before * onehot, axis=1)
     place = owner * capacity + slot
-    pick = (place[:, None] == jnp.arange(groups * capacity, dtype=jnp.int32)[None, :]).astype(bf16)
-    prev = jnp.dot(pick, state_high, preferred_element_type=f32) + jnp.dot(
-        pick, state_low, preferred_element_type=f32
-    )
-
-    squares = grad_units * grad_units
-    row_mean = jnp.mean(squares, axis=2) + epsilon
-    row_new = decay_rate * prev + (1.0 - decay_rate) * row_mean
-    col_part = jnp.sum(squares.reshape(tensors, blocks * unit_rows, head), axis=1)
-    row_part = jnp.sum(row_new.reshape(tensors, blocks * unit_rows), axis=1)
-    stats = jnp.concatenate(
-        [col_part, jnp.broadcast_to(row_part[:, None], (tensors, head))], axis=0
-    )
-    stats = lax.all_to_all(
-        jnp.broadcast_to(stats[None], (intra,) + stats.shape), "intra", 0, 0, tiled=True
-    )
-    total = jnp.sum(stats, axis=0)
-    col_total, row_total = total[:tensors], total[tensors:]
-    col_new = decay_rate * col_state + (1.0 - decay_rate) * (col_total / d_model + epsilon)
-    row_avg = row_total / d_model
-    col_factor = col_new / row_avg
-    variance = row_new.reshape(tensors, blocks * unit_rows, 1) * col_factor[:, None, :]
-    weight_units = to_units(weights).reshape(tensors, blocks * unit_rows, head)
-    updated = weight_units.astype(f32) - step_size * grad_units.reshape(
-        tensors, blocks * unit_rows, head
-    ) / jnp.sqrt(variance)
-    new_weights = (
-        updated.astype(bf16).transpose(1, 0, 2).reshape(slab, width)
-    )
-
     mine = (
         place[None, :] == my_group * capacity + jnp.arange(capacity, dtype=jnp.int32)[:, None]
     )
     filled = jnp.any(mine, axis=1)
+
+    def two_parts(a):
+        high = a.astype(bf16)
+        return jnp.concatenate([high, (a - high.astype(f32)).astype(bf16)], axis=1)
+
+    state_sum = jnp.where(filled, jnp.sum(row_state[0, 0], axis=1), 0.0)
+    of_tensor = jnp.any(mine.reshape(capacity, tensors, blocks), axis=2)
+    sums = jnp.sum(jnp.where(of_tensor, state_sum[:, None], 0.0), axis=0)
+    half = capacity * unit_rows
+    rows = [two_parts(row_state.reshape(1, half)), two_parts(sums[None, :])]
+    rows = [jnp.pad(r, ((0, 0), (0, head - r.shape[1]))) for r in rows]
+    extra = jnp.concatenate(rows + [jnp.zeros((unit_rows - 2, head), bf16)], axis=0)
+    sent = jax.ShapeDtypeStruct((n_z, got.shape[1] + unit_rows, head), bf16)
+    sent = small_kernel(sum_z_kernel, sent, got, extra)
+    got = lax.all_to_all(sent, "grp", 0, 0, axis_index_groups=z_groups, tiled=True)
+    full = per_x * unit_rows
+    state_rows = n_z + -n_z % unit_rows
+    shapes = (
+        jax.ShapeDtypeStruct((full + state_rows, head), bf16),
+        jax.ShapeDtypeStruct((N_X * intra, 8, head), f32),
+    )
+    body = functools.partial(pack_kernel, per_z * unit_rows)
+    sent, stats = small_kernel(body, shapes, got)
+    plane = N_X * intra
+    planes = [list(range(z * plane, (z + 1) * plane)) for z in range(n_z)]
+    stats = lax.all_to_all(
+        stats, ("grp", "intra"), 0, 0, axis_index_groups=planes, tiled=True
+    )
+    fetched = [sent]
+    for k in range(1, N_X):
+        pairs = [
+            (z * N_X + (x + k) % N_X, z * N_X + x) for z in range(n_z) for x in range(N_X)
+        ]
+        fetched.append(lax.ppermute(sent, "grp", pairs))
+
+    seat = ((owner - my_group) % N_X) * state_rows + owner // N_X
+    pick = seat[:, None, None] == jnp.arange(N_X * state_rows, dtype=jnp.int32)
+    pick = jnp.broadcast_to(pick, (units, unit_rows, N_X * state_rows)).astype(bf16)
+    lane = slot[:, None, None] * unit_rows + jnp.arange(unit_rows, dtype=jnp.int32)[None, :, None]
+    lane = (lane == jnp.arange(head, dtype=jnp.int32) % half).astype(bf16)
+    count = units * unit_rows
+    shapes = (
+        jax.ShapeDtypeStruct((count, head), f32),
+        jax.ShapeDtypeStruct((count, 8), f32),
+    )
+    scaled, row_mean = small_kernel(
+        rows_kernel, shapes, pick.reshape(count, -1), lane.reshape(count, head), *fetched
+    )
+    shapes = (
+        jax.ShapeDtypeStruct(weights.shape, weights.dtype),
+        jax.ShapeDtypeStruct(col_state.shape, f32),
+    )
+    new_weights, col_new = small_kernel(update_kernel, shapes, stats, scaled, weights, col_state)
+    row_mean = row_mean[:, 0].reshape(units, unit_rows)
     own_mean = jnp.dot(mine.astype(f32), row_mean, precision=lax.Precision.HIGHEST)
     row_moments = jnp.where(
         filled[:, None], decay_rate * row_state[0, 0] + (1.0 - decay_rate) * own_mean, 0.0

time: 161 us -> 158 us (0.981)
  starting transfers between devices: 70.9 us -> 83.6 us
  blocking collectives: 9.33 us -> 0 us
  waiting for transfers between devices: 61.3 us -> 55.7 us
  local copies, waits for them, and re-layouts: 6.75 us -> 3.45 us
  Pallas kernels: 5.18 us -> 7.84 us
    ppermute x0 -> x3, starting transfers between devices: none -> 9.55 us  [on_device(): fetched.append(lax.ppermute(sent, 'grp', pairs))]
    all_to_all x1 -> x0, blocking collectives: 9.33 us -> none  [on_device(): lax.all_to_all(own, 'grp', 0, 0, axis_index_groups=x_groups, tiled=True)]
    all_to_all x2, waiting for transfers between devices: 14.5 us -> 6.64 us  [the longest x1 6.64 us: on_device(): lax.all_to_all(own, 'grp', 0, 0, axis_index_groups=x_groups, tiled=True)]
    ppermute x0 -> x3, waiting for transfers between devices: none -> 6.51 us  [on_device(): fetched.append(lax.ppermute(sent, 'grp', pairs))]
    ppermute x7, waiting for transfers between devices: 24.8 us -> 18.6 us  [hop(): return lax.ppermute(a, 'intra', ring)]
    ppermute x7, starting transfers between devices: 17.3 us -> 20.4 us  [hop(): return lax.ppermute(a, 'intra', ring)]
    all_to_all x2, waiting for transfers between devices: 20.5 us -> 22.4 us  [on_device(): lax.all_to_all(sent, 'grp', 0, 0, axis_index_groups=z_groups, tiled=True)]
    pallas_call x3 -> x5, Pallas kernels: 2.29 us -> 4.16 us  [small_kernel(): pl.pallas_call(body, out_shape=out_shape, in_specs=[vmem] * len(operands)...]
  transfers between devices with their start and end apart: 14 -> 17, of which waited for: 11 -> 11; matrix products, arithmetic and copies ran while one was open for 2% -> 4% of each run, Pallas kernels for 0% -> 0%
where the time goes in v2:
time: 158 us; the launch traced here: 157 us
  starting transfers between devices  83.6 us (53%)
  waiting for transfers between devices  55.7 us (35%)
  Pallas kernels  7.84 us (5%)
  other arithmetic  4.73 us (3%)
  local copies, waits for them, and re-layouts  3.45 us (2%)
    all_to_all x2, waiting for transfers between devices, on_device(): lax.all_to_all(sent, 'grp', 0, 0, axis_index_groups=z_groups, tiled=True)  22.4 us
    ppermute x7, starting transfers between devices, hop(): return lax.ppermute(a, 'intra', ring)  20.4 us
    ppermute x7, waiting for transfers between devices, hop(): return lax.ppermute(a, 'intra', ring)  18.6 us
    all_to_all x1, starting transfers between devices, on_device(): lax.all_to_all(stats, ('grp', 'intra'), 0, 0, axis_index_groups=planes, t...  16.8 us
    all_to_all x2, starting transfers between devices, on_device(): lax.all_to_all(sent, 'grp', 0, 0, axis_index_groups=z_groups, tiled=True)  13.2 us
    ppermute x1, starting transfers between devices, on_device(): got = lax.ppermute(theirs, 'intra', swap)  12.4 us
    ppermute x3, starting transfers between devices, on_device(): fetched.append(lax.ppermute(sent, 'grp', pairs))  9.55 us
    all_to_all x1, waiting for transfers between devices, on_device(): lax.all_to_all(own, 'grp', 0, 0, axis_index_groups=x_groups, tiled=True)  6.64 us
  transfers between devices with their start and end apart: 17, of which 11 were waited for; matrix products, arithmetic and copies ran while one was open for 4% of the time, Pallas kernels for 0%

profile of v2, /device:TPU:1, one launch (start us, length us, event | category | flops | bytes accessed | tf_op | source)
XLA Modules:
  0.0 157.1 jit_solution(9970263885563481033)
XLA Ops:
  2.8 12.4 %collective-permute-start = (bf16[128,2048]{1,0:T(8,128)(2,1)S(1)}, bf16[128,2048]{1,0:T(8,128)(2,1)S(1)}, u32[]{:S(2)}, u32[]{:S(2)}) collective-permute-start(bf16[128,2048]{1,0:T(8,128)(2,1)S(1)} %get-tuple-element.19), channel_id=1, source_target_pairs={{0,1},{1,0},{2,3},{3,2},{4,5},{5,4},{6,7},{7,6},{8,9},{9,8},{10,11... | collective-permute-start | bytes 1572872 | tf_op jit(solution)/shard_map/ppermute | solution.py:232
  19.1 2.1 %products.3 = (bf16[256,1024]{1,0:T(8,128)(2,1)S(1)}, bf16[256,1024]{1,0:T(8,128)(2,1)S(1)}, bf16[256,1024]{1,0:T(8,128)(2,1)S(1)}, bf16[256,1024]{1,0:T(8,128)(...) custom-call(bf16[128,2048]{1,0:T(8,128)(2,1)S(1)} %get-tuple-element.18.x_ref,, ...), custom_call_target="tpu_custom_call" | custom-call | flops 939524096 | bytes 7340032 | tf_op jit(solution)/shard_map/products/pallas_call | solution.py:69
  25.0 6.4 %collective-permute-done.6 = bf16[256,1024]{1,0:T(8,128)(2,1)S(1)} collective-permute-done((bf16[256,1024]{1,0:T(8,128)(2,1)S(1)}, bf16[256,1024]{1,0:T(8,128)(2,1)S(1)}, u32[]{:S(2)}, u32[]{:S(2)}) %collective-permute-start.6) | collective-permute-done | bytes 524320 | tf_op jit(solution)/shard_map/ppermute | solution.py:245
  31.6 2.8 %collective-permute-start.7 = (bf16[256,1024]{1,0:T(8,128)(2,1)S(1)}, bf16[256,1024]{1,0:T(8,128)(2,1)S(1)}, u32[]{:S(2)}, u32[]{:S(2)}) collective-permute-start(bf16[256,1024]{1,0:T(8,128)(2,1)S(1)} %add_convert_fusion.2), channel_id=1, source_target_pairs={{0,2},{1,15},{2,4},{3,1},{4,6},{5,3},{6,8},{7,5},{8,10},{9,7},{10,... | collective-permute-start | bytes 1572872 | tf_op jit(solution)/shard_map/ppermute | solution.py:245
  34.4 2.6 %collective-permute-done.2 = bf16[256,1024]{1,0:T(8,128)(2,1)S(1)} collective-permute-done((bf16[256,1024]{1,0:T(8,128)(2,1)S(1)}, bf16[256,1024]{1,0:T(8,128)(2,1)S(1)}, u32[]{:S(2)}, u32[]{:S(2)}) %collective-permute-start.2) | collective-permute-done | bytes 524320 | tf_op jit(solution)/shard_map/ppermute | solution.py:245
  38.0 3.0 %collective-permute-start.3 = (bf16[256,1024]{1,0:T(8,128)(2,1)}, bf16[256,1024]{1,0:T(8,128)(2,1)}, u32[]{:S(2)}, u32[]{:S(2)}) collective-permute-start(bf16[256,1024]{1,0:T(8,128)(2,1)} %add_convert_fusion.5), channel_id=1, source_target_pairs={{0,2},{1,15},{2,4},{3,1},{4,6},{5,3},{6,8},{7,5},{8,10},{9,7},{10,... | collective-permute-start | bytes 1572872 | tf_op jit(solution)/shard_map/ppermute | solution.py:245
  42.8 2.9 %collective-permute-start.8 = (bf16[256,1024]{1,0:T(8,128)(2,1)S(1)}, bf16[256,1024]{1,0:T(8,128)(2,1)S(1)}, u32[]{:S(2)}, u32[]{:S(2)}) collective-permute-start(bf16[256,1024]{1,0:T(8,128)(2,1)S(1)} %add_convert_fusion.1), channel_id=1, source_target_pairs={{0,2},{1,15},{2,4},{3,1},{4,6},{5,3},{6,8},{7,5},{8,10},{9,7},{10,... | collective-permute-start | bytes 1572872 | tf_op jit(solution)/shard_map/ppermute | solution.py:245
  45.7 2.9 %collective-permute-done.3 = bf16[256,1024]{1,0:T(8,128)(2,1)} collective-permute-done((bf16[256,1024]{1,0:T(8,128)(2,1)}, bf16[256,1024]{1,0:T(8,128)(2,1)}, u32[]{:S(2)}, u32[]{:S(2)}) %collective-permute-start.3) | collective-permute-done | bytes 524320 | tf_op jit(solution)/shard_map/ppermute | solution.py:245
  49.9 3.8 %collective-permute-start.4 = (bf16[256,1024]{1,0:T(8,128)(2,1)S(1)}, bf16[256,1024]{1,0:T(8,128)(2,1)S(1)}, u32[]{:S(2)}, u32[]{:S(2)}) collective-permute-start(bf16[256,1024]{1,0:T(8,128)(2,1)S(1)} %add_convert_fusion.4), channel_id=1, source_target_pairs={{0,2},{1,15},{2,4},{3,1},{4,6},{5,3},{6,8},{7,5},{8,10},{9,7},{10,... | collective-permute-start | bytes 1572872 | tf_op jit(solution)/shard_map/ppermute | solution.py:245
  54.8 5.9 %collective-permute-start.9 = (bf16[256,1024]{1,0:T(8,128)(2,1)S(1)}, bf16[256,1024]{1,0:T(8,128)(2,1)S(1)}, u32[]{:S(2)}, u32[]{:S(2)}) collective-permute-start(bf16[256,1024]{1,0:T(8,128)(2,1)S(1)} %add_convert_fusion), channel_id=1, source_target_pairs={{0,1},{1,0},{2,3},{3,2},{4,5},{5,4},{6,7},{7,6},{8,9},{9,8},{10,11... | collective-permute-start | bytes 1572872 | tf_op jit(solution)/shard_map/ppermute | solution.py:254
  60.9 4.1 %collective-permute-start.5 = (bf16[256,1024]{1,0:T(8,128)(2,1)S(1)}, bf16[256,1024]{1,0:T(8,128)(2,1)S(1)}, u32[]{:S(2)}, u32[]{:S(2)}) collective-permute-start(bf16[256,1024]{1,0:T(8,128)(2,1)S(1)} %add_convert_fusion.3), channel_id=1, source_target_pairs={{0,2},{1,15},{2,4},{3,1},{4,6},{5,3},{6,8},{7,5},{8,10},{9,7},{10,... | collective-permute-start | bytes 1572872 | tf_op jit(solution)/shard_map/ppermute | solution.py:245
  65.5 5.6 %collective-permute-done.5.a_ref = bf16[256,1024]{1,0:T(8,128)(2,1)S(1)} collective-permute-done((bf16[256,1024]{1,0:T(8,128)(2,1)S(1)}, bf16[256,1024]{1,0:T(8,128)(2,1)S(1)}, u32[]{:S(2)}, u32[]{:S(2)}) %collective-permute-start.5) | collective-permute-done | bytes 524320 | tf_op jit(solution)/shard_map/ppermute | solution.py:245
  72.0 3.5 %all-to-all-start = ((bf16[4,512,128]{2,1,0:T(8,128)(2,1)}), bf16[4,512,128]{2,1,0:T(8,128)(2,1)S(1)}, u32[]{:S(2)}, u32[]{:S(2)}) async-start(bf16[4,512,128]{2,1,0:T(8,128)(2,1)} %finish.1), calls=%async_computation | async-start | bytes 1048576 | tf_op jit(solution)/shard_map/all_to_all | solution.py:259
  75.8 6.6 %all-to-all-done.got_ref = bf16[4,512,128]{2,1,0:T(8,128)(2,1)S(1)} async-done(((bf16[4,512,128]{2,1,0:T(8,128)(2,1)}), bf16[4,512,128]{2,1,0:T(8,128)(2,1)S(1)}, u32[]{:S(2)}, u32[]{:S(2)}) %all-to-all-start) | async-done | bytes 524320 | tf_op jit(solution)/shard_map/all_to_all | solution.py:259
  83.1 9.6 %all-to-all-start.1 = ((bf16[12,48,128]{2,1,0:T(8,128)(2,1)}), bf16[12,48,128]{2,1,0:T(8,128)(2,1)S(1)}, u32[]{:S(2)}, u32[]{:S(2)}) async-start(bf16[12,48,128]{2,1,0:T(8,128)(2,1)} %shard_map.94), calls=%async_computation.1 | async-start | bytes 294912 | tf_op jit(solution)/shard_map/all_to_all | solution.py:262
  92.9 10.6 %all-to-all-done.1.got_ref = bf16[12,48,128]{2,1,0:T(8,128)(2,1)S(1)} async-done(((bf16[12,48,128]{2,1,0:T(8,128)(2,1)}), bf16[12,48,128]{2,1,0:T(8,128)(2,1)S(1)}, u32[]{:S(2)}, u32[]{:S(2)}) %all-to-all-start.1) | async-done | bytes 147488 | tf_op jit(solution)/shard_map/all_to_all | solution.py:262
  104.2 3.5 %all-to-all-start.2 = ((bf16[12,64,128]{2,1,0:T(8,128)(2,1)}), bf16[12,64,128]{2,1,0:T(8,128)(2,1)S(1)}, u32[]{:S(2)}, u32[]{:S(2)}) async-start(bf16[12,64,128]{2,1,0:T(8,128)(2,1)} %shard_map.95), calls=%async_computation.2 | async-start | bytes 393216 | tf_op jit(solution)/shard_map/all_to_all | solution.py:287
  108.0 11.8 %all-to-all-done.2.got_ref = bf16[12,64,128]{2,1,0:T(8,128)(2,1)S(1)} async-done(((bf16[12,64,128]{2,1,0:T(8,128)(2,1)}), bf16[12,64,128]{2,1,0:T(8,128)(2,1)S(1)}, u32[]{:S(2)}, u32[]{:S(2)}) %all-to-all-start.2) | async-done | bytes 196640 | tf_op jit(solution)/shard_map/all_to_all | solution.py:287
  120.5 16.8 %all-to-all-start.3 = ((f32[64,8,128]{2,1,0:T(8,128)}), f32[64,8,128]{2,1,0:T(8,128)S(1)}, u32[]{:S(2)}, u32[]{:S(2)}) async-start(f32[64,8,128]{2,1,0:T(8,128)} %get-tuple-element.27), calls=%async_computation.3 | async-start | bytes 524288 | tf_op jit(solution)/shard_map/all_to_all | solution.py:298
  137.6 4.7 %collective-permute-start.10 = (bf16[528,128]{1,0:T(8,128)(2,1)S(1)}, bf16[528,128]{1,0:T(8,128)(2,1)S(1)}, u32[]{:S(2)}, u32[]{:S(2)}) collective-permute-start(bf16[528,128]{1,0:T(8,128)(2,1)S(1)} %get-tuple-element.28.refs_0_), channel_id=1, source_target_pairs={{16,0},{32,16},{48,32},{0,48},{80,64},{96,80},{112,96},{64,112},{1... | collective-permute-start | bytes 405512 | tf_op jit(solution)/shard_map/ppermute | solution.py:306
  142.3 2.3 %collective-permute-start.11 = (bf16[528,128]{1,0:T(8,128)(2,1)S(1)}, bf16[528,128]{1,0:T(8,128)(2,1)S(1)}, u32[]{:S(2)}, u32[]{:S(2)}) collective-permute-start(bf16[528,128]{1,0:T(8,128)(2,1)S(1)} %get-tuple-element.28.refs_0_), channel_id=1, source_target_pairs={{32,0},{48,16},{0,32},{16,48},{96,64},{112,80},{64,96},{80,112},{1... | collective-permute-start | bytes 405512 | tf_op jit(solution)/shard_map/ppermute | solution.py:306
  144.6 2.6 %collective-permute-start.12 = (bf16[528,128]{1,0:T(8,128)(2,1)S(1)}, bf16[528,128]{1,0:T(8,128)(2,1)S(1)}, u32[]{:S(2)}, u32[]{:S(2)}) collective-permute-start(bf16[528,128]{1,0:T(8,128)(2,1)S(1)} %get-tuple-element.28.refs_0_), channel_id=1, source_target_pairs={{48,0},{0,16},{16,32},{32,48},{112,64},{64,80},{80,96},{96,112},{1... | collective-permute-start | bytes 405512 | tf_op jit(solution)/shard_map/ppermute | solution.py:306
  147.3 3.3 %collective-permute-done.11.refs_2_ = bf16[528,128]{1,0:T(8,128)(2,1)S(1)} collective-permute-done((bf16[528,128]{1,0:T(8,128)(2,1)S(1)}, bf16[528,128]{1,0:T(8,128)(2,1)S(1)}, u32[]{:S(2)}, u32[]{:S(2)}) %collective-permute-start.11) | collective-permute-done | bytes 135200 | tf_op jit(solution)/shard_map/ppermute | solution.py:306
  150.6 3.2 %collective-permute-done.12.refs_3_ = bf16[528,128]{1,0:T(8,128)(2,1)S(1)} collective-permute-done((bf16[528,128]{1,0:T(8,128)(2,1)S(1)}, bf16[528,128]{1,0:T(8,128)(2,1)S(1)}, u32[]{:S(2)}, u32[]{:S(2)}) %collective-permute-start.12) | collective-permute-done | bytes 135200 | tf_op jit(solution)/shard_map/ppermute | solution.py:306
  (70 shorter events, 23.2 us)
Async XLA Ops:
  0.6 1.2 copy-start
  1.9 0.7 copy-start.3
  2.6 12.6 %copy-start.2 = (bf16[128,1024]{1,0:T(8,128)(2,1)S(1)}, bf16[128,1024]{1,0:T(8,128)(2,1)}, u32[]{:S(2)}) copy-start(bf16[128,1024]{1,0:T(8,128)(2,1)} %c_ref.3) | copy-start | bytes 786436
  2.8 15.8 %collective-permute-start = (bf16[128,2048]{1,0:T(8,128)(2,1)S(1)}, bf16[128,2048]{1,0:T(8,128)(2,1)S(1)}, u32[]{:S(2)}, u32[]{:S(2)}) collective-permute-start(bf16[128,2048]{1,0:T(8,128)(2,1)S(1)} %get-tuple-element.19), channel_id=1, source_target_pairs={{0,1},{1,0},{2,3},{3,2},{4,5},{5,4},{6,7},{7,6},{8,9},{9,8},{10,11... | collective-permute-start | bytes 1572872 | tf_op jit(solution)/shard_map/ppermute | solution.py:232
  15.2 3.4 %collective-permute-start.1 = (bf16[128,1024]{1,0:T(8,128)(2,1)S(1)}, bf16[128,1024]{1,0:T(8,128)(2,1)S(1)}, u32[]{:S(2)}, u32[]{:S(2)}) collective-permute-start(bf16[128,1024]{1,0:T(8,128)(2,1)S(1)} %copy-done.2), channel_id=1, source_target_pairs={{0,1},{1,0},{2,3},{3,2},{4,5},{5,4},{6,7},{7,6},{8,9},{9,8},{10,11... | collective-permute-start | bytes 786440 | tf_op jit(solution)/shard_map/ppermute | solution.py:230
  21.1 10.2 %collective-permute-start.6 = (bf16[256,1024]{1,0:T(8,128)(2,1)S(1)}, bf16[256,1024]{1,0:T(8,128)(2,1)S(1)}, u32[]{:S(2)}, u32[]{:S(2)}) collective-permute-start(bf16[256,1024]{1,0:T(8,128)(2,1)S(1)} %get-tuple-element.23), channel_id=1, source_target_pairs={{0,2},{1,15},{2,4},{3,1},{4,6},{5,3},{6,8},{7,5},{8,10},{9,7},{10,... | collective-permute-start | bytes 1572872 | tf_op jit(solution)/shard_map/ppermute | solution.py:245
  23.1 13.9 %collective-permute-start.2 = (bf16[256,1024]{1,0:T(8,128)(2,1)S(1)}, bf16[256,1024]{1,0:T(8,128)(2,1)S(1)}, u32[]{:S(2)}, u32[]{:S(2)}) collective-permute-start(bf16[256,1024]{1,0:T(8,128)(2,1)S(1)} %products.2.outs_0_), channel_id=1, source_target_pairs={{0,2},{1,15},{2,4},{3,1},{4,6},{5,3},{6,8},{7,5},{8,10},{9,7},{10,... | collective-permute-start | bytes 1572872 | tf_op jit(solution)/shard_map/ppermute | solution.py:245
  31.6 11.0 %collective-permute-start.7 = (bf16[256,1024]{1,0:T(8,128)(2,1)S(1)}, bf16[256,1024]{1,0:T(8,128)(2,1)S(1)}, u32[]{:S(2)}, u32[]{:S(2)}) collective-permute-start(bf16[256,1024]{1,0:T(8,128)(2,1)S(1)} %add_convert_fusion.2), channel_id=1, source_target_pairs={{0,2},{1,15},{2,4},{3,1},{4,6},{5,3},{6,8},{7,5},{8,10},{9,7},{10,... | collective-permute-start | bytes 1572872 | tf_op jit(solution)/shard_map/ppermute | solution.py:245
  38.0 3.0 %copy-start.6 = (s32[128,1]{0,1:T(1,128)S(1)}, s32[128,1]{0,1:T(1,128)}, u32[]{:S(2)}) copy-start(s32[128,1]{0,1:T(1,128)} %param.13) | copy-start | bytes 1540
  38.0 10.7 %collective-permute-start.3 = (bf16[256,1024]{1,0:T(8,128)(2,1)}, bf16[256,1024]{1,0:T(8,128)(2,1)}, u32[]{:S(2)}, u32[]{:S(2)}) collective-permute-start(bf16[256,1024]{1,0:T(8,128)(2,1)} %add_convert_fusion.5), channel_id=1, source_target_pairs={{0,2},{1,15},{2,4},{3,1},{4,6},{5,3},{6,8},{7,5},{8,10},{9,7},{10,... | collective-permute-start | bytes 1572872 | tf_op jit(solution)/shard_map/ppermute | solution.py:245
  42.8 11.8 %collective-permute-start.8 = (bf16[256,1024]{1,0:T(8,128)(2,1)S(1)}, bf16[256,1024]{1,0:T(8,128)(2,1)S(1)}, u32[]{:S(2)}, u32[]{:S(2)}) collective-permute-start(bf16[256,1024]{1,0:T(8,128)(2,1)S(1)} %add_convert_fusion.1), channel_id=1, source_target_pairs={{0,2},{1,15},{2,4},{3,1},{4,6},{5,3},{6,8},{7,5},{8,10},{9,7},{10,... | collective-permute-start | bytes 1572872 | tf_op jit(solution)/shard_map/ppermute | solution.py:245
  49.9 10.8 %collective-permute-start.4 = (bf16[256,1024]{1,0:T(8,128)(2,1)S(1)}, bf16[256,1024]{1,0:T(8,128)(2,1)S(1)}, u32[]{:S(2)}, u32[]{:S(2)}) collective-permute-start(bf16[256,1024]{1,0:T(8,128)(2,1)S(1)} %add_convert_fusion.4), channel_id=1, source_target_pairs={{0,2},{1,15},{2,4},{3,1},{4,6},{5,3},{6,8},{7,5},{8,10},{9,7},{10,... | collective-permute-start | bytes 1572872 | tf_op jit(solution)/shard_map/ppermute | solution.py:245
  53.7 0.7 copy-start.5
  54.8 10.7 %collective-permute-start.9 = (bf16[256,1024]{1,0:T(8,128)(2,1)S(1)}, bf16[256,1024]{1,0:T(8,128)(2,1)S(1)}, u32[]{:S(2)}, u32[]{:S(2)}) collective-permute-start(bf16[256,1024]{1,0:T(8,128)(2,1)S(1)} %add_convert_fusion), channel_id=1, source_target_pairs={{0,1},{1,0},{2,3},{3,2},{4,5},{5,4},{6,7},{7,6},{8,9},{9,8},{10,11... | collective-permute-start | bytes 1572872 | tf_op jit(solution)/shard_map/ppermute | solution.py:254
  60.9 10.2 %collective-permute-start.5 = (bf16[256,1024]{1,0:T(8,128)(2,1)S(1)}, bf16[256,1024]{1,0:T(8,128)(2,1)S(1)}, u32[]{:S(2)}, u32[]{:S(2)}) collective-permute-start(bf16[256,1024]{1,0:T(8,128)(2,1)S(1)} %add_convert_fusion.3), channel_id=1, source_target_pairs={{0,2},{1,15},{2,4},{3,1},{4,6},{5,3},{6,8},{7,5},{8,10},{9,7},{10,... | collective-permute-start | bytes 1572872 | tf_op jit(solution)/shard_map/ppermute | solution.py:245
  72.0 10.4 %all-to-all-start = ((bf16[4,512,128]{2,1,0:T(8,128)(2,1)}), bf16[4,512,128]{2,1,0:T(8,128)(2,1)S(1)}, u32[]{:S(2)}, u32[]{:S(2)}) async-start(bf16[4,512,128]{2,1,0:T(8,128)(2,1)} %finish.1), calls=%async_computation | async-start | bytes 1048576 | tf_op jit(solution)/shard_map/all_to_all | solution.py:259
  83.1 20.4 %all-to-all-start.1 = ((bf16[12,48,128]{2,1,0:T(8,128)(2,1)}), bf16[12,48,128]{2,1,0:T(8,128)(2,1)S(1)}, u32[]{:S(2)}, u32[]{:S(2)}) async-start(bf16[12,48,128]{2,1,0:T(8,128)(2,1)} %shard_map.94), calls=%async_computation.1 | async-start | bytes 294912 | tf_op jit(solution)/shard_map/all_to_all | solution.py:262
  104.2 15.5 %all-to-all-start.2 = ((bf16[12,64,128]{2,1,0:T(8,128)(2,1)}), bf16[12,64,128]{2,1,0:T(8,128)(2,1)S(1)}, u32[]{:S(2)}, u32[]{:S(2)}) async-start(bf16[12,64,128]{2,1,0:T(8,128)(2,1)} %shard_map.95), calls=%async_computation.2 | async-start | bytes 393216 | tf_op jit(solution)/shard_map/all_to_all | solution.py:287
  120.5 35.3 %all-to-all-start.3 = ((f32[64,8,128]{2,1,0:T(8,128)}), f32[64,8,128]{2,1,0:T(8,128)S(1)}, u32[]{:S(2)}, u32[]{:S(2)}) async-start(f32[64,8,128]{2,1,0:T(8,128)} %get-tuple-element.27), calls=%async_computation.3 | async-start | bytes 524288 | tf_op jit(solution)/shard_map/all_to_all | solution.py:298
  137.6 9.7 %collective-permute-start.10 = (bf16[528,128]{1,0:T(8,128)(2,1)S(1)}, bf16[528,128]{1,0:T(8,128)(2,1)S(1)}, u32[]{:S(2)}, u32[]{:S(2)}) collective-permute-start(bf16[528,128]{1,0:T(8,128)(2,1)S(1)} %get-tuple-element.28.refs_0_), channel_id=1, source_target_pairs={{16,0},{32,16},{48,32},{0,48},{80,64},{96,80},{112,96},{64,112},{1... | collective-permute-start | bytes 405512 | tf_op jit(solution)/shard_map/ppermute | solution.py:306
  142.3 8.3 %collective-permute-start.11 = (bf16[528,128]{1,0:T(8,128)(2,1)S(1)}, bf16[528,128]{1,0:T(8,128)(2,1)S(1)}, u32[]{:S(2)}, u32[]{:S(2)}) collective-permute-start(bf16[528,128]{1,0:T(8,128)(2,1)S(1)} %get-tuple-element.28.refs_0_), channel_id=1, source_target_pairs={{32,0},{48,16},{0,32},{16,48},{96,64},{112,80},{64,96},{80,112},{1... | collective-permute-start | bytes 405512 | tf_op jit(solution)/shard_map/ppermute | solution.py:306
  144.6 9.2 %collective-permute-start.12 = (bf16[528,128]{1,0:T(8,128)(2,1)S(1)}, bf16[528,128]{1,0:T(8,128)(2,1)S(1)}, u32[]{:S(2)}, u32[]{:S(2)}) collective-permute-start(bf16[528,128]{1,0:T(8,128)(2,1)S(1)} %get-tuple-element.28.refs_0_), channel_id=1, source_target_pairs={{48,0},{0,16},{16,32},{32,48},{112,64},{64,80},{80,96},{96,112},{1... | collective-permute-start | bytes 405512 | tf_op jit(solution)/shard_map/ppermute | solution.py:306
  154.6 1.2 copy-start.1
  155.0 0.8 copy-start.4

commit v3 on v2

--- a/solution.py
+++ b/solution.py
@@ -106,14 +106,16 @@
     )(a, b)
 
 
-def small_kernel(body, out_shape, *operands):
+def small_kernel(body, out_shape, *operands, scalars=0, scratch=()):
     vmem = pl.BlockSpec(memory_space=pltpu.VMEM)
+    smem = pl.BlockSpec(memory_space=pltpu.SMEM)
     size = sum(a.size for a in operands)
     return pl.pallas_call(
         body,
         out_shape=out_shape,
-        in_specs=[vmem] * len(operands),
+        in_specs=[smem] * scalars + [vmem] * (len(operands) - scalars),
         out_specs=jax.tree.map(lambda _: vmem, out_shape),
+        scratch_shapes=scratch,
         cost_estimate=pl.CostEstimate(flops=size, bytes_accessed=4 * size, transcendentals=0),
         compiler_params=pltpu.CompilerParams(vmem_limit_bytes=8 << 20),
     )(*operands)
@@ -170,8 +172,8 @@
         stats_ref[j] = stats
 
 
-def rows_kernel(pick_ref, lane_ref, *refs):
-    *got, out_ref, mean_ref = refs
+def rows_kernel(index_ref, state_ref, pick_ref, lane_ref, *refs):
+    *got, out_ref, own_ref, mean_ref = refs
     my_x = lax.axis_index("grp") % N_X
     head = out_ref.shape[1]
     full = out_ref.shape[0] // N_X
@@ -179,14 +181,23 @@
     states = jnp.concatenate([ref[full:, :] for ref in got], axis=0)
     for k, ref in enumerate(got):
         for t in range(2):
-            begin = ((my_x + k) % N_X) * full + t * slab
+            begin = (my_x ^ k) * full + t * slab
             where = pl.ds(pl.multiple_of(begin, slab), slab)
             grad = ref[t * slab : (t + 1) * slab, :].astype(jnp.float32)
             state = jnp.dot(pick_ref[where, :], states, preferred_element_type=jnp.float32)
             prev = jnp.sum(state * lane_ref[where, :].astype(jnp.float32), axis=1, keepdims=True)
             mean = jnp.sum(grad * grad, axis=1, keepdims=True) / head + epsilon
-            mean_ref[where, :] = jnp.broadcast_to(mean, (slab, mean_ref.shape[1]))
+            mean_ref[where, :] = jnp.broadcast_to(mean, (slab, head))
             out_ref[where, :] = grad * lax.rsqrt(decay_rate * prev + (1.0 - decay_rate) * mean)
+    capacity, unit_rows = own_ref.shape
+    shape = (unit_rows, unit_rows)
+    eye = lax.broadcasted_iota(jnp.int32, shape, 0) == lax.broadcasted_iota(jnp.int32, shape, 1)
+    for c in range(capacity):
+        unit = jnp.maximum(index_ref[c], 0)
+        column = mean_ref[pl.ds(pl.multiple_of(unit * unit_rows, unit_rows), unit_rows), :]
+        mean = jnp.sum(jnp.where(eye, column[:, :unit_rows], 0.0), axis=0, keepdims=True)
+        new = decay_rate * state_ref[c : c + 1, :] + (1.0 - decay_rate) * mean
+        own_ref[c : c + 1, :] = jnp.where(index_ref[c] >= 0, new, 0.0)
 
 
 def update_kernel(stats_ref, grad_ref, weight_ref, state_ref, out_ref, col_ref):
@@ -209,6 +220,86 @@
         out_ref[:, cols] = (weight_ref[:, cols].astype(jnp.float32) - change).astype(out_ref.dtype)
 
 
+def tables_kernel(owner_ref, state_ref, pick_ref, lane_ref, extra_ref, index_ref):
+    f32, bf16 = jnp.float32, jnp.bfloat16
+    me = lax.axis_index("grp")
+    units = owner_ref.shape[0]
+    capacity, unit_rows = state_ref.shape
+    count, head = lane_ref.shape
+    half = capacity * unit_rows
+    tensors = units // unit_rows
+    seats = pick_ref.shape[1]
+
+    def at(shape, axis):
+        return lax.broadcasted_iota(jnp.int32, shape, axis)
+
+    owner = owner_ref[...]
+    hot = (owner == at((units, head), 1)).astype(f32)
+    earlier = (at((units, units), 1) < at((units, units), 0)).astype(bf16)
+    before = jnp.dot(earlier, hot.astype(bf16), preferred_element_type=f32)
+    slot = jnp.sum(before * hot, axis=1, keepdims=True).astype(jnp.int32)
+
+    seat = ((owner ^ me) & (N_X - 1)) * (seats // N_X) + owner // N_X
+    spread = ((at((count, units), 0) // unit_rows) == at((count, units), 1)).astype(bf16)
+    hot = (seat == at((units, seats), 1)).astype(bf16)
+    pick_ref[...] = jnp.dot(spread, hot, preferred_element_type=f32).astype(bf16)
+    lanes = at((units, head), 1)
+    hot = (slot == (lanes % half) // unit_rows).astype(bf16)
+    match = (at((count, head), 0) % unit_rows) == (at((count, head), 1) % unit_rows)
+    hot = jnp.dot(spread, hot, preferred_element_type=f32)
+    lane_ref[...] = jnp.where(match, hot, 0.0).astype(bf16)
+
+    state = state_ref[...]
+    high = state.astype(bf16)
+    low = (state - high.astype(f32)).astype(bf16)
+    copies = (at((unit_rows, head), 0) == at((unit_rows, head), 1) % unit_rows).astype(bf16)
+    high = jnp.dot(high, copies, preferred_element_type=f32)
+    low = jnp.dot(low, copies, preferred_element_type=f32)
+    lanes = at((capacity, head), 1)
+    parts = jnp.where(lanes < half, high, low)
+    mine = (lanes % half) // unit_rows == at((capacity, head), 0)
+    state_row = jnp.sum(jnp.where(mine, parts, 0.0), axis=0, keepdims=True)
+    number = at((units, 1), 0)
+    sums = jnp.zeros((units, 1), f32)
+    for c in range(capacity):
+        here = (owner == me) & (slot == c)
+        total = jnp.sum(state[c : c + 1, :], axis=1, keepdims=True)
+        sums = sums + jnp.where(here, total, 0.0)
+        index_ref[c] = jnp.max(jnp.where(here, number.astype(f32), -1.0)).astype(jnp.int32)
+    lanes = at((units, head), 1)
+    tensor = at((units, head), 0) // unit_rows
+    here = (lanes % tensors == tensor) & (lanes < 2 * tensors)
+    value = jnp.sum(jnp.where(here, sums, 0.0), axis=0, keepdims=True)
+    high = value.astype(bf16).astype(f32)
+    sum_row = jnp.where(at((1, head), 1) < tensors, high, value - high)
+    rows = [state_row, sum_row, jnp.zeros((extra_ref.shape[0] - 2, head), f32)]
+    extra_ref[...] = jnp.concatenate(rows, axis=0).astype(bf16)
+
+
+def tables(owner_table, state, head, seats):
+    capacity, unit_rows = state.shape
+    count = owner_table.shape[0] * unit_rows
+    vmem = pl.BlockSpec(memory_space=pltpu.VMEM)
+    smem = pl.BlockSpec(memory_space=pltpu.SMEM)
+    bf16 = jnp.bfloat16
+    return pl.pallas_call(
+        tables_kernel,
+        out_shape=(
+            jax.ShapeDtypeStruct((count, seats), bf16),
+            jax.ShapeDtypeStruct((count, head), bf16),
+            jax.ShapeDtypeStruct((unit_rows, head), bf16),
+            jax.ShapeDtypeStruct((capacity,), jnp.int32),
+        ),
+        in_specs=[vmem, vmem],
+        out_specs=(vmem, vmem, vmem, smem),
+        cost_estimate=pl.CostEstimate(
+            flops=count * head * 100, bytes_accessed=4 * count * head, transcendentals=0
+        ),
+        compiler_params=pltpu.CompilerParams(vmem_limit_bytes=8 << 20),
+        name="tables",
+    )(owner_table, state)
+
+
 def on_device(normed, cotangent, norm_gain, weights, row_state, col_state, owner_table):
     bf16, f32 = jnp.bfloat16, jnp.float32
     groups = lax.axis_size("grp")
@@ -224,7 +315,6 @@
     x_groups = [[z * N_X + x for x in range(N_X)] for z in range(n_z)]
     z_groups = [[z * N_X + x for z in range(n_z)] for x in range(N_X)]
 
-    my_group = lax.axis_index("grp")
 
     swap = [(i, i ^ 1) for i in range(intra)]
     cot_got = lax.ppermute(cotangent, "intra", swap)
@@ -252,7 +342,13 @@
     last = hop(first)
     give = add(hop(second), parts[-1]).astype(bf16)
     other = lax.ppermute(give, "intra", swap)
+    state_rows = n_z + -n_z % unit_rows
+    pick, lane, extra, my_index = tables(owner_table, row_state[0, 0], head, N_X * state_rows)
+    last, other, extra, pick, lane, my_index = lax.optimization_barrier(
+        (last, other, extra, pick, lane, my_index)
+    )
     own = finish(last, other, head)
+
 
     per_x = units // N_X
     per_z = -(-per_x // n_z)
@@ -261,32 +357,10 @@
     sent = small_kernel(sum_x_kernel, sent, got)
     got = lax.all_to_all(sent, "grp", 0, 0, axis_index_groups=z_groups, tiled=True)
 
-    owner = owner_table[:, 0]
-    onehot = (owner[:, None] == jnp.arange(groups, dtype=jnp.int32)[None, :]).astype(jnp.int32)
-    before = jnp.cumsum(onehot, axis=0) - onehot
-    slot = jnp.sum(before * onehot, axis=1)
-    place = owner * capacity + slot
-    mine = (
-        place[None, :] == my_group * capacity + jnp.arange(capacity, dtype=jnp.int32)[:, None]
-    )
-    filled = jnp.any(mine, axis=1)
-
-    def two_parts(a):
-        high = a.astype(bf16)
-        return jnp.concatenate([high, (a - high.astype(f32)).astype(bf16)], axis=1)
-
-    state_sum = jnp.where(filled, jnp.sum(row_state[0, 0], axis=1), 0.0)
-    of_tensor = jnp.any(mine.reshape(capacity, tensors, blocks), axis=2)
-    sums = jnp.sum(jnp.where(of_tensor, state_sum[:, None], 0.0), axis=0)
-    half = capacity * unit_rows
-    rows = [two_parts(row_state.reshape(1, half)), two_parts(sums[None, :])]
-    rows = [jnp.pad(r, ((0, 0), (0, head - r.shape[1]))) for r in rows]
-    extra = jnp.concatenate(rows + [jnp.zeros((unit_rows - 2, head), bf16)], axis=0)
     sent = jax.ShapeDtypeStruct((n_z, got.shape[1] + unit_rows, head), bf16)
     sent = small_kernel(sum_z_kernel, sent, got, extra)
     got = lax.all_to_all(sent, "grp", 0, 0, axis_index_groups=z_groups, tiled=True)
     full = per_x * unit_rows
-    state_rows = n_z + -n_z % unit_rows
     shapes = (
         jax.ShapeDtypeStruct((full + state_rows, head), bf16),
         jax.ShapeDtypeStruct((N_X * intra, 8, head), f32),
@@ -298,36 +372,35 @@
     stats = lax.all_to_all(
         stats, ("grp", "intra"), 0, 0, axis_index_groups=planes, tiled=True
     )
-    fetched = [sent]
-    for k in range(1, N_X):
-        pairs = [
-            (z * N_X + (x + k) % N_X, z * N_X + x) for z in range(n_z) for x in range(N_X)
-        ]
-        fetched.append(lax.ppermute(sent, "grp", pairs))
-
-    seat = ((owner - my_group) % N_X) * state_rows + owner // N_X
-    pick = seat[:, None, None] == jnp.arange(N_X * state_rows, dtype=jnp.int32)
-    pick = jnp.broadcast_to(pick, (units, unit_rows, N_X * state_rows)).astype(bf16)
-    lane = slot[:, None, None] * unit_rows + jnp.arange(unit_rows, dtype=jnp.int32)[None, :, None]
-    lane = (lane == jnp.arange(head, dtype=jnp.int32) % half).astype(bf16)
+
+    def trade(a, k):
+        pairs = [(g, g ^ k) for g in range(groups)]
+        return lax.ppermute(a, "grp", pairs)
+
+    near, wrap = trade(sent, 1), trade(sent, N_X - 1)
+    fetched = [sent, near, trade(near, N_X - 1), wrap]
+
     count = units * unit_rows
     shapes = (
         jax.ShapeDtypeStruct((count, head), f32),
-        jax.ShapeDtypeStruct((count, 8), f32),
-    )
-    scaled, row_mean = small_kernel(
-        rows_kernel, shapes, pick.reshape(count, -1), lane.reshape(count, head), *fetched
+        jax.ShapeDtypeStruct((capacity, unit_rows), f32),
+    )
+    scaled, row_moments = small_kernel(
+        rows_kernel,
+        shapes,
+        my_index,
+        row_state[0, 0],
+        pick,
+        lane,
+        *fetched,
+        scalars=1,
+        scratch=[pltpu.VMEM((count, head), f32)],
     )
     shapes = (
         jax.ShapeDtypeStruct(weights.shape, weights.dtype),
         jax.ShapeDtypeStruct(col_state.shape, f32),
     )
     new_weights, col_new = small_kernel(update_kernel, shapes, stats, scaled, weights, col_state)
-    row_mean = row_mean[:, 0].reshape(units, unit_rows)
-    own_mean = jnp.dot(mine.astype(f32), row_mean, precision=lax.Precision.HIGHEST)
-    row_moments = jnp.where(
-        filled[:, None], decay_rate * row_state[0, 0] + (1.0 - decay_rate) * own_mean, 0.0
-    )
     return (new_weights, row_moments[None, None], col_new)
 
 

time: 158 us -> 152 us (0.962)
  the two profiles are of different devices: /device:TPU:1 before, /device:TPU:6 now
where the time goes in v3:
time: 152 us; the launch traced here: 151 us
  blocking collectives  52.6 us (35%)
  waiting for transfers between devices  45.2 us (30%)
  starting transfers between devices  41.3 us (27%)
  Pallas kernels  8.04 us (5%)
  local copies, waits for them, and re-layouts  2.07 us (1%)
    all_to_all x2, blocking collectives, on_device(): lax.all_to_all(sent, 'grp', 0, 0, axis_index_groups=z_groups, tiled=True)  35 us
    ppermute x7, waiting for transfers between devices, hop(): return lax.ppermute(a, 'intra', ring)  34.3 us
    all_to_all x1, blocking collectives, on_device(): lax.all_to_all(own, 'grp', 0, 0, axis_index_groups=x_groups, tiled=True)  17.6 us
    ppermute x7, starting transfers between devices, hop(): return lax.ppermute(a, 'intra', ring)  16.8 us
    all_to_all x1, starting transfers between devices, on_device(): lax.all_to_all(stats, ('grp', 'intra'), 0, 0, axis_index_groups=planes, t...  10.3 us
    ppermute x3, waiting for transfers between devices, trade(): return lax.ppermute(a, 'grp', pairs)  9.76 us
    ppermute x3, starting transfers between devices, trade(): return lax.ppermute(a, 'grp', pairs)  7.95 us
    pallas_call x5, Pallas kernels, small_kernel(): pl.pallas_call(body, out_shape=out_shape, in_specs=[smem] * scalars + [vm...  3.94 us
  transfers between devices with their start and end apart: 14, of which 10 were waited for; matrix products, arithmetic and copies ran while one was open for 1% of the time, Pallas kernels for 2%

profile of v3, /device:TPU:6, one launch (start us, length us, event | category | flops | bytes accessed | tf_op | source)
XLA Modules:
  0.0 151.2 jit_solution(2795261474561713816)
XLA Ops:
  2.8 1.9 %collective-permute-start = (bf16[128,2048]{1,0:T(8,128)(2,1)S(1)}, bf16[128,2048]{1,0:T(8,128)(2,1)S(1)}, u32[]{:S(2)}, u32[]{:S(2)}) collective-permute-start(bf16[128,2048]{1,0:T(8,128)(2,1)S(1)} %get-tuple-element.29), channel_id=1, source_target_pairs={{0,1},{1,0},{2,3},{3,2},{4,5},{5,4},{6,7},{7,6},{8,9},{9,8},{10,11... | collective-permute-start | bytes 1572872 | tf_op jit(solution)/shard_map/ppermute | solution.py:322
  4.7 2.4 %collective-permute-start.1 = (bf16[128,1024]{1,0:T(8,128)(2,1)S(1)}, bf16[128,1024]{1,0:T(8,128)(2,1)S(1)}, u32[]{:S(2)}, u32[]{:S(2)}) collective-permute-start(bf16[128,1024]{1,0:T(8,128)(2,1)S(1)} %copy-done.2), channel_id=1, source_target_pairs={{0,1},{1,0},{2,3},{3,2},{4,5},{5,4},{6,7},{7,6},{8,9},{9,8},{10,11... | collective-permute-start | bytes 786440 | tf_op jit(solution)/shard_map/ppermute | solution.py:320
  8.7 2.1 %products.3 = (bf16[256,1024]{1,0:T(8,128)(2,1)S(1)}, bf16[256,1024]{1,0:T(8,128)(2,1)S(1)}, bf16[256,1024]{1,0:T(8,128)(2,1)S(1)}, bf16[256,1024]{1,0:T(8,128)(...) custom-call(bf16[128,2048]{1,0:T(8,128)(2,1)S(1)} %get-tuple-element.28.x_ref,, ...), custom_call_target="tpu_custom_call" | custom-call | flops 939524096 | bytes 7340032 | tf_op jit(solution)/shard_map/products/pallas_call | solution.py:69
  10.8 3.5 %collective-permute-start.6 = (bf16[256,1024]{1,0:T(8,128)(2,1)S(1)}, bf16[256,1024]{1,0:T(8,128)(2,1)S(1)}, u32[]{:S(2)}, u32[]{:S(2)}) collective-permute-start(bf16[256,1024]{1,0:T(8,128)(2,1)S(1)} %get-tuple-element.33), channel_id=1, source_target_pairs={{0,2},{1,15},{2,4},{3,1},{4,6},{5,3},{6,8},{7,5},{8,10},{9,7},{10,... | collective-permute-start | bytes 1572872 | tf_op jit(solution)/shard_map/ppermute | solution.py:335
  14.3 3.5 %collective-permute-start.2 = (bf16[256,1024]{1,0:T(8,128)(2,1)S(1)}, bf16[256,1024]{1,0:T(8,128)(2,1)S(1)}, u32[]{:S(2)}, u32[]{:S(2)}) collective-permute-start(bf16[256,1024]{1,0:T(8,128)(2,1)S(1)} %products.2.outs_0_), channel_id=1, source_target_pairs={{0,2},{1,15},{2,4},{3,1},{4,6},{5,3},{6,8},{7,5},{8,10},{9,7},{10,... | collective-permute-start | bytes 1572872 | tf_op jit(solution)/shard_map/ppermute | solution.py:335
  17.8 5.5 %collective-permute-done.6 = bf16[256,1024]{1,0:T(8,128)(2,1)S(1)} collective-permute-done((bf16[256,1024]{1,0:T(8,128)(2,1)S(1)}, bf16[256,1024]{1,0:T(8,128)(2,1)S(1)}, u32[]{:S(2)}, u32[]{:S(2)}) %collective-permute-start.6) | collective-permute-done | bytes 524320 | tf_op jit(solution)/shard_map/ppermute | solution.py:335
  23.5 2.0 %collective-permute-start.7 = (bf16[256,1024]{1,0:T(8,128)(2,1)S(1)}, bf16[256,1024]{1,0:T(8,128)(2,1)S(1)}, u32[]{:S(2)}, u32[]{:S(2)}) collective-permute-start(bf16[256,1024]{1,0:T(8,128)(2,1)S(1)} %add_convert_fusion.2), channel_id=1, source_target_pairs={{0,2},{1,15},{2,4},{3,1},{4,6},{5,3},{6,8},{7,5},{8,10},{9,7},{10,... | collective-permute-start | bytes 1572872 | tf_op jit(solution)/shard_map/ppermute | solution.py:335
  25.6 3.4 %collective-permute-done.2 = bf16[256,1024]{1,0:T(8,128)(2,1)S(1)} collective-permute-done((bf16[256,1024]{1,0:T(8,128)(2,1)S(1)}, bf16[256,1024]{1,0:T(8,128)(2,1)S(1)}, u32[]{:S(2)}, u32[]{:S(2)}) %collective-permute-start.2) | collective-permute-done | bytes 524320 | tf_op jit(solution)/shard_map/ppermute | solution.py:335
  29.2 2.0 %collective-permute-start.3 = (bf16[256,1024]{1,0:T(8,128)(2,1)S(1)}, bf16[256,1024]{1,0:T(8,128)(2,1)S(1)}, u32[]{:S(2)}, u32[]{:S(2)}) collective-permute-start(bf16[256,1024]{1,0:T(8,128)(2,1)S(1)} %add_convert_fusion.5), channel_id=1, source_target_pairs={{0,2},{1,15},{2,4},{3,1},{4,6},{5,3},{6,8},{7,5},{8,10},{9,7},{10,... | collective-permute-start | bytes 1572872 | tf_op jit(solution)/shard_map/ppermute | solution.py:335
  31.2 4.6 %collective-permute-done.7 = bf16[256,1024]{1,0:T(8,128)(2,1)S(1)} collective-permute-done((bf16[256,1024]{1,0:T(8,128)(2,1)S(1)}, bf16[256,1024]{1,0:T(8,128)(2,1)S(1)}, u32[]{:S(2)}, u32[]{:S(2)}) %collective-permute-start.7) | collective-permute-done | bytes 524320 | tf_op jit(solution)/shard_map/ppermute | solution.py:335
  37.9 3.5 %collective-permute-done.3 = bf16[256,1024]{1,0:T(8,128)(2,1)S(1)} collective-permute-done((bf16[256,1024]{1,0:T(8,128)(2,1)S(1)}, bf16[256,1024]{1,0:T(8,128)(2,1)S(1)}, u32[]{:S(2)}, u32[]{:S(2)}) %collective-permute-start.3) | collective-permute-done | bytes 524320 | tf_op jit(solution)/shard_map/ppermute | solution.py:335
  41.6 1.9 %collective-permute-start.4 = (bf16[256,1024]{1,0:T(8,128)(2,1)S(1)}, bf16[256,1024]{1,0:T(8,128)(2,1)S(1)}, u32[]{:S(2)}, u32[]{:S(2)}) collective-permute-start(bf16[256,1024]{1,0:T(8,128)(2,1)S(1)} %add_convert_fusion.4), channel_id=1, source_target_pairs={{0,2},{1,15},{2,4},{3,1},{4,6},{5,3},{6,8},{7,5},{8,10},{9,7},{10,... | collective-permute-start | bytes 1572872 | tf_op jit(solution)/shard_map/ppermute | solution.py:335
  43.6 4.7 %collective-permute-done.8 = bf16[256,1024]{1,0:T(8,128)(2,1)S(1)} collective-permute-done((bf16[256,1024]{1,0:T(8,128)(2,1)S(1)}, bf16[256,1024]{1,0:T(8,128)(2,1)S(1)}, u32[]{:S(2)}, u32[]{:S(2)}) %collective-permute-start.8) | collective-permute-done | bytes 524320 | tf_op jit(solution)/shard_map/ppermute | solution.py:335
  50.4 3.5 %collective-permute-done.4 = bf16[256,1024]{1,0:T(8,128)(2,1)S(1)} collective-permute-done((bf16[256,1024]{1,0:T(8,128)(2,1)S(1)}, bf16[256,1024]{1,0:T(8,128)(2,1)S(1)}, u32[]{:S(2)}, u32[]{:S(2)}) %collective-permute-start.4) | collective-permute-done | bytes 524320 | tf_op jit(solution)/shard_map/ppermute | solution.py:335
  57.4 9.0 %collective-permute-done.5.a_ref = bf16[256,1024]{1,0:T(8,128)(2,1)S(1)} collective-permute-done((bf16[256,1024]{1,0:T(8,128)(2,1)S(1)}, bf16[256,1024]{1,0:T(8,128)(2,1)S(1)}, u32[]{:S(2)}, u32[]{:S(2)}) %collective-permute-start.5) | collective-permute-done | bytes 524320 | tf_op jit(solution)/shard_map/ppermute | solution.py:335
  66.6 17.6 %all_to_all.20.got_ref = bf16[4,512,128]{2,1,0:T(8,128)(2,1)S(1)} all-to-all(bf16[4,512,128]{2,1,0:T(8,128)(2,1)S(1)} %finish.1), channel_id=1, replica_groups={{0,16,32,48},{64,80,96,112},{128,144,160,176},{192,208,224,240},{256,27..., dimensions={0} | all-to-all | bytes 1048576 | tf_op jit(solution)/shard_map/all_to_all | solution.py:355
  84.3 19.8 %all_to_all.21.got_ref = bf16[12,48,128]{2,1,0:T(8,128)(2,1)S(1)} all-to-all(bf16[12,48,128]{2,1,0:T(8,128)(2,1)S(1)} %shard_map.94), channel_id=1, replica_groups={{0,64,128,192,256,320,384,448,512,576,640,704},{16,80,144,208,272,336,4..., dimensions={0} | all-to-all | bytes 294912 | tf_op jit(solution)/shard_map/all_to_all | solution.py:358
  104.1 15.2 %all_to_all.22.got_ref = bf16[12,64,128]{2,1,0:T(8,128)(2,1)S(1)} all-to-all(bf16[12,64,128]{2,1,0:T(8,128)(2,1)S(1)} %shard_map.95), channel_id=1, replica_groups={{0,64,128,192,256,320,384,448,512,576,640,704},{16,80,144,208,272,336,4..., dimensions={0} | all-to-all | bytes 393216 | tf_op jit(solution)/shard_map/all_to_all | solution.py:362
  120.1 10.3 %all-to-all-start.3 = ((f32[64,8,128]{2,1,0:T(8,128)}), f32[64,8,128]{2,1,0:T(8,128)S(1)}, u32[]{:S(2)}, u32[]{:S(2)}) async-start(f32[64,8,128]{2,1,0:T(8,128)} %get-tuple-element.44), calls=%async_computation.3 | async-start | bytes 524288 | tf_op jit(solution)/shard_map/all_to_all | solution.py:372
  130.4 2.8 %collective-permute-start.10 = (bf16[528,128]{1,0:T(8,128)(2,1)S(1)}, bf16[528,128]{1,0:T(8,128)(2,1)S(1)}, u32[]{:S(2)}, u32[]{:S(2)}) collective-permute-start(bf16[528,128]{1,0:T(8,128)(2,1)S(1)} %get-tuple-element.48.refs_0_), channel_id=1, source_target_pairs={{0,16},{16,0},{32,48},{48,32},{64,80},{80,64},{96,112},{112,96},{1... | collective-permute-start | bytes 405512 | tf_op jit(solution)/shard_map/ppermute | solution.py:378
  133.2 3.0 %collective-permute-start.12 = (bf16[528,128]{1,0:T(8,128)(2,1)S(1)}, bf16[528,128]{1,0:T(8,128)(2,1)S(1)}, u32[]{:S(2)}, u32[]{:S(2)}) collective-permute-start(bf16[528,128]{1,0:T(8,128)(2,1)S(1)} %get-tuple-element.48.refs_0_), channel_id=1, source_target_pairs={{0,48},{16,32},{32,16},{48,0},{64,112},{80,96},{96,80},{112,64},{1... | collective-permute-start | bytes 405512 | tf_op jit(solution)/shard_map/ppermute | solution.py:378
  136.2 3.9 %collective-permute-done.10.refs_1_ = bf16[528,128]{1,0:T(8,128)(2,1)S(1)} collective-permute-done((bf16[528,128]{1,0:T(8,128)(2,1)S(1)}, bf16[528,128]{1,0:T(8,128)(2,1)S(1)}, u32[]{:S(2)}, u32[]{:S(2)}) %collective-permute-start.10) | collective-permute-done | bytes 135200 | tf_op jit(solution)/shard_map/ppermute | solution.py:378
  140.0 2.2 %collective-permute-start.11 = (bf16[528,128]{1,0:T(8,128)(2,1)S(1)}, bf16[528,128]{1,0:T(8,128)(2,1)S(1)}, u32[]{:S(2)}, u32[]{:S(2)}) collective-permute-start(bf16[528,128]{1,0:T(8,128)(2,1)S(1)} %collective-permute-done.10.refs_1_), channel_id=1, source_target_pairs={{0,48},{16,32},{32,16},{48,0},{64,112},{80,96},{96,80},{112,64},{1... | collective-permute-start | bytes 405512 | tf_op jit(solution)/shard_map/ppermute | solution.py:378
  142.2 5.9 %collective-permute-done.11.refs_2_ = bf16[528,128]{1,0:T(8,128)(2,1)S(1)} collective-permute-done((bf16[528,128]{1,0:T(8,128)(2,1)S(1)}, bf16[528,128]{1,0:T(8,128)(2,1)S(1)}, u32[]{:S(2)}, u32[]{:S(2)}) %collective-permute-start.11) | collective-permute-done | bytes 135200 | tf_op jit(solution)/shard_map/ppermute | solution.py:378
  (38 shorter events, 16.1 us)
Async XLA Ops:
  0.6 1.2 copy-start
  1.9 0.7 copy-start.3
  2.6 2.1 %copy-start.2 = (bf16[128,1024]{1,0:T(8,128)(2,1)S(1)}, bf16[128,1024]{1,0:T(8,128)(2,1)}, u32[]{:S(2)}) copy-start(bf16[128,1024]{1,0:T(8,128)(2,1)} %c_ref.3) | copy-start | bytes 786436
  2.8 5.5 %collective-permute-start = (bf16[128,2048]{1,0:T(8,128)(2,1)S(1)}, bf16[128,2048]{1,0:T(8,128)(2,1)S(1)}, u32[]{:S(2)}, u32[]{:S(2)}) collective-permute-start(bf16[128,2048]{1,0:T(8,128)(2,1)S(1)} %get-tuple-element.29), channel_id=1, source_target_pairs={{0,1},{1,0},{2,3},{3,2},{4,5},{5,4},{6,7},{7,6},{8,9},{9,8},{10,11... | collective-permute-start | bytes 1572872 | tf_op jit(solution)/shard_map/ppermute | solution.py:322
  4.7 3.6 %collective-permute-start.1 = (bf16[128,1024]{1,0:T(8,128)(2,1)S(1)}, bf16[128,1024]{1,0:T(8,128)(2,1)S(1)}, u32[]{:S(2)}, u32[]{:S(2)}) collective-permute-start(bf16[128,1024]{1,0:T(8,128)(2,1)S(1)} %copy-done.2), channel_id=1, source_target_pairs={{0,1},{1,0},{2,3},{3,2},{4,5},{5,4},{6,7},{7,6},{8,9},{9,8},{10,11... | collective-permute-start | bytes 786440 | tf_op jit(solution)/shard_map/ppermute | solution.py:320
  10.8 12.5 %collective-permute-start.6 = (bf16[256,1024]{1,0:T(8,128)(2,1)S(1)}, bf16[256,1024]{1,0:T(8,128)(2,1)S(1)}, u32[]{:S(2)}, u32[]{:S(2)}) collective-permute-start(bf16[256,1024]{1,0:T(8,128)(2,1)S(1)} %get-tuple-element.33), channel_id=1, source_target_pairs={{0,2},{1,15},{2,4},{3,1},{4,6},{5,3},{6,8},{7,5},{8,10},{9,7},{10,... | collective-permute-start | bytes 1572872 | tf_op jit(solution)/shard_map/ppermute | solution.py:335
  14.3 14.6 %collective-permute-start.2 = (bf16[256,1024]{1,0:T(8,128)(2,1)S(1)}, bf16[256,1024]{1,0:T(8,128)(2,1)S(1)}, u32[]{:S(2)}, u32[]{:S(2)}) collective-permute-start(bf16[256,1024]{1,0:T(8,128)(2,1)S(1)} %products.2.outs_0_), channel_id=1, source_target_pairs={{0,2},{1,15},{2,4},{3,1},{4,6},{5,3},{6,8},{7,5},{8,10},{9,7},{10,... | collective-permute-start | bytes 1572872 | tf_op jit(solution)/shard_map/ppermute | solution.py:335
  23.5 12.3 %collective-permute-start.7 = (bf16[256,1024]{1,0:T(8,128)(2,1)S(1)}, bf16[256,1024]{1,0:T(8,128)(2,1)S(1)}, u32[]{:S(2)}, u32[]{:S(2)}) collective-permute-start(bf16[256,1024]{1,0:T(8,128)(2,1)S(1)} %add_convert_fusion.2), channel_id=1, source_target_pairs={{0,2},{1,15},{2,4},{3,1},{4,6},{5,3},{6,8},{7,5},{8,10},{9,7},{10,... | collective-permute-start | bytes 1572872 | tf_op jit(solution)/shard_map/ppermute | solution.py:335
  29.2 12.3 %collective-permute-start.3 = (bf16[256,1024]{1,0:T(8,128)(2,1)S(1)}, bf16[256,1024]{1,0:T(8,128)(2,1)S(1)}, u32[]{:S(2)}, u32[]{:S(2)}) collective-permute-start(bf16[256,1024]{1,0:T(8,128)(2,1)S(1)} %add_convert_fusion.5), channel_id=1, source_target_pairs={{0,2},{1,15},{2,4},{3,1},{4,6},{5,3},{6,8},{7,5},{8,10},{9,7},{10,... | collective-permute-start | bytes 1572872 | tf_op jit(solution)/shard_map/ppermute | solution.py:335
  36.0 12.3 %collective-permute-start.8 = (bf16[256,1024]{1,0:T(8,128)(2,1)S(1)}, bf16[256,1024]{1,0:T(8,128)(2,1)S(1)}, u32[]{:S(2)}, u32[]{:S(2)}) collective-permute-start(bf16[256,1024]{1,0:T(8,128)(2,1)S(1)} %add_convert_fusion.1), channel_id=1, source_target_pairs={{0,2},{1,15},{2,4},{3,1},{4,6},{5,3},{6,8},{7,5},{8,10},{9,7},{10,... | collective-permute-start | bytes 1572872 | tf_op jit(solution)/shard_map/ppermute | solution.py:335
  41.6 12.3 %collective-permute-start.4 = (bf16[256,1024]{1,0:T(8,128)(2,1)S(1)}, bf16[256,1024]{1,0:T(8,128)(2,1)S(1)}, u32[]{:S(2)}, u32[]{:S(2)}) collective-permute-start(bf16[256,1024]{1,0:T(8,128)(2,1)S(1)} %add_convert_fusion.4), channel_id=1, source_target_pairs={{0,2},{1,15},{2,4},{3,1},{4,6},{5,3},{6,8},{7,5},{8,10},{9,7},{10,... | collective-permute-start | bytes 1572872 | tf_op jit(solution)/shard_map/ppermute | solution.py:335
  48.5 8.9 %collective-permute-start.9 = (bf16[256,1024]{1,0:T(8,128)(2,1)S(1)}, bf16[256,1024]{1,0:T(8,128)(2,1)S(1)}, u32[]{:S(2)}, u32[]{:S(2)}) collective-permute-start(bf16[256,1024]{1,0:T(8,128)(2,1)S(1)} %add_convert_fusion), channel_id=1, source_target_pairs={{0,1},{1,0},{2,3},{3,2},{4,5},{5,4},{6,7},{7,6},{8,9},{9,8},{10,11... | collective-permute-start | bytes 1572872 | tf_op jit(solution)/shard_map/ppermute | solution.py:344
  53.9 2.1 %copy-start.6 = (s32[128,1]{0,1:T(1,128)S(1)}, s32[128,1]{0,1:T(1,128)}, u32[]{:S(2)}) copy-start(s32[128,1]{0,1:T(1,128)} %param.13) | copy-start | bytes 1540
  54.1 2.1 %copy-start.5 = (f32[1,1,4,16]{3,2,1,0:T(4,128)S(1)}, f32[1,1,4,16]{3,2,1,0:T(4,128)}, u32[]{:S(2)}) copy-start(f32[1,1,4,16]{3,2,1,0:T(4,128)} %param.11) | copy-start | bytes 772
  54.1 12.3 %collective-permute-start.5 = (bf16[256,1024]{1,0:T(8,128)(2,1)S(1)}, bf16[256,1024]{1,0:T(8,128)(2,1)S(1)}, u32[]{:S(2)}, u32[]{:S(2)}) collective-permute-start(bf16[256,1024]{1,0:T(8,128)(2,1)S(1)} %add_convert_fusion.3), channel_id=1, source_target_pairs={{0,2},{1,15},{2,4},{3,1},{4,6},{5,3},{6,8},{7,5},{8,10},{9,7},{10,... | collective-permute-start | bytes 1572872 | tf_op jit(solution)/shard_map/ppermute | solution.py:335
  120.1 29.9 %all-to-all-start.3 = ((f32[64,8,128]{2,1,0:T(8,128)}), f32[64,8,128]{2,1,0:T(8,128)S(1)}, u32[]{:S(2)}, u32[]{:S(2)}) async-start(f32[64,8,128]{2,1,0:T(8,128)} %get-tuple-element.44), calls=%async_computation.3 | async-start | bytes 524288 | tf_op jit(solution)/shard_map/all_to_all | solution.py:372
  130.3 19.6 %copy-start.1 = (bf16[256,1024]{1,0:T(8,128)(2,1)S(1)}, bf16[256,1024]{1,0:T(8,128)(2,1)}, u32[]{:S(2)}) copy-start(bf16[256,1024]{1,0:T(8,128)(2,1)} %weight_ref.1) | copy-start | bytes 1572868
  130.4 9.6 %collective-permute-start.10 = (bf16[528,128]{1,0:T(8,128)(2,1)S(1)}, bf16[528,128]{1,0:T(8,128)(2,1)S(1)}, u32[]{:S(2)}, u32[]{:S(2)}) collective-permute-start(bf16[528,128]{1,0:T(8,128)(2,1)S(1)} %get-tuple-element.48.refs_0_), channel_id=1, source_target_pairs={{0,16},{16,0},{32,48},{48,32},{64,80},{80,64},{96,112},{112,96},{1... | collective-permute-start | bytes 405512 | tf_op jit(solution)/shard_map/ppermute | solution.py:378
  133.2 9.0 %collective-permute-start.12 = (bf16[528,128]{1,0:T(8,128)(2,1)S(1)}, bf16[528,128]{1,0:T(8,128)(2,1)S(1)}, u32[]{:S(2)}, u32[]{:S(2)}) collective-permute-start(bf16[528,128]{1,0:T(8,128)(2,1)S(1)} %get-tuple-element.48.refs_0_), channel_id=1, source_target_pairs={{0,48},{16,32},{32,16},{48,0},{64,112},{80,96},{96,80},{112,64},{1... | collective-permute-start | bytes 405512 | tf_op jit(solution)/shard_map/ppermute | solution.py:378
  140.0 8.1 %collective-permute-start.11 = (bf16[528,128]{1,0:T(8,128)(2,1)S(1)}, bf16[528,128]{1,0:T(8,128)(2,1)S(1)}, u32[]{:S(2)}, u32[]{:S(2)}) collective-permute-start(bf16[528,128]{1,0:T(8,128)(2,1)S(1)} %collective-permute-done.10.refs_1_), channel_id=1, source_target_pairs={{0,48},{16,32},{32,16},{48,0},{64,112},{80,96},{96,80},{112,64},{1... | collective-permute-start | bytes 405512 | tf_op jit(solution)/shard_map/ppermute | solution.py:378
  148.1 1.8 %copy-start.4 = (f32[8,128]{1,0:T(8,128)S(1)}, f32[8,128]{1,0:T(8,128)}, u32[]{:S(2)}) copy-start(f32[8,128]{1,0:T(8,128)} %state_ref.1) | copy-start | bytes 12292

commit v4 on v3

--- a/solution.py
+++ b/solution.py
@@ -51,14 +51,18 @@
 
 def products_kernel(slab, begin, after, x_ref, xg_ref, c_ref, cg_ref, *outs):
     dims = (((0,), (0,)), ((), ()))
-    for u, out in enumerate(outs[after:], begin):
+    outs = outs[after:]
+    half = outs[0].shape[1]
+    for u in range(begin, begin + len(outs) // 2):
         cols = slice(u * slab, (u + 1) * slab)
         total = lax.dot_general(
             x_ref[:, cols], c_ref[...], dims, preferred_element_type=jnp.float32
         ) + lax.dot_general(
             xg_ref[:, cols], cg_ref[...], dims, preferred_element_type=jnp.float32
         )
-        out[...] = total.astype(out.dtype)
+        for h in range(2):
+            out = outs[2 * (u - begin) + h]
+            out[...] = total[:, h * half : (h + 1) * half].astype(out.dtype)
 
 
 def products(mine, got, cot, cot_got, slab, begin, end, *after):
@@ -68,9 +72,11 @@
     vmem = pl.BlockSpec(memory_space=pltpu.VMEM)
     return pl.pallas_call(
         functools.partial(products_kernel, slab, begin, len(after)),
-        out_shape=tuple(jax.ShapeDtypeStruct((slab, width), cot.dtype) for _ in range(count)),
+        out_shape=tuple(
+            jax.ShapeDtypeStruct((slab, width // 2), cot.dtype) for _ in range(2 * count)
+        ),
         in_specs=[vmem] * 4 + [pl.BlockSpec(memory_space=pl.ANY)] * len(after),
-        out_specs=tuple([vmem] * count),
+        out_specs=tuple([vmem] * (2 * count)),
         cost_estimate=pl.CostEstimate(
             flops=4 * tokens * count * slab * width,
             bytes_accessed=4 * count * slab * width,
@@ -81,29 +87,16 @@
     )(mine, got, cot, cot_got, *after)
 
 
-def finish_kernel(a_ref, b_ref, out_ref):
+def finish_kernel(*refs):
+    *halves, out_ref = refs
     head = out_ref.shape[2]
-    slab = a_ref.shape[0]
-    for t in range(a_ref.shape[1] // head):
-        cols = slice(t * head, (t + 1) * head)
-        total = a_ref[:, cols].astype(jnp.float32) + b_ref[:, cols].astype(jnp.float32)
+    slab, width = halves[0].shape
+    for t in range(2 * width // head):
+        h, column = divmod(t * head, width)
+        cols = slice(column, column + head)
+        total = halves[h][:, cols].astype(jnp.float32) + halves[2 + h][:, cols].astype(jnp.float32)
         x, row = divmod(t * slab, out_ref.shape[1])
         out_ref[x, row : row + slab, :] = total.astype(out_ref.dtype)
-
-
-def finish(a, b, head):
-    vmem = pl.BlockSpec(memory_space=pltpu.VMEM)
-    return pl.pallas_call(
-        finish_kernel,
-        out_shape=jax.ShapeDtypeStruct((N_X, a.size // (N_X * head), head), a.dtype),
-        in_specs=[vmem, vmem],
-        out_specs=vmem,
-        cost_estimate=pl.CostEstimate(
-            flops=a.size, bytes_accessed=6 * a.size, transcendentals=0
-        ),
-        compiler_params=pltpu.CompilerParams(vmem_limit_bytes=8 << 20),
-        name="finish",
-    )(a, b)
 
 
 def small_kernel(body, out_shape, *operands, scalars=0, scratch=()):
@@ -307,6 +300,7 @@
     n_y = intra // CORES
     n_z = groups // N_X
     tensors, head = col_state.shape
+    width = tensors * head
     capacity, unit_rows = row_state.shape[2:]
     slab = weights.shape[0]
     blocks = slab // unit_rows
@@ -334,20 +328,26 @@
     def hop(a):
         return lax.ppermute(a, "intra", ring)
 
-    first, second = parts[0], parts[2]
+    parts = [parts[2 * k : 2 * k + 2] for k in range(len(parts) // 2)]
+    first, second = list(parts[0]), list(parts[2])
     for k in range(1, len(parts) - 2, 2):
-        first = add(hop(first), parts[k]).astype(bf16)
-        if k > 1:
-            second = add(hop(second), parts[k + 1]).astype(bf16)
-    last = hop(first)
-    give = add(hop(second), parts[-1]).astype(bf16)
-    other = lax.ppermute(give, "intra", swap)
+        for h in range(2):
+            first[h] = add(hop(first[h]), parts[k][h]).astype(bf16)
+            if k > 1:
+                second[h] = add(hop(second[h]), parts[k + 1][h]).astype(bf16)
+    last, other = [], []
+    for h in range(2):
+        last.append(hop(first[h]))
+        give = add(hop(second[h]), parts[-1][h]).astype(bf16)
+        other.append(lax.ppermute(give, "intra", swap))
+
     state_rows = n_z + -n_z % unit_rows
     pick, lane, extra, my_index = tables(owner_table, row_state[0, 0], head, N_X * state_rows)
     last, other, extra, pick, lane, my_index = lax.optimization_barrier(
         (last, other, extra, pick, lane, my_index)
     )
-    own = finish(last, other, head)
+    own = jax.ShapeDtypeStruct((N_X, slab * width // (N_X * head), head), bf16)
+    own = small_kernel(finish_kernel, own, *last, *other)
 
 
     per_x = units // N_X

time: 152 us -> 150 us (0.987)
  waiting for transfers between devices: 45.2 us -> 16.6 us
  starting transfers between devices: 41.3 us -> 68.5 us
    ppermute x7 -> x14, waiting for transfers between devices: 34.3 us -> 5.65 us  [hop(): return lax.ppermute(a, 'intra', ring)]
    ppermute x7 -> x14, starting transfers between devices: 16.8 us -> 44.9 us  [hop(): return lax.ppermute(a, 'intra', ring)]
    all_to_all x1, blocking collectives: 17.6 us -> 13 us  [on_device(): lax.all_to_all(own, 'grp', 0, 0, axis_index_groups=x_groups, tiled=True)]
    all_to_all x2, blocking collectives: 35 us -> 39.3 us  [on_device(): lax.all_to_all(sent, 'grp', 0, 0, axis_index_groups=z_groups, tiled=True)]
    all_to_all x1, starting transfers between devices: 10.3 us -> 7.01 us  [on_device(): lax.all_to_all(stats, ('grp', 'intra'), 0, 0, axis_index_groups=planes, t...]
    ppermute x1 -> x2, starting transfers between devices: 1.92 us -> 4.33 us  [on_device(): other.append(lax.ppermute(give, 'intra', swap))]
    pallas_call x5 -> x6, Pallas kernels: 3.94 us -> 4.06 us  [small_kernel(): pl.pallas_call(body, out_shape=out_shape, in_specs=[smem] * scalars + [vm...]
  transfers between devices with their start and end apart: 14 -> 22, of which waited for: 10 -> 5; matrix products, arithmetic and copies ran while one was open for 1% -> 1% of each run, Pallas kernels for 2% -> 2%
where the time goes in v4:
time: 150 us; the launch traced here: 149 us
  starting transfers between devices  68.5 us (46%)
  blocking collectives  52.3 us (35%)
  waiting for transfers between devices  16.6 us (11%)
  Pallas kernels  7.98 us (5%)
  local copies, waits for them, and re-layouts  2.07 us (1%)
    ppermute x14, starting transfers between devices, hop(): return lax.ppermute(a, 'intra', ring)  44.9 us
    all_to_all x2, blocking collectives, on_device(): lax.all_to_all(sent, 'grp', 0, 0, axis_index_groups=z_groups, tiled=True)  39.3 us
    all_to_all x1, blocking collectives, on_device(): lax.all_to_all(own, 'grp', 0, 0, axis_index_groups=x_groups, tiled=True)  13 us
    ppermute x3, waiting for transfers between devices, trade(): return lax.ppermute(a, 'grp', pairs)  9.76 us
    ppermute x3, starting transfers between devices, trade(): return lax.ppermute(a, 'grp', pairs)  7.95 us
    all_to_all x1, starting transfers between devices, on_device(): lax.all_to_all(stats, ('grp', 'intra'), 0, 0, axis_index_groups=planes, t...  7.01 us
    ppermute x14, waiting for transfers between devices, hop(): return lax.ppermute(a, 'intra', ring)  5.65 us
    ppermute x2, starting transfers between devices, on_device(): other.append(lax.ppermute(give, 'intra', swap))  4.33 us
  transfers between devices with their start and end apart: 22, of which 5 were waited for; matrix products, arithmetic and copies ran while one was open for 1% of the time, Pallas kernels for 2%

profile of v4, /device:TPU:6, one launch (start us, length us, event | category | flops | bytes accessed | tf_op | source)
XLA Modules:
  0.0 149.3 jit_solution(17009674295764545937)
XLA Ops:
  10.8 3.5 %collective-permute-start.14 = (bf16[256,512]{1,0:T(8,128)(2,1)S(1)}, bf16[256,512]{1,0:T(8,128)(2,1)S(1)}, u32[]{:S(2)}, u32[]{:S(2)}) collective-permute-start(bf16[256,512]{1,0:T(8,128)(2,1)S(1)} %get-tuple-element.53), channel_id=1, source_target_pairs={{0,2},{1,15},{2,4},{3,1},{4,6},{5,3},{6,8},{7,5},{8,10},{9,7},{10,... | collective-permute-start | bytes 786440 | tf_op jit(solution)/shard_map/ppermute | solution.py:329
  14.3 3.5 %collective-permute-start.10 = (bf16[256,512]{1,0:T(8,128)(2,1)S(1)}, bf16[256,512]{1,0:T(8,128)(2,1)S(1)}, u32[]{:S(2)}, u32[]{:S(2)}) collective-permute-start(bf16[256,512]{1,0:T(8,128)(2,1)S(1)} %get-tuple-element.49), channel_id=1, source_target_pairs={{0,2},{1,15},{2,4},{3,1},{4,6},{5,3},{6,8},{7,5},{8,10},{9,7},{10,... | collective-permute-start | bytes 786440 | tf_op jit(solution)/shard_map/ppermute | solution.py:329
  17.8 3.5 %collective-permute-start.2 = (bf16[256,512]{1,0:T(8,128)(2,1)S(1)}, bf16[256,512]{1,0:T(8,128)(2,1)S(1)}, u32[]{:S(2)}, u32[]{:S(2)}) collective-permute-start(bf16[256,512]{1,0:T(8,128)(2,1)S(1)} %get-tuple-element.41.outs_0_), channel_id=1, source_target_pairs={{0,2},{1,15},{2,4},{3,1},{4,6},{5,3},{6,8},{7,5},{8,10},{9,7},{10,... | collective-permute-start | bytes 786440 | tf_op jit(solution)/shard_map/ppermute | solution.py:329
  21.3 4.7 %collective-permute-start.6 = (bf16[256,512]{1,0:T(8,128)(2,1)S(1)}, bf16[256,512]{1,0:T(8,128)(2,1)S(1)}, u32[]{:S(2)}, u32[]{:S(2)}) collective-permute-start(bf16[256,512]{1,0:T(8,128)(2,1)S(1)} %get-tuple-element.45), channel_id=1, source_target_pairs={{0,2},{1,15},{2,4},{3,1},{4,6},{5,3},{6,8},{7,5},{8,10},{9,7},{10,... | collective-permute-start | bytes 786440 | tf_op jit(solution)/shard_map/ppermute | solution.py:329
  26.1 2.6 %collective-permute-start.15 = (bf16[256,512]{1,0:T(8,128)(2,1)S(1)}, bf16[256,512]{1,0:T(8,128)(2,1)S(1)}, u32[]{:S(2)}, u32[]{:S(2)}) collective-permute-start(bf16[256,512]{1,0:T(8,128)(2,1)S(1)} %add_convert_fusion.2), channel_id=1, source_target_pairs={{0,2},{1,15},{2,4},{3,1},{4,6},{5,3},{6,8},{7,5},{8,10},{9,7},{10,... | collective-permute-start | bytes 786440 | tf_op jit(solution)/shard_map/ppermute | solution.py:329
  28.8 2.6 %collective-permute-start.11 = (bf16[256,512]{1,0:T(8,128)(2,1)S(1)}, bf16[256,512]{1,0:T(8,128)(2,1)S(1)}, u32[]{:S(2)}, u32[]{:S(2)}) collective-permute-start(bf16[256,512]{1,0:T(8,128)(2,1)S(1)} %add_convert_fusion.5), channel_id=1, source_target_pairs={{0,2},{1,15},{2,4},{3,1},{4,6},{5,3},{6,8},{7,5},{8,10},{9,7},{10,... | collective-permute-start | bytes 786440 | tf_op jit(solution)/shard_map/ppermute | solution.py:329
  31.4 2.6 %collective-permute-start.3 = (bf16[256,512]{1,0:T(8,128)(2,1)S(1)}, bf16[256,512]{1,0:T(8,128)(2,1)S(1)}, u32[]{:S(2)}, u32[]{:S(2)}) collective-permute-start(bf16[256,512]{1,0:T(8,128)(2,1)S(1)} %add_convert_fusion.11), channel_id=1, source_target_pairs={{0,2},{1,15},{2,4},{3,1},{4,6},{5,3},{6,8},{7,5},{8,10},{9,7},{10,... | collective-permute-start | bytes 786440 | tf_op jit(solution)/shard_map/ppermute | solution.py:329
  36.1 3.3 %collective-permute-start.16 = (bf16[256,512]{1,0:T(8,128)(2,1)S(1)}, bf16[256,512]{1,0:T(8,128)(2,1)S(1)}, u32[]{:S(2)}, u32[]{:S(2)}) collective-permute-start(bf16[256,512]{1,0:T(8,128)(2,1)S(1)} %add_convert_fusion.1), channel_id=1, source_target_pairs={{0,2},{1,15},{2,4},{3,1},{4,6},{5,3},{6,8},{7,5},{8,10},{9,7},{10,... | collective-permute-start | bytes 786440 | tf_op jit(solution)/shard_map/ppermute | solution.py:329
  39.5 3.5 %collective-permute-start.12 = (bf16[256,512]{1,0:T(8,128)(2,1)S(1)}, bf16[256,512]{1,0:T(8,128)(2,1)S(1)}, u32[]{:S(2)}, u32[]{:S(2)}) collective-permute-start(bf16[256,512]{1,0:T(8,128)(2,1)S(1)} %add_convert_fusion.4), channel_id=1, source_target_pairs={{0,2},{1,15},{2,4},{3,1},{4,6},{5,3},{6,8},{7,5},{8,10},{9,7},{10,... | collective-permute-start | bytes 786440 | tf_op jit(solution)/shard_map/ppermute | solution.py:329
  43.0 3.5 %collective-permute-start.4 = (bf16[256,512]{1,0:T(8,128)(2,1)S(1)}, bf16[256,512]{1,0:T(8,128)(2,1)S(1)}, u32[]{:S(2)}, u32[]{:S(2)}) collective-permute-start(bf16[256,512]{1,0:T(8,128)(2,1)S(1)} %add_convert_fusion.10), channel_id=1, source_target_pairs={{0,2},{1,15},{2,4},{3,1},{4,6},{5,3},{6,8},{7,5},{8,10},{9,7},{10,... | collective-permute-start | bytes 786440 | tf_op jit(solution)/shard_map/ppermute | solution.py:329
  46.6 4.7 %collective-permute-start.8 = (bf16[256,512]{1,0:T(8,128)(2,1)S(1)}, bf16[256,512]{1,0:T(8,128)(2,1)S(1)}, u32[]{:S(2)}, u32[]{:S(2)}) collective-permute-start(bf16[256,512]{1,0:T(8,128)(2,1)S(1)} %add_convert_fusion.7), channel_id=1, source_target_pairs={{0,2},{1,15},{2,4},{3,1},{4,6},{5,3},{6,8},{7,5},{8,10},{9,7},{10,... | collective-permute-start | bytes 786440 | tf_op jit(solution)/shard_map/ppermute | solution.py:329
  53.4 2.4 %collective-permute-start.13 = (bf16[256,512]{1,0:T(8,128)(2,1)S(1)}, bf16[256,512]{1,0:T(8,128)(2,1)S(1)}, u32[]{:S(2)}, u32[]{:S(2)}) collective-permute-start(bf16[256,512]{1,0:T(8,128)(2,1)S(1)} %add_convert_fusion.3), channel_id=1, source_target_pairs={{0,1},{1,0},{2,3},{3,2},{4,5},{5,4},{6,7},{7,6},{8,9},{9,8},{10,11... | collective-permute-start | bytes 786440 | tf_op jit(solution)/shard_map/ppermute | solution.py:342
  55.9 2.6 %collective-permute-start.5 = (bf16[256,512]{1,0:T(8,128)(2,1)S(1)}, bf16[256,512]{1,0:T(8,128)(2,1)S(1)}, u32[]{:S(2)}, u32[]{:S(2)}) collective-permute-start(bf16[256,512]{1,0:T(8,128)(2,1)S(1)} %add_convert_fusion.9), channel_id=1, source_target_pairs={{0,2},{1,15},{2,4},{3,1},{4,6},{5,3},{6,8},{7,5},{8,10},{9,7},{10,... | collective-permute-start | bytes 786440 | tf_op jit(solution)/shard_map/ppermute | solution.py:329
  58.6 2.6 %collective-permute-start.9 = (bf16[256,512]{1,0:T(8,128)(2,1)S(1)}, bf16[256,512]{1,0:T(8,128)(2,1)S(1)}, u32[]{:S(2)}, u32[]{:S(2)}) collective-permute-start(bf16[256,512]{1,0:T(8,128)(2,1)S(1)} %add_convert_fusion.6), channel_id=1, source_target_pairs={{0,2},{1,15},{2,4},{3,1},{4,6},{5,3},{6,8},{7,5},{8,10},{9,7},{10,... | collective-permute-start | bytes 786440 | tf_op jit(solution)/shard_map/ppermute | solution.py:329
  62.5 2.8 %collective-permute-done.5.refs_0_ = bf16[256,512]{1,0:T(8,128)(2,1)S(1)} collective-permute-done((bf16[256,512]{1,0:T(8,128)(2,1)S(1)}, bf16[256,512]{1,0:T(8,128)(2,1)S(1)}, u32[]{:S(2)}, u32[]{:S(2)}) %collective-permute-start.5) | collective-permute-done | bytes 262176 | tf_op jit(solution)/shard_map/ppermute | solution.py:329
  65.4 2.8 %collective-permute-done.9.refs_1_ = bf16[256,512]{1,0:T(8,128)(2,1)S(1)} collective-permute-done((bf16[256,512]{1,0:T(8,128)(2,1)S(1)}, bf16[256,512]{1,0:T(8,128)(2,1)S(1)}, u32[]{:S(2)}, u32[]{:S(2)}) %collective-permute-start.9) | collective-permute-done | bytes 262176 | tf_op jit(solution)/shard_map/ppermute | solution.py:329
  68.3 13.0 %all_to_all.20.got_ref = bf16[4,512,128]{2,1,0:T(8,128)(2,1)S(1)} all-to-all(bf16[4,512,128]{2,1,0:T(8,128)(2,1)S(1)} %shard_map.94), channel_id=1, replica_groups={{0,16,32,48},{64,80,96,112},{128,144,160,176},{192,208,224,240},{256,27..., dimensions={0} | all-to-all | bytes 1048576 | tf_op jit(solution)/shard_map/all_to_all | solution.py:355
  81.4 24.4 %all_to_all.21.got_ref = bf16[12,48,128]{2,1,0:T(8,128)(2,1)S(1)} all-to-all(bf16[12,48,128]{2,1,0:T(8,128)(2,1)S(1)} %shard_map.95), channel_id=1, replica_groups={{0,64,128,192,256,320,384,448,512,576,640,704},{16,80,144,208,272,336,4..., dimensions={0} | all-to-all | bytes 294912 | tf_op jit(solution)/shard_map/all_to_all | solution.py:358
  105.8 14.9 %all_to_all.22.got_ref = bf16[12,64,128]{2,1,0:T(8,128)(2,1)S(1)} all-to-all(bf16[12,64,128]{2,1,0:T(8,128)(2,1)S(1)} %shard_map.96), channel_id=1, replica_groups={{0,64,128,192,256,320,384,448,512,576,640,704},{16,80,144,208,272,336,4..., dimensions={0} | all-to-all | bytes 393216 | tf_op jit(solution)/shard_map/all_to_all | solution.py:362
  121.5 7.0 %all-to-all-start.3 = ((f32[64,8,128]{2,1,0:T(8,128)}), f32[64,8,128]{2,1,0:T(8,128)S(1)}, u32[]{:S(2)}, u32[]{:S(2)}) async-start(f32[64,8,128]{2,1,0:T(8,128)} %get-tuple-element.66), calls=%async_computation.3 | async-start | bytes 524288 | tf_op jit(solution)/shard_map/all_to_all | solution.py:372
  128.5 2.8 %collective-permute-start.18 = (bf16[528,128]{1,0:T(8,128)(2,1)S(1)}, bf16[528,128]{1,0:T(8,128)(2,1)S(1)}, u32[]{:S(2)}, u32[]{:S(2)}) collective-permute-start(bf16[528,128]{1,0:T(8,128)(2,1)S(1)} %get-tuple-element.70.refs_0_), channel_id=1, source_target_pairs={{0,16},{16,0},{32,48},{48,32},{64,80},{80,64},{96,112},{112,96},{1... | collective-permute-start | bytes 405512 | tf_op jit(solution)/shard_map/ppermute | solution.py:378
  131.3 3.0 %collective-permute-start.20 = (bf16[528,128]{1,0:T(8,128)(2,1)S(1)}, bf16[528,128]{1,0:T(8,128)(2,1)S(1)}, u32[]{:S(2)}, u32[]{:S(2)}) collective-permute-start(bf16[528,128]{1,0:T(8,128)(2,1)S(1)} %get-tuple-element.70.refs_0_), channel_id=1, source_target_pairs={{0,48},{16,32},{32,16},{48,0},{64,112},{80,96},{96,80},{112,64},{1... | collective-permute-start | bytes 405512 | tf_op jit(solution)/shard_map/ppermute | solution.py:378
  134.3 3.9 %collective-permute-done.18.refs_1_ = bf16[528,128]{1,0:T(8,128)(2,1)S(1)} collective-permute-done((bf16[528,128]{1,0:T(8,128)(2,1)S(1)}, bf16[528,128]{1,0:T(8,128)(2,1)S(1)}, u32[]{:S(2)}, u32[]{:S(2)}) %collective-permute-start.18) | collective-permute-done | bytes 135200 | tf_op jit(solution)/shard_map/ppermute | solution.py:378
  140.4 5.9 %collective-permute-done.19.refs_2_ = bf16[528,128]{1,0:T(8,128)(2,1)S(1)} collective-permute-done((bf16[528,128]{1,0:T(8,128)(2,1)S(1)}, bf16[528,128]{1,0:T(8,128)(2,1)S(1)}, u32[]{:S(2)}, u32[]{:S(2)}) %collective-permute-start.19) | collective-permute-done | bytes 135200 | tf_op jit(solution)/shard_map/ppermute | solution.py:378
  (60 shorter events, 22.4 us)
Async XLA Ops:
  2.8 5.5 %collective-permute-start = (bf16[128,2048]{1,0:T(8,128)(2,1)S(1)}, bf16[128,2048]{1,0:T(8,128)(2,1)S(1)}, u32[]{:S(2)}, u32[]{:S(2)}) collective-permute-start(bf16[128,2048]{1,0:T(8,128)(2,1)S(1)} %get-tuple-element.40), channel_id=1, source_target_pairs={{0,1},{1,0},{2,3},{3,2},{4,5},{5,4},{6,7},{7,6},{8,9},{9,8},{10,11... | collective-permute-start | bytes 1572872 | tf_op jit(solution)/shard_map/ppermute | solution.py:316
  4.7 3.6 %collective-permute-start.1 = (bf16[128,1024]{1,0:T(8,128)(2,1)S(1)}, bf16[128,1024]{1,0:T(8,128)(2,1)S(1)}, u32[]{:S(2)}, u32[]{:S(2)}) collective-permute-start(bf16[128,1024]{1,0:T(8,128)(2,1)S(1)} %copy-done.2), channel_id=1, source_target_pairs={{0,1},{1,0},{2,3},{3,2},{4,5},{5,4},{6,7},{7,6},{8,9},{9,8},{10,11... | collective-permute-start | bytes 786440 | tf_op jit(solution)/shard_map/ppermute | solution.py:314
  10.8 15.2 %collective-permute-start.14 = (bf16[256,512]{1,0:T(8,128)(2,1)S(1)}, bf16[256,512]{1,0:T(8,128)(2,1)S(1)}, u32[]{:S(2)}, u32[]{:S(2)}) collective-permute-start(bf16[256,512]{1,0:T(8,128)(2,1)S(1)} %get-tuple-element.53), channel_id=1, source_target_pairs={{0,2},{1,15},{2,4},{3,1},{4,6},{5,3},{6,8},{7,5},{8,10},{9,7},{10,... | collective-permute-start | bytes 786440 | tf_op jit(solution)/shard_map/ppermute | solution.py:329
  14.3 14.4 %collective-permute-start.10 = (bf16[256,512]{1,0:T(8,128)(2,1)S(1)}, bf16[256,512]{1,0:T(8,128)(2,1)S(1)}, u32[]{:S(2)}, u32[]{:S(2)}) collective-permute-start(bf16[256,512]{1,0:T(8,128)(2,1)S(1)} %get-tuple-element.49), channel_id=1, source_target_pairs={{0,2},{1,15},{2,4},{3,1},{4,6},{5,3},{6,8},{7,5},{8,10},{9,7},{10,... | collective-permute-start | bytes 786440 | tf_op jit(solution)/shard_map/ppermute | solution.py:329
  17.8 13.5 %collective-permute-start.2 = (bf16[256,512]{1,0:T(8,128)(2,1)S(1)}, bf16[256,512]{1,0:T(8,128)(2,1)S(1)}, u32[]{:S(2)}, u32[]{:S(2)}) collective-permute-start(bf16[256,512]{1,0:T(8,128)(2,1)S(1)} %get-tuple-element.41.outs_0_), channel_id=1, source_target_pairs={{0,2},{1,15},{2,4},{3,1},{4,6},{5,3},{6,8},{7,5},{8,10},{9,7},{10,... | collective-permute-start | bytes 786440 | tf_op jit(solution)/shard_map/ppermute | solution.py:329
  21.3 12.7 %collective-permute-start.6 = (bf16[256,512]{1,0:T(8,128)(2,1)S(1)}, bf16[256,512]{1,0:T(8,128)(2,1)S(1)}, u32[]{:S(2)}, u32[]{:S(2)}) collective-permute-start(bf16[256,512]{1,0:T(8,128)(2,1)S(1)} %get-tuple-element.45), channel_id=1, source_target_pairs={{0,2},{1,15},{2,4},{3,1},{4,6},{5,3},{6,8},{7,5},{8,10},{9,7},{10,... | collective-permute-start | bytes 786440 | tf_op jit(solution)/shard_map/ppermute | solution.py:329
  26.1 10.0 %collective-permute-start.15 = (bf16[256,512]{1,0:T(8,128)(2,1)S(1)}, bf16[256,512]{1,0:T(8,128)(2,1)S(1)}, u32[]{:S(2)}, u32[]{:S(2)}) collective-permute-start(bf16[256,512]{1,0:T(8,128)(2,1)S(1)} %add_convert_fusion.2), channel_id=1, source_target_pairs={{0,2},{1,15},{2,4},{3,1},{4,6},{5,3},{6,8},{7,5},{8,10},{9,7},{10,... | collective-permute-start | bytes 786440 | tf_op jit(solution)/shard_map/ppermute | solution.py:329
  28.8 10.6 %collective-permute-start.11 = (bf16[256,512]{1,0:T(8,128)(2,1)S(1)}, bf16[256,512]{1,0:T(8,128)(2,1)S(1)}, u32[]{:S(2)}, u32[]{:S(2)}) collective-permute-start(bf16[256,512]{1,0:T(8,128)(2,1)S(1)} %add_convert_fusion.5), channel_id=1, source_target_pairs={{0,2},{1,15},{2,4},{3,1},{4,6},{5,3},{6,8},{7,5},{8,10},{9,7},{10,... | collective-permute-start | bytes 786440 | tf_op jit(solution)/shard_map/ppermute | solution.py:329
  31.4 11.5 %collective-permute-start.3 = (bf16[256,512]{1,0:T(8,128)(2,1)S(1)}, bf16[256,512]{1,0:T(8,128)(2,1)S(1)}, u32[]{:S(2)}, u32[]{:S(2)}) collective-permute-start(bf16[256,512]{1,0:T(8,128)(2,1)S(1)} %add_convert_fusion.11), channel_id=1, source_target_pairs={{0,2},{1,15},{2,4},{3,1},{4,6},{5,3},{6,8},{7,5},{8,10},{9,7},{10,... | collective-permute-start | bytes 786440 | tf_op jit(solution)/shard_map/ppermute | solution.py:329
  34.1 12.4 %collective-permute-start.7 = (bf16[256,512]{1,0:T(8,128)(2,1)S(1)}, bf16[256,512]{1,0:T(8,128)(2,1)S(1)}, u32[]{:S(2)}, u32[]{:S(2)}) collective-permute-start(bf16[256,512]{1,0:T(8,128)(2,1)S(1)} %add_convert_fusion.8), channel_id=1, source_target_pairs={{0,2},{1,15},{2,4},{3,1},{4,6},{5,3},{6,8},{7,5},{8,10},{9,7},{10,... | collective-permute-start | bytes 786440 | tf_op jit(solution)/shard_map/ppermute | solution.py:329
  36.1 15.2 %collective-permute-start.16 = (bf16[256,512]{1,0:T(8,128)(2,1)S(1)}, bf16[256,512]{1,0:T(8,128)(2,1)S(1)}, u32[]{:S(2)}, u32[]{:S(2)}) collective-permute-start(bf16[256,512]{1,0:T(8,128)(2,1)S(1)} %add_convert_fusion.1), channel_id=1, source_target_pairs={{0,2},{1,15},{2,4},{3,1},{4,6},{5,3},{6,8},{7,5},{8,10},{9,7},{10,... | collective-permute-start | bytes 786440 | tf_op jit(solution)/shard_map/ppermute | solution.py:329
  39.5 13.8 %collective-permute-start.12 = (bf16[256,512]{1,0:T(8,128)(2,1)S(1)}, bf16[256,512]{1,0:T(8,128)(2,1)S(1)}, u32[]{:S(2)}, u32[]{:S(2)}) collective-permute-start(bf16[256,512]{1,0:T(8,128)(2,1)S(1)} %add_convert_fusion.4), channel_id=1, source_target_pairs={{0,2},{1,15},{2,4},{3,1},{4,6},{5,3},{6,8},{7,5},{8,10},{9,7},{10,... | collective-permute-start | bytes 786440 | tf_op jit(solution)/shard_map/ppermute | solution.py:329
  43.0 12.8 %collective-permute-start.4 = (bf16[256,512]{1,0:T(8,128)(2,1)S(1)}, bf16[256,512]{1,0:T(8,128)(2,1)S(1)}, u32[]{:S(2)}, u32[]{:S(2)}) collective-permute-start(bf16[256,512]{1,0:T(8,128)(2,1)S(1)} %add_convert_fusion.10), channel_id=1, source_target_pairs={{0,2},{1,15},{2,4},{3,1},{4,6},{5,3},{6,8},{7,5},{8,10},{9,7},{10,... | collective-permute-start | bytes 786440 | tf_op jit(solution)/shard_map/ppermute | solution.py:329
  46.6 11.9 %collective-permute-start.8 = (bf16[256,512]{1,0:T(8,128)(2,1)S(1)}, bf16[256,512]{1,0:T(8,128)(2,1)S(1)}, u32[]{:S(2)}, u32[]{:S(2)}) collective-permute-start(bf16[256,512]{1,0:T(8,128)(2,1)S(1)} %add_convert_fusion.7), channel_id=1, source_target_pairs={{0,2},{1,15},{2,4},{3,1},{4,6},{5,3},{6,8},{7,5},{8,10},{9,7},{10,... | collective-permute-start | bytes 786440 | tf_op jit(solution)/shard_map/ppermute | solution.py:329
  51.4 11.2 %collective-permute-start.17 = (bf16[256,512]{1,0:T(8,128)(2,1)S(1)}, bf16[256,512]{1,0:T(8,128)(2,1)S(1)}, u32[]{:S(2)}, u32[]{:S(2)}) collective-permute-start(bf16[256,512]{1,0:T(8,128)(2,1)S(1)} %add_convert_fusion), channel_id=1, source_target_pairs={{0,1},{1,0},{2,3},{3,2},{4,5},{5,4},{6,7},{7,6},{8,9},{9,8},{10,11... | collective-permute-start | bytes 786440 | tf_op jit(solution)/shard_map/ppermute | solution.py:342
  53.4 9.2 %collective-permute-start.13 = (bf16[256,512]{1,0:T(8,128)(2,1)S(1)}, bf16[256,512]{1,0:T(8,128)(2,1)S(1)}, u32[]{:S(2)}, u32[]{:S(2)}) collective-permute-start(bf16[256,512]{1,0:T(8,128)(2,1)S(1)} %add_convert_fusion.3), channel_id=1, source_target_pairs={{0,1},{1,0},{2,3},{3,2},{4,5},{5,4},{6,7},{7,6},{8,9},{9,8},{10,11... | collective-permute-start | bytes 786440 | tf_op jit(solution)/shard_map/ppermute | solution.py:342
  55.9 9.5 %collective-permute-start.5 = (bf16[256,512]{1,0:T(8,128)(2,1)S(1)}, bf16[256,512]{1,0:T(8,128)(2,1)S(1)}, u32[]{:S(2)}, u32[]{:S(2)}) collective-permute-start(bf16[256,512]{1,0:T(8,128)(2,1)S(1)} %add_convert_fusion.9), channel_id=1, source_target_pairs={{0,2},{1,15},{2,4},{3,1},{4,6},{5,3},{6,8},{7,5},{8,10},{9,7},{10,... | collective-permute-start | bytes 786440 | tf_op jit(solution)/shard_map/ppermute | solution.py:329
  58.6 2.7 %copy-start.5 = (f32[1,1,4,16]{3,2,1,0:T(4,128)S(1)}, f32[1,1,4,16]{3,2,1,0:T(4,128)}, u32[]{:S(2)}) copy-start(f32[1,1,4,16]{3,2,1,0:T(4,128)} %param.11) | copy-start | bytes 772
  58.6 9.6 %collective-permute-start.9 = (bf16[256,512]{1,0:T(8,128)(2,1)S(1)}, bf16[256,512]{1,0:T(8,128)(2,1)S(1)}, u32[]{:S(2)}, u32[]{:S(2)}) collective-permute-start(bf16[256,512]{1,0:T(8,128)(2,1)S(1)} %add_convert_fusion.6), channel_id=1, source_target_pairs={{0,2},{1,15},{2,4},{3,1},{4,6},{5,3},{6,8},{7,5},{8,10},{9,7},{10,... | collective-permute-start | bytes 786440 | tf_op jit(solution)/shard_map/ppermute | solution.py:329
  121.5 26.6 %all-to-all-start.3 = ((f32[64,8,128]{2,1,0:T(8,128)}), f32[64,8,128]{2,1,0:T(8,128)S(1)}, u32[]{:S(2)}, u32[]{:S(2)}) async-start(f32[64,8,128]{2,1,0:T(8,128)} %get-tuple-element.66), calls=%async_computation.3 | async-start | bytes 524288 | tf_op jit(solution)/shard_map/all_to_all | solution.py:372
  128.5 19.6 %copy-start.1 = (bf16[256,1024]{1,0:T(8,128)(2,1)S(1)}, bf16[256,1024]{1,0:T(8,128)(2,1)}, u32[]{:S(2)}) copy-start(bf16[256,1024]{1,0:T(8,128)(2,1)} %weight_ref.1) | copy-start | bytes 1572868
  128.5 9.6 %collective-permute-start.18 = (bf16[528,128]{1,0:T(8,128)(2,1)S(1)}, bf16[528,128]{1,0:T(8,128)(2,1)S(1)}, u32[]{:S(2)}, u32[]{:S(2)}) collective-permute-start(bf16[528,128]{1,0:T(8,128)(2,1)S(1)} %get-tuple-element.70.refs_0_), channel_id=1, source_target_pairs={{0,16},{16,0},{32,48},{48,32},{64,80},{80,64},{96,112},{112,96},{1... | collective-permute-start | bytes 405512 | tf_op jit(solution)/shard_map/ppermute | solution.py:378
  131.3 9.0 %collective-permute-start.20 = (bf16[528,128]{1,0:T(8,128)(2,1)S(1)}, bf16[528,128]{1,0:T(8,128)(2,1)S(1)}, u32[]{:S(2)}, u32[]{:S(2)}) collective-permute-start(bf16[528,128]{1,0:T(8,128)(2,1)S(1)} %get-tuple-element.70.refs_0_), channel_id=1, source_target_pairs={{0,48},{16,32},{32,16},{48,0},{64,112},{80,96},{96,80},{112,64},{1... | collective-permute-start | bytes 405512 | tf_op jit(solution)/shard_map/ppermute | solution.py:378
  138.2 8.1 %collective-permute-start.19 = (bf16[528,128]{1,0:T(8,128)(2,1)S(1)}, bf16[528,128]{1,0:T(8,128)(2,1)S(1)}, u32[]{:S(2)}, u32[]{:S(2)}) collective-permute-start(bf16[528,128]{1,0:T(8,128)(2,1)S(1)} %collective-permute-done.18.refs_1_), channel_id=1, source_target_pairs={{0,48},{16,32},{32,16},{48,0},{64,112},{80,96},{96,80},{112,64},{1... | collective-permute-start | bytes 405512 | tf_op jit(solution)/shard_map/ppermute | solution.py:378
  (5 other events, 8.6 us)

commit v5 on v3

--- a/solution.py
+++ b/solution.py
@@ -106,7 +106,7 @@
     )(a, b)
 
 
-def small_kernel(body, out_shape, *operands, scalars=0, scratch=()):
+def small_kernel(body, out_shape, *operands, scalars=0):
     vmem = pl.BlockSpec(memory_space=pltpu.VMEM)
     smem = pl.BlockSpec(memory_space=pltpu.SMEM)
     size = sum(a.size for a in operands)
@@ -115,7 +115,6 @@
         out_shape=out_shape,
         in_specs=[smem] * scalars + [vmem] * (len(operands) - scalars),
         out_specs=jax.tree.map(lambda _: vmem, out_shape),
-        scratch_shapes=scratch,
         cost_estimate=pl.CostEstimate(flops=size, bytes_accessed=4 * size, transcendentals=0),
         compiler_params=pltpu.CompilerParams(vmem_limit_bytes=8 << 20),
     )(*operands)
@@ -125,102 +124,96 @@
     return sum(ref[j, rows, :].astype(jnp.float32) for j in range(ref.shape[0]))
 
 
-def sum_x_kernel(got_ref, out_ref):
-    rows = out_ref.shape[1]
+def sum_x_kernel(rows, got_ref, out_ref):
+    total = total_of(got_ref)
+    full, head = total.shape
     for j in range(out_ref.shape[0]):
-        begin = min(j * rows, got_ref.shape[1])
-        end = min(begin + rows, got_ref.shape[1])
-        if end > begin:
-            out_ref[j, : end - begin, :] = total_of(got_ref, slice(begin, end)).astype(out_ref.dtype)
-        if end - begin < rows:
-            out_ref[j, end - begin :, :] = jnp.zeros(
-                (rows - end + begin, out_ref.shape[2]), out_ref.dtype
-            )
+        begin, end = min(j * rows, full), min(j * rows + rows, full)
+        fill = jnp.zeros((out_ref.shape[1] - end + begin, head), jnp.float32)
+        block = jnp.concatenate([total[begin:end], fill], axis=0)
+        out_ref[j] = block.astype(out_ref.dtype)
 
 
 def sum_z_kernel(got_ref, extra_ref, out_ref):
-    rows = got_ref.shape[1]
-    total = total_of(got_ref).astype(out_ref.dtype)
+    total = total_of(got_ref) + extra_ref[...].astype(jnp.float32)
     for j in range(out_ref.shape[0]):
-        out_ref[j, :rows, :] = total
-        out_ref[j, rows:, :] = extra_ref[...]
+        out_ref[j] = total.astype(out_ref.dtype)
 
 
 def pack_kernel(rows, got_ref, out_ref, stats_ref):
     count, _, head = got_ref.shape
     pad = -count % 16
     full = out_ref.shape[0] - count - pad
-    cols = [jnp.zeros((1, head), jnp.float32)] * 2
-    for j in range(count):
-        begin = min(j * rows, full)
-        end = min(begin + rows, full)
-        if end > begin:
-            out_ref[begin:end, :] = got_ref[j, : end - begin, :]
-        for t in range(2):
-            low, high = max(begin, t * full // 2), min(end, (t + 1) * full // 2)
-            if high > low:
-                part = got_ref[j, low - begin : high - begin, :].astype(jnp.float32)
-                cols[t] = cols[t] + jnp.sum(part * part, axis=0, keepdims=True)
-    extra = [got_ref[j, rows : rows + 16, :].astype(jnp.float32) for j in range(count)]
-    tail = [e[:1] for e in extra] + [jnp.zeros((pad, head), jnp.float32)]
-    tail = jnp.concatenate(tail, axis=0).astype(out_ref.dtype)
-    out_ref[full:, :] = tail
-    sums = sum(e[1:2] for e in extra)
-    stats = cols + [sums, jnp.zeros((stats_ref.shape[1] - 3, head), jnp.float32)]
+    blocks = [got_ref[j].astype(jnp.float32) for j in range(count)]
+    grad = jnp.concatenate([block[:rows] for block in blocks], axis=0)[:full]
+    out_ref[:full, :] = grad.astype(out_ref.dtype)
+    tail = [block[rows : rows + 1] for block in blocks] + [jnp.zeros((pad, head), jnp.float32)]
+    out_ref[full:, :] = jnp.concatenate(tail, axis=0).astype(out_ref.dtype)
+    squares = grad * grad
+    half = full // 2
+    stats = [jnp.sum(squares[t * half : (t + 1) * half], axis=0, keepdims=True) for t in range(2)]
+    stats.append(sum(block[rows + 1 : rows + 2] for block in blocks))
+    stats.append(jnp.zeros((stats_ref.shape[1] - 3, head), jnp.float32))
     stats = jnp.concatenate(stats, axis=0)
     for j in range(stats_ref.shape[0]):
         stats_ref[j] = stats
 
 
-def rows_kernel(index_ref, state_ref, pick_ref, lane_ref, *refs):
-    *got, out_ref, own_ref, mean_ref = refs
+def update_kernel(index_ref, state_ref, pick_ref, lane_ref, *refs):
+    *got, stats_ref, weight_ref, col_state_ref, out_ref, own_ref, col_ref = refs
     my_x = lax.axis_index("grp") % N_X
-    head = out_ref.shape[1]
-    full = out_ref.shape[0] // N_X
-    slab = full // 2
+    tensors, head = col_ref.shape
+    slab = weight_ref.shape[0]
+    full = pick_ref.shape[0] // N_X
+    plane = stats_ref.shape[0] // N_X
+    d_model = slab * plane
+
+    sums = jnp.sum(stats_ref[:, 2, :], axis=0, keepdims=True)
+    factors = []
+    for t in range(tensors):
+        x = t // 2
+        col = jnp.sum(stats_ref[x * plane : (x + 1) * plane, t % 2, :], axis=0, keepdims=True)
+        col = col / d_model + epsilon
+        col_new = decay_rate * col_state_ref[t : t + 1, :] + (1.0 - decay_rate) * col
+        col_ref[t : t + 1, :] = col_new
+        prev = (sums[:, t : t + 1] + sums[:, tensors + t : tensors + t + 1]) / d_model
+        average = decay_rate * prev + (1.0 - decay_rate) * jnp.mean(col, axis=1, keepdims=True)
+        factors.append(step_size * lax.rsqrt(col_new / average))
+
     states = jnp.concatenate([ref[full:, :] for ref in got], axis=0)
-    for k, ref in enumerate(got):
-        for t in range(2):
-            begin = (my_x ^ k) * full + t * slab
-            where = pl.ds(pl.multiple_of(begin, slab), slab)
-            grad = ref[t * slab : (t + 1) * slab, :].astype(jnp.float32)
-            state = jnp.dot(pick_ref[where, :], states, preferred_element_type=jnp.float32)
-            prev = jnp.sum(state * lane_ref[where, :].astype(jnp.float32), axis=1, keepdims=True)
-            mean = jnp.sum(grad * grad, axis=1, keepdims=True) / head + epsilon
-            mean_ref[where, :] = jnp.broadcast_to(mean, (slab, head))
-            out_ref[where, :] = grad * lax.rsqrt(decay_rate * prev + (1.0 - decay_rate) * mean)
+    for t in range(tensors):
+        rows = slice((t % 2) * slab, (t % 2 + 1) * slab)
+        grad = got[0][rows, :]
+        for k in range(1, N_X):
+            grad = jnp.where((my_x ^ k) == t // 2, got[k][rows, :], grad)
+        grad = grad.astype(jnp.float32)
+        where = slice(t * slab, (t + 1) * slab)
+        state = jnp.dot(pick_ref[where, :], states, preferred_element_type=jnp.float32)
+        prev = jnp.sum(state * lane_ref[where, :].astype(jnp.float32), axis=1, keepdims=True)
+        mean = jnp.sum(grad * grad, axis=1, keepdims=True) / head + epsilon
+        scale = lax.rsqrt(decay_rate * prev + (1.0 - decay_rate) * mean)
+        cols = slice(t * head, (t + 1) * head)
+        change = grad * scale * factors[t]
+        out_ref[:, cols] = (weight_ref[:, cols].astype(jnp.float32) - change).astype(out_ref.dtype)
+
     capacity, unit_rows = own_ref.shape
+    per_piece = full // unit_rows
     shape = (unit_rows, unit_rows)
     eye = lax.broadcasted_iota(jnp.int32, shape, 0) == lax.broadcasted_iota(jnp.int32, shape, 1)
     for c in range(capacity):
         unit = jnp.maximum(index_ref[c], 0)
-        column = mean_ref[pl.ds(pl.multiple_of(unit * unit_rows, unit_rows), unit_rows), :]
-        mean = jnp.sum(jnp.where(eye, column[:, :unit_rows], 0.0), axis=0, keepdims=True)
+        rows = pl.ds(pl.multiple_of((unit % per_piece) * unit_rows, unit_rows), unit_rows)
+        grad = got[0][rows, :]
+        for k in range(1, N_X):
+            grad = jnp.where((my_x ^ k) == unit // per_piece, got[k][rows, :], grad)
+        grad = grad.astype(jnp.float32)
+        mean = jnp.sum(grad * grad, axis=1, keepdims=True) / head + epsilon
+        mean = jnp.sum(jnp.where(eye, mean, 0.0), axis=0, keepdims=True)
         new = decay_rate * state_ref[c : c + 1, :] + (1.0 - decay_rate) * mean
         own_ref[c : c + 1, :] = jnp.where(index_ref[c] >= 0, new, 0.0)
 
 
-def update_kernel(stats_ref, grad_ref, weight_ref, state_ref, out_ref, col_ref):
-    tensors, head = state_ref.shape
-    slab = weight_ref.shape[0]
-    d_model = slab * stats_ref.shape[0] // N_X
-    plane = stats_ref.shape[0] // N_X
-    sums = jnp.sum(stats_ref[:, 2, :], axis=0, keepdims=True)
-    for t in range(tensors):
-        x = t // 2
-        col = jnp.sum(stats_ref[x * plane : (x + 1) * plane, t % 2, :], axis=0, keepdims=True)
-        col = col / d_model + epsilon
-        col_new = decay_rate * state_ref[t : t + 1, :] + (1.0 - decay_rate) * col
-        col_ref[t : t + 1, :] = col_new
-        prev = (sums[:, t : t + 1] + sums[:, tensors + t : tensors + t + 1]) / d_model
-        average = decay_rate * prev + (1.0 - decay_rate) * jnp.mean(col, axis=1, keepdims=True)
-        factor = step_size * lax.rsqrt(col_new / average)
-        cols = slice(t * head, (t + 1) * head)
-        change = grad_ref[t * slab : (t + 1) * slab, :] * factor
-        out_ref[:, cols] = (weight_ref[:, cols].astype(jnp.float32) - change).astype(out_ref.dtype)
-
-
-def tables_kernel(owner_ref, state_ref, pick_ref, lane_ref, extra_ref, index_ref):
+def tables_kernel(row, owner_ref, state_ref, pick_ref, lane_ref, extra_ref, index_ref):
     f32, bf16 = jnp.float32, jnp.bfloat16
     me = lax.axis_index("grp")
     units = owner_ref.shape[0]
@@ -272,22 +265,23 @@
     value = jnp.sum(jnp.where(here, sums, 0.0), axis=0, keepdims=True)
     high = value.astype(bf16).astype(f32)
     sum_row = jnp.where(at((1, head), 1) < tensors, high, value - high)
-    rows = [state_row, sum_row, jnp.zeros((extra_ref.shape[0] - 2, head), f32)]
-    extra_ref[...] = jnp.concatenate(rows, axis=0).astype(bf16)
-
-
-def tables(owner_table, state, head, seats):
+    at_row = at(extra_ref.shape, 0)
+    extra = jnp.where(at_row == row, state_row, jnp.where(at_row == row + 1, sum_row, 0.0))
+    extra_ref[...] = extra.astype(bf16)
+
+
+def tables(owner_table, state, head, seats, row, rows):
     capacity, unit_rows = state.shape
     count = owner_table.shape[0] * unit_rows
     vmem = pl.BlockSpec(memory_space=pltpu.VMEM)
     smem = pl.BlockSpec(memory_space=pltpu.SMEM)
     bf16 = jnp.bfloat16
     return pl.pallas_call(
-        tables_kernel,
+        functools.partial(tables_kernel, row),
         out_shape=(
             jax.ShapeDtypeStruct((count, seats), bf16),
             jax.ShapeDtypeStruct((count, head), bf16),
-            jax.ShapeDtypeStruct((unit_rows, head), bf16),
+            jax.ShapeDtypeStruct((rows, head), bf16),
             jax.ShapeDtypeStruct((capacity,), jnp.int32),
         ),
         in_specs=[vmem, vmem],
@@ -343,29 +337,31 @@
     give = add(hop(second), parts[-1]).astype(bf16)
     other = lax.ppermute(give, "intra", swap)
     state_rows = n_z + -n_z % unit_rows
-    pick, lane, extra, my_index = tables(owner_table, row_state[0, 0], head, N_X * state_rows)
+    per_x = units // N_X
+    full = per_x * unit_rows
+    share = -(-full // (4 * n_z)) * 4
+    sent_rows = -(-(share + 2) // unit_rows) * unit_rows
+    pick, lane, extra, my_index = tables(
+        owner_table, row_state[0, 0], head, N_X * state_rows, share, sent_rows
+    )
     last, other, extra, pick, lane, my_index = lax.optimization_barrier(
         (last, other, extra, pick, lane, my_index)
     )
     own = finish(last, other, head)
 
 
-    per_x = units // N_X
-    per_z = -(-per_x // n_z)
     got = lax.all_to_all(own, "grp", 0, 0, axis_index_groups=x_groups, tiled=True)
-    sent = jax.ShapeDtypeStruct((n_z, per_z * unit_rows, head), bf16)
-    sent = small_kernel(sum_x_kernel, sent, got)
+    block = jax.ShapeDtypeStruct((n_z, sent_rows, head), bf16)
+    sent = small_kernel(functools.partial(sum_x_kernel, share), block, got)
     got = lax.all_to_all(sent, "grp", 0, 0, axis_index_groups=z_groups, tiled=True)
 
-    sent = jax.ShapeDtypeStruct((n_z, got.shape[1] + unit_rows, head), bf16)
-    sent = small_kernel(sum_z_kernel, sent, got, extra)
+    sent = small_kernel(sum_z_kernel, block, got, extra)
     got = lax.all_to_all(sent, "grp", 0, 0, axis_index_groups=z_groups, tiled=True)
-    full = per_x * unit_rows
     shapes = (
         jax.ShapeDtypeStruct((full + state_rows, head), bf16),
         jax.ShapeDtypeStruct((N_X * intra, 8, head), f32),
     )
-    body = functools.partial(pack_kernel, per_z * unit_rows)
+    body = functools.partial(pack_kernel, share)
     sent, stats = small_kernel(body, shapes, got)
     plane = N_X * intra
     planes = [list(range(z * plane, (z + 1) * plane)) for z in range(n_z)]
@@ -380,27 +376,24 @@
     near, wrap = trade(sent, 1), trade(sent, N_X - 1)
     fetched = [sent, near, trade(near, N_X - 1), wrap]
 
-    count = units * unit_rows
     shapes = (
-        jax.ShapeDtypeStruct((count, head), f32),
+        jax.ShapeDtypeStruct(weights.shape, weights.dtype),
         jax.ShapeDtypeStruct((capacity, unit_rows), f32),
-    )
-    scaled, row_moments = small_kernel(
-        rows_kernel,
+        jax.ShapeDtypeStruct(col_state.shape, f32),
+    )
+    new_weights, row_moments, col_new = small_kernel(
+        update_kernel,
         shapes,
         my_index,
         row_state[0, 0],
         pick,
         lane,
         *fetched,
+        stats,
+        weights,
+        col_state,
         scalars=1,
-        scratch=[pltpu.VMEM((count, head), f32)],
-    )
-    shapes = (
-        jax.ShapeDtypeStruct(weights.shape, weights.dtype),
-        jax.ShapeDtypeStruct(col_state.shape, f32),
-    )
-    new_weights, col_new = small_kernel(update_kernel, shapes, stats, scaled, weights, col_state)
+    )
     return (new_weights, row_moments[None, None], col_new)
 
 

time: 152 us -> 152 us (level)
    pallas_call x5 -> x4, Pallas kernels: 3.94 us -> 3.29 us  [small_kernel(): pl.pallas_call(body, out_shape=out_shape, in_specs=[smem] * scalars + [vm...]
  transfers between devices with their start and end apart: 14 -> 14, of which waited for: 10 -> 10; matrix products, arithmetic and copies ran while one was open for 1% -> 1% of each run, Pallas kernels for 2% -> 1%
where the time goes in v5:
time: 152 us; the launch traced here: 151 us
  blocking collectives  52 us (34%)
  waiting for transfers between devices  45.5 us (30%)
  starting transfers between devices  41.4 us (27%)
  Pallas kernels  7.37 us (5%)
  local copies, waits for them, and re-layouts  2.07 us (1%)
  other arithmetic  1.94 us (1%)
    ppermute x7, waiting for transfers between devices, hop(): return lax.ppermute(a, 'intra', ring)  34.5 us
    all_to_all x2, blocking collectives, on_device(): lax.all_to_all(sent, 'grp', 0, 0, axis_index_groups=z_groups, tiled=True)  34.3 us
    all_to_all x1, blocking collectives, on_device(): lax.all_to_all(own, 'grp', 0, 0, axis_index_groups=x_groups, tiled=True)  17.6 us
    ppermute x7, starting transfers between devices, hop(): return lax.ppermute(a, 'intra', ring)  16.9 us
    all_to_all x1, starting transfers between devices, on_device(): lax.all_to_all(stats, ('grp', 'intra'), 0, 0, axis_index_groups=planes, t...  10.4 us
    ppermute x3, waiting for transfers between devices, trade(): return lax.ppermute(a, 'grp', pairs)  9.83 us
    ppermute x3, starting transfers between devices, trade(): return lax.ppermute(a, 'grp', pairs)  7.8 us
    pallas_call x4, Pallas kernels, small_kernel(): pl.pallas_call(body, out_shape=out_shape, in_specs=[smem] * scalars + [vm...  3.29 us
  transfers between devices with their start and end apart: 14, of which 10 were waited for; matrix products, arithmetic and copies ran while one was open for 1% of the time, Pallas kernels for 1%

profile of v5, /device:TPU:6, one launch (start us, length us, event | category | flops | bytes accessed | tf_op | source)
XLA Modules:
  0.0 151.1 jit_solution(17762768911741400439)
XLA Ops:
  4.7 2.4 %collective-permute-start.1 = (bf16[128,1024]{1,0:T(8,128)(2,1)S(1)}, bf16[128,1024]{1,0:T(8,128)(2,1)S(1)}, u32[]{:S(2)}, u32[]{:S(2)}) collective-permute-start(bf16[128,1024]{1,0:T(8,128)(2,1)S(1)} %copy-done.2), channel_id=1, source_target_pairs={{0,1},{1,0},{2,3},{3,2},{4,5},{5,4},{6,7},{7,6},{8,9},{9,8},{10,11... | collective-permute-start | bytes 786440 | tf_op jit(solution)/shard_map/ppermute | solution.py:314
  8.7 2.1 %products.3 = (bf16[256,1024]{1,0:T(8,128)(2,1)S(1)}, bf16[256,1024]{1,0:T(8,128)(2,1)S(1)}, bf16[256,1024]{1,0:T(8,128)(2,1)S(1)}, bf16[256,1024]{1,0:T(8,128)(...) custom-call(bf16[128,2048]{1,0:T(8,128)(2,1)S(1)} %get-tuple-element.27.x_ref,, ...), custom_call_target="tpu_custom_call" | custom-call | flops 939524096 | bytes 7340032 | tf_op jit(solution)/shard_map/products/pallas_call | solution.py:69
  10.8 3.5 %collective-permute-start.6 = (bf16[256,1024]{1,0:T(8,128)(2,1)S(1)}, bf16[256,1024]{1,0:T(8,128)(2,1)S(1)}, u32[]{:S(2)}, u32[]{:S(2)}) collective-permute-start(bf16[256,1024]{1,0:T(8,128)(2,1)S(1)} %get-tuple-element.32), channel_id=1, source_target_pairs={{0,2},{1,15},{2,4},{3,1},{4,6},{5,3},{6,8},{7,5},{8,10},{9,7},{10,... | collective-permute-start | bytes 1572872 | tf_op jit(solution)/shard_map/ppermute | solution.py:329
  14.3 3.5 %collective-permute-start.2 = (bf16[256,1024]{1,0:T(8,128)(2,1)S(1)}, bf16[256,1024]{1,0:T(8,128)(2,1)S(1)}, u32[]{:S(2)}, u32[]{:S(2)}) collective-permute-start(bf16[256,1024]{1,0:T(8,128)(2,1)S(1)} %products.2.outs_0_), channel_id=1, source_target_pairs={{0,2},{1,15},{2,4},{3,1},{4,6},{5,3},{6,8},{7,5},{8,10},{9,7},{10,... | collective-permute-start | bytes 1572872 | tf_op jit(solution)/shard_map/ppermute | solution.py:329
  17.8 5.5 %collective-permute-done.6 = bf16[256,1024]{1,0:T(8,128)(2,1)S(1)} collective-permute-done((bf16[256,1024]{1,0:T(8,128)(2,1)S(1)}, bf16[256,1024]{1,0:T(8,128)(2,1)S(1)}, u32[]{:S(2)}, u32[]{:S(2)}) %collective-permute-start.6) | collective-permute-done | bytes 524320 | tf_op jit(solution)/shard_map/ppermute | solution.py:329
  23.5 2.0 %collective-permute-start.7 = (bf16[256,1024]{1,0:T(8,128)(2,1)S(1)}, bf16[256,1024]{1,0:T(8,128)(2,1)S(1)}, u32[]{:S(2)}, u32[]{:S(2)}) collective-permute-start(bf16[256,1024]{1,0:T(8,128)(2,1)S(1)} %add_convert_fusion.2), channel_id=1, source_target_pairs={{0,2},{1,15},{2,4},{3,1},{4,6},{5,3},{6,8},{7,5},{8,10},{9,7},{10,... | collective-permute-start | bytes 1572872 | tf_op jit(solution)/shard_map/ppermute | solution.py:329
  25.6 3.4 %collective-permute-done.2 = bf16[256,1024]{1,0:T(8,128)(2,1)S(1)} collective-permute-done((bf16[256,1024]{1,0:T(8,128)(2,1)S(1)}, bf16[256,1024]{1,0:T(8,128)(2,1)S(1)}, u32[]{:S(2)}, u32[]{:S(2)}) %collective-permute-start.2) | collective-permute-done | bytes 524320 | tf_op jit(solution)/shard_map/ppermute | solution.py:329
  29.2 2.0 %collective-permute-start.3 = (bf16[256,1024]{1,0:T(8,128)(2,1)S(1)}, bf16[256,1024]{1,0:T(8,128)(2,1)S(1)}, u32[]{:S(2)}, u32[]{:S(2)}) collective-permute-start(bf16[256,1024]{1,0:T(8,128)(2,1)S(1)} %add_convert_fusion.5), channel_id=1, source_target_pairs={{0,2},{1,15},{2,4},{3,1},{4,6},{5,3},{6,8},{7,5},{8,10},{9,7},{10,... | collective-permute-start | bytes 1572872 | tf_op jit(solution)/shard_map/ppermute | solution.py:329
  31.2 4.6 %collective-permute-done.7 = bf16[256,1024]{1,0:T(8,128)(2,1)S(1)} collective-permute-done((bf16[256,1024]{1,0:T(8,128)(2,1)S(1)}, bf16[256,1024]{1,0:T(8,128)(2,1)S(1)}, u32[]{:S(2)}, u32[]{:S(2)}) %collective-permute-start.7) | collective-permute-done | bytes 524320 | tf_op jit(solution)/shard_map/ppermute | solution.py:329
  37.9 3.5 %collective-permute-done.3 = bf16[256,1024]{1,0:T(8,128)(2,1)S(1)} collective-permute-done((bf16[256,1024]{1,0:T(8,128)(2,1)S(1)}, bf16[256,1024]{1,0:T(8,128)(2,1)S(1)}, u32[]{:S(2)}, u32[]{:S(2)}) %collective-permute-start.3) | collective-permute-done | bytes 524320 | tf_op jit(solution)/shard_map/ppermute | solution.py:329
  43.6 4.7 %collective-permute-done.8 = bf16[256,1024]{1,0:T(8,128)(2,1)S(1)} collective-permute-done((bf16[256,1024]{1,0:T(8,128)(2,1)S(1)}, bf16[256,1024]{1,0:T(8,128)(2,1)S(1)}, u32[]{:S(2)}, u32[]{:S(2)}) %collective-permute-start.8) | collective-permute-done | bytes 524320 | tf_op jit(solution)/shard_map/ppermute | solution.py:329
  50.4 3.5 %collective-permute-done.4 = bf16[256,1024]{1,0:T(8,128)(2,1)S(1)} collective-permute-done((bf16[256,1024]{1,0:T(8,128)(2,1)S(1)}, bf16[256,1024]{1,0:T(8,128)(2,1)S(1)}, u32[]{:S(2)}, u32[]{:S(2)}) %collective-permute-start.4) | collective-permute-done | bytes 524320 | tf_op jit(solution)/shard_map/ppermute | solution.py:329
  54.9 2.0 %collective-permute-start.5 = (bf16[256,1024]{1,0:T(8,128)(2,1)}, bf16[256,1024]{1,0:T(8,128)(2,1)S(1)}, u32[]{:S(2)}, u32[]{:S(2)}) collective-permute-start(bf16[256,1024]{1,0:T(8,128)(2,1)} %add_convert_fusion.3), channel_id=1, source_target_pairs={{0,2},{1,15},{2,4},{3,1},{4,6},{5,3},{6,8},{7,5},{8,10},{9,7},{10,... | collective-permute-start | bytes 1572872 | tf_op jit(solution)/shard_map/ppermute | solution.py:329
  58.3 9.2 %collective-permute-done.5.a_ref = bf16[256,1024]{1,0:T(8,128)(2,1)S(1)} collective-permute-done((bf16[256,1024]{1,0:T(8,128)(2,1)}, bf16[256,1024]{1,0:T(8,128)(2,1)S(1)}, u32[]{:S(2)}, u32[]{:S(2)}) %collective-permute-start.5) | collective-permute-done | bytes 524320 | tf_op jit(solution)/shard_map/ppermute | solution.py:329
  67.7 17.6 %all_to_all.20.got_ref = bf16[4,512,128]{2,1,0:T(8,128)(2,1)S(1)} all-to-all(bf16[4,512,128]{2,1,0:T(8,128)(2,1)S(1)} %finish.1), channel_id=1, replica_groups={{0,16,32,48},{64,80,96,112},{128,144,160,176},{192,208,224,240},{256,27..., dimensions={0} | all-to-all | bytes 1048576 | tf_op jit(solution)/shard_map/all_to_all | solution.py:353
  85.4 19.8 %all_to_all.21.got_ref = bf16[12,48,128]{2,1,0:T(8,128)(2,1)S(1)} all-to-all(bf16[12,48,128]{2,1,0:T(8,128)(2,1)S(1)} %shard_map.94), channel_id=1, replica_groups={{0,64,128,192,256,320,384,448,512,576,640,704},{16,80,144,208,272,336,4..., dimensions={0} | all-to-all | bytes 294912 | tf_op jit(solution)/shard_map/all_to_all | solution.py:356
  105.2 14.6 %all_to_all.22.got_ref = bf16[12,48,128]{2,1,0:T(8,128)(2,1)S(1)} all-to-all(bf16[12,48,128]{2,1,0:T(8,128)(2,1)S(1)} %shard_map.95), channel_id=1, replica_groups={{0,64,128,192,256,320,384,448,512,576,640,704},{16,80,144,208,272,336,4..., dimensions={0} | all-to-all | bytes 294912 | tf_op jit(solution)/shard_map/all_to_all | solution.py:359
  120.6 10.4 %all-to-all-start.3 = ((f32[64,8,128]{2,1,0:T(8,128)}), f32[64,8,128]{2,1,0:T(8,128)S(1)}, u32[]{:S(2)}, u32[]{:S(2)}) async-start(f32[64,8,128]{2,1,0:T(8,128)} %get-tuple-element.47), calls=%async_computation.3 | async-start | bytes 524288 | tf_op jit(solution)/shard_map/all_to_all | solution.py:368
  131.0 2.7 %collective-permute-start.10 = (bf16[528,128]{1,0:T(8,128)(2,1)S(1)}, bf16[528,128]{1,0:T(8,128)(2,1)S(1)}, u32[]{:S(2)}, u32[]{:S(2)}) collective-permute-start(bf16[528,128]{1,0:T(8,128)(2,1)S(1)} %get-tuple-element.46.refs_0_), channel_id=1, source_target_pairs={{0,16},{16,0},{32,48},{48,32},{64,80},{80,64},{96,112},{112,96},{1... | collective-permute-start | bytes 405512 | tf_op jit(solution)/shard_map/ppermute | solution.py:374
  133.7 3.0 %collective-permute-start.12 = (bf16[528,128]{1,0:T(8,128)(2,1)S(1)}, bf16[528,128]{1,0:T(8,128)(2,1)S(1)}, u32[]{:S(2)}, u32[]{:S(2)}) collective-permute-start(bf16[528,128]{1,0:T(8,128)(2,1)S(1)} %get-tuple-element.46.refs_0_), channel_id=1, source_target_pairs={{0,48},{16,32},{32,16},{48,0},{64,112},{80,96},{96,80},{112,64},{1... | collective-permute-start | bytes 405512 | tf_op jit(solution)/shard_map/ppermute | solution.py:374
  136.7 3.9 %collective-permute-done.10.refs_1_ = bf16[528,128]{1,0:T(8,128)(2,1)S(1)} collective-permute-done((bf16[528,128]{1,0:T(8,128)(2,1)S(1)}, bf16[528,128]{1,0:T(8,128)(2,1)S(1)}, u32[]{:S(2)}, u32[]{:S(2)}) %collective-permute-start.10) | collective-permute-done | bytes 135200 | tf_op jit(solution)/shard_map/ppermute | solution.py:374
  140.6 2.2 %collective-permute-start.11 = (bf16[528,128]{1,0:T(8,128)(2,1)S(1)}, bf16[528,128]{1,0:T(8,128)(2,1)S(1)}, u32[]{:S(2)}, u32[]{:S(2)}) collective-permute-start(bf16[528,128]{1,0:T(8,128)(2,1)S(1)} %collective-permute-done.10.refs_1_), channel_id=1, source_target_pairs={{0,48},{16,32},{32,16},{48,0},{64,112},{80,96},{96,80},{112,64},{1... | collective-permute-start | bytes 405512 | tf_op jit(solution)/shard_map/ppermute | solution.py:374
  142.8 5.9 %collective-permute-done.11.refs_2_ = bf16[528,128]{1,0:T(8,128)(2,1)S(1)} collective-permute-done((bf16[528,128]{1,0:T(8,128)(2,1)S(1)}, bf16[528,128]{1,0:T(8,128)(2,1)S(1)}, u32[]{:S(2)}, u32[]{:S(2)}) %collective-permute-start.11) | collective-permute-done | bytes 135200 | tf_op jit(solution)/shard_map/ppermute | solution.py:374
  148.7 2.4 %shard_map.97 = (bf16[256,1024]{1,0:T(8,128)(2,1)}, f32[4,16]{1,0:T(4,128)}, f32[8,128]{1,0:T(8,128)}) custom-call(s32[4]{0:T(128)S(1)} %get-tuple-element.40.index_ref, f32[4,16]{1,0:T(4,128)S(1)} %bitcast.5, bf16[2048,64]{1,0:T(8,128)(2,1)S(1)} %get-tuple-element.41.pick_ref, bf16[2048,128]{1,0:T(8,128)(2,1)S(1)} %get-tuple-element.42.lane_ref, ...), custom_call_target="tpu_custom_call" | custom-call | flops 992324 | bytes 3969296 | tf_op jit(solution)/shard_map/pallas_call | solution.py:113
  (37 shorter events, 15.7 us)
Async XLA Ops:
  0.6 1.2 copy-start
  1.9 0.7 copy-start.3
  2.6 2.1 %copy-start.2 = (bf16[128,1024]{1,0:T(8,128)(2,1)S(1)}, bf16[128,1024]{1,0:T(8,128)(2,1)}, u32[]{:S(2)}) copy-start(bf16[128,1024]{1,0:T(8,128)(2,1)} %c_ref.3) | copy-start | bytes 786436
  2.8 5.5 %collective-permute-start = (bf16[128,2048]{1,0:T(8,128)(2,1)S(1)}, bf16[128,2048]{1,0:T(8,128)(2,1)S(1)}, u32[]{:S(2)}, u32[]{:S(2)}) collective-permute-start(bf16[128,2048]{1,0:T(8,128)(2,1)S(1)} %get-tuple-element.28), channel_id=1, source_target_pairs={{0,1},{1,0},{2,3},{3,2},{4,5},{5,4},{6,7},{7,6},{8,9},{9,8},{10,11... | collective-permute-start | bytes 1572872 | tf_op jit(solution)/shard_map/ppermute | solution.py:316
  4.7 3.6 %collective-permute-start.1 = (bf16[128,1024]{1,0:T(8,128)(2,1)S(1)}, bf16[128,1024]{1,0:T(8,128)(2,1)S(1)}, u32[]{:S(2)}, u32[]{:S(2)}) collective-permute-start(bf16[128,1024]{1,0:T(8,128)(2,1)S(1)} %copy-done.2), channel_id=1, source_target_pairs={{0,1},{1,0},{2,3},{3,2},{4,5},{5,4},{6,7},{7,6},{8,9},{9,8},{10,11... | collective-permute-start | bytes 786440 | tf_op jit(solution)/shard_map/ppermute | solution.py:314
  10.8 12.5 %collective-permute-start.6 = (bf16[256,1024]{1,0:T(8,128)(2,1)S(1)}, bf16[256,1024]{1,0:T(8,128)(2,1)S(1)}, u32[]{:S(2)}, u32[]{:S(2)}) collective-permute-start(bf16[256,1024]{1,0:T(8,128)(2,1)S(1)} %get-tuple-element.32), channel_id=1, source_target_pairs={{0,2},{1,15},{2,4},{3,1},{4,6},{5,3},{6,8},{7,5},{8,10},{9,7},{10,... | collective-permute-start | bytes 1572872 | tf_op jit(solution)/shard_map/ppermute | solution.py:329
  14.3 14.6 %collective-permute-start.2 = (bf16[256,1024]{1,0:T(8,128)(2,1)S(1)}, bf16[256,1024]{1,0:T(8,128)(2,1)S(1)}, u32[]{:S(2)}, u32[]{:S(2)}) collective-permute-start(bf16[256,1024]{1,0:T(8,128)(2,1)S(1)} %products.2.outs_0_), channel_id=1, source_target_pairs={{0,2},{1,15},{2,4},{3,1},{4,6},{5,3},{6,8},{7,5},{8,10},{9,7},{10,... | collective-permute-start | bytes 1572872 | tf_op jit(solution)/shard_map/ppermute | solution.py:329
  23.5 12.3 %collective-permute-start.7 = (bf16[256,1024]{1,0:T(8,128)(2,1)S(1)}, bf16[256,1024]{1,0:T(8,128)(2,1)S(1)}, u32[]{:S(2)}, u32[]{:S(2)}) collective-permute-start(bf16[256,1024]{1,0:T(8,128)(2,1)S(1)} %add_convert_fusion.2), channel_id=1, source_target_pairs={{0,2},{1,15},{2,4},{3,1},{4,6},{5,3},{6,8},{7,5},{8,10},{9,7},{10,... | collective-permute-start | bytes 1572872 | tf_op jit(solution)/shard_map/ppermute | solution.py:329
  29.2 12.3 %collective-permute-start.3 = (bf16[256,1024]{1,0:T(8,128)(2,1)S(1)}, bf16[256,1024]{1,0:T(8,128)(2,1)S(1)}, u32[]{:S(2)}, u32[]{:S(2)}) collective-permute-start(bf16[256,1024]{1,0:T(8,128)(2,1)S(1)} %add_convert_fusion.5), channel_id=1, source_target_pairs={{0,2},{1,15},{2,4},{3,1},{4,6},{5,3},{6,8},{7,5},{8,10},{9,7},{10,... | collective-permute-start | bytes 1572872 | tf_op jit(solution)/shard_map/ppermute | solution.py:329
  36.0 12.3 %collective-permute-start.8 = (bf16[256,1024]{1,0:T(8,128)(2,1)S(1)}, bf16[256,1024]{1,0:T(8,128)(2,1)S(1)}, u32[]{:S(2)}, u32[]{:S(2)}) collective-permute-start(bf16[256,1024]{1,0:T(8,128)(2,1)S(1)} %add_convert_fusion.1), channel_id=1, source_target_pairs={{0,2},{1,15},{2,4},{3,1},{4,6},{5,3},{6,8},{7,5},{8,10},{9,7},{10,... | collective-permute-start | bytes 1572872 | tf_op jit(solution)/shard_map/ppermute | solution.py:329
  41.6 12.3 %collective-permute-start.4 = (bf16[256,1024]{1,0:T(8,128)(2,1)S(1)}, bf16[256,1024]{1,0:T(8,128)(2,1)S(1)}, u32[]{:S(2)}, u32[]{:S(2)}) collective-permute-start(bf16[256,1024]{1,0:T(8,128)(2,1)S(1)} %add_convert_fusion.4), channel_id=1, source_target_pairs={{0,2},{1,15},{2,4},{3,1},{4,6},{5,3},{6,8},{7,5},{8,10},{9,7},{10,... | collective-permute-start | bytes 1572872 | tf_op jit(solution)/shard_map/ppermute | solution.py:329
  48.5 9.8 %collective-permute-start.9 = (bf16[256,1024]{1,0:T(8,128)(2,1)S(1)}, bf16[256,1024]{1,0:T(8,128)(2,1)S(1)}, u32[]{:S(2)}, u32[]{:S(2)}) collective-permute-start(bf16[256,1024]{1,0:T(8,128)(2,1)S(1)} %add_convert_fusion), channel_id=1, source_target_pairs={{0,1},{1,0},{2,3},{3,2},{4,5},{5,4},{6,7},{7,6},{8,9},{9,8},{10,11... | collective-permute-start | bytes 1572872 | tf_op jit(solution)/shard_map/ppermute | solution.py:338
  53.9 3.0 %copy-start.6 = (s32[128,1]{0,1:T(1,128)S(1)}, s32[128,1]{0,1:T(1,128)}, u32[]{:S(2)}) copy-start(s32[128,1]{0,1:T(1,128)} %param.13) | copy-start | bytes 1540
  54.9 2.2 %copy-start.5 = (f32[1,1,4,16]{3,2,1,0:T(4,128)S(1)}, f32[1,1,4,16]{3,2,1,0:T(4,128)}, u32[]{:S(2)}) copy-start(f32[1,1,4,16]{3,2,1,0:T(4,128)} %param.11) | copy-start | bytes 772
  54.9 12.6 %collective-permute-start.5 = (bf16[256,1024]{1,0:T(8,128)(2,1)}, bf16[256,1024]{1,0:T(8,128)(2,1)S(1)}, u32[]{:S(2)}, u32[]{:S(2)}) collective-permute-start(bf16[256,1024]{1,0:T(8,128)(2,1)} %add_convert_fusion.3), channel_id=1, source_target_pairs={{0,2},{1,15},{2,4},{3,1},{4,6},{5,3},{6,8},{7,5},{8,10},{9,7},{10,... | collective-permute-start | bytes 1572872 | tf_op jit(solution)/shard_map/ppermute | solution.py:329
  105.2 43.5 %copy-start.1 = (bf16[256,1024]{1,0:T(8,128)(2,1)S(1)}, bf16[256,1024]{1,0:T(8,128)(2,1)}, u32[]{:S(2)}) copy-start(bf16[256,1024]{1,0:T(8,128)(2,1)} %refs_5_.1) | copy-start | bytes 1572868
  120.6 28.1 %copy-start.4 = (f32[8,128]{1,0:T(8,128)S(1)}, f32[8,128]{1,0:T(8,128)}, u32[]{:S(2)}) copy-start(f32[8,128]{1,0:T(8,128)} %refs_6_.1) | copy-start | bytes 12292
  120.6 28.1 %all-to-all-start.3 = ((f32[64,8,128]{2,1,0:T(8,128)}), f32[64,8,128]{2,1,0:T(8,128)S(1)}, u32[]{:S(2)}, u32[]{:S(2)}) async-start(f32[64,8,128]{2,1,0:T(8,128)} %get-tuple-element.47), calls=%async_computation.3 | async-start | bytes 524288 | tf_op jit(solution)/shard_map/all_to_all | solution.py:368
  131.0 9.6 %collective-permute-start.10 = (bf16[528,128]{1,0:T(8,128)(2,1)S(1)}, bf16[528,128]{1,0:T(8,128)(2,1)S(1)}, u32[]{:S(2)}, u32[]{:S(2)}) collective-permute-start(bf16[528,128]{1,0:T(8,128)(2,1)S(1)} %get-tuple-element.46.refs_0_), channel_id=1, source_target_pairs={{0,16},{16,0},{32,48},{48,32},{64,80},{80,64},{96,112},{112,96},{1... | collective-permute-start | bytes 405512 | tf_op jit(solution)/shard_map/ppermute | solution.py:374
  133.7 9.1 %collective-permute-start.12 = (bf16[528,128]{1,0:T(8,128)(2,1)S(1)}, bf16[528,128]{1,0:T(8,128)(2,1)S(1)}, u32[]{:S(2)}, u32[]{:S(2)}) collective-permute-start(bf16[528,128]{1,0:T(8,128)(2,1)S(1)} %get-tuple-element.46.refs_0_), channel_id=1, source_target_pairs={{0,48},{16,32},{32,16},{48,0},{64,112},{80,96},{96,80},{112,64},{1... | collective-permute-start | bytes 405512 | tf_op jit(solution)/shard_map/ppermute | solution.py:374
  140.6 8.1 %collective-permute-start.11 = (bf16[528,128]{1,0:T(8,128)(2,1)S(1)}, bf16[528,128]{1,0:T(8,128)(2,1)S(1)}, u32[]{:S(2)}, u32[]{:S(2)}) collective-permute-start(bf16[528,128]{1,0:T(8,128)(2,1)S(1)} %collective-permute-done.10.refs_1_), channel_id=1, source_target_pairs={{0,48},{16,32},{32,16},{48,0},{64,112},{80,96},{96,80},{112,64},{1... | collective-permute-start | bytes 405512 | tf_op jit(solution)/shard_map/ppermute | solution.py:374

commit v6 on v5

--- a/solution.py
+++ b/solution.py
@@ -140,61 +140,54 @@
         out_ref[j] = total.astype(out_ref.dtype)
 
 
-def pack_kernel(rows, got_ref, out_ref, stats_ref):
+def pack_kernel(rows, got_ref, out_ref):
     count, _, head = got_ref.shape
     pad = -count % 16
-    full = out_ref.shape[0] - count - pad
+    full = out_ref.shape[1] - count - pad
     blocks = [got_ref[j].astype(jnp.float32) for j in range(count)]
     grad = jnp.concatenate([block[:rows] for block in blocks], axis=0)[:full]
-    out_ref[:full, :] = grad.astype(out_ref.dtype)
-    tail = [block[rows : rows + 1] for block in blocks] + [jnp.zeros((pad, head), jnp.float32)]
-    out_ref[full:, :] = jnp.concatenate(tail, axis=0).astype(out_ref.dtype)
-    squares = grad * grad
+    grad = grad.astype(out_ref.dtype)
+    sums = sum(block[rows + 1 : rows + 2] for block in blocks)
+    high = sums.astype(out_ref.dtype).astype(jnp.float32)
+    tail = [block[rows : rows + 1] for block in blocks] + [high, sums - high]
+    tail = jnp.concatenate(tail + [jnp.zeros((pad - 2, head), jnp.float32)], axis=0)
+    for x in range(out_ref.shape[0]):
+        out_ref[x, :full, :] = grad
+        out_ref[x, full:, :] = tail.astype(out_ref.dtype)
+
+
+def stats_kernel(count, full, got_ref, out_ref):
     half = full // 2
-    stats = [jnp.sum(squares[t * half : (t + 1) * half], axis=0, keepdims=True) for t in range(2)]
-    stats.append(sum(block[rows + 1 : rows + 2] for block in blocks))
-    stats.append(jnp.zeros((stats_ref.shape[1] - 3, head), jnp.float32))
-    stats = jnp.concatenate(stats, axis=0)
-    for j in range(stats_ref.shape[0]):
-        stats_ref[j] = stats
-
-
-def update_kernel(index_ref, state_ref, pick_ref, lane_ref, *refs):
-    *got, stats_ref, weight_ref, col_state_ref, out_ref, own_ref, col_ref = refs
-    my_x = lax.axis_index("grp") % N_X
-    tensors, head = col_ref.shape
-    slab = weight_ref.shape[0]
-    full = pick_ref.shape[0] // N_X
-    plane = stats_ref.shape[0] // N_X
-    d_model = slab * plane
-
-    sums = jnp.sum(stats_ref[:, 2, :], axis=0, keepdims=True)
-    factors = []
-    for t in range(tensors):
-        x = t // 2
-        col = jnp.sum(stats_ref[x * plane : (x + 1) * plane, t % 2, :], axis=0, keepdims=True)
-        col = col / d_model + epsilon
-        col_new = decay_rate * col_state_ref[t : t + 1, :] + (1.0 - decay_rate) * col
-        col_ref[t : t + 1, :] = col_new
-        prev = (sums[:, t : t + 1] + sums[:, tensors + t : tensors + t + 1]) / d_model
-        average = decay_rate * prev + (1.0 - decay_rate) * jnp.mean(col, axis=1, keepdims=True)
-        factors.append(step_size * lax.rsqrt(col_new / average))
-
-    states = jnp.concatenate([ref[full:, :] for ref in got], axis=0)
-    for t in range(tensors):
-        rows = slice((t % 2) * slab, (t % 2 + 1) * slab)
-        grad = got[0][rows, :]
-        for k in range(1, N_X):
-            grad = jnp.where((my_x ^ k) == t // 2, got[k][rows, :], grad)
-        grad = grad.astype(jnp.float32)
+    rows = []
+    for x in range(got_ref.shape[0]):
+        for t in range(2):
+            grad = got_ref[x, t * half : (t + 1) * half, :].astype(jnp.float32)
+            rows.append(jnp.sum(grad * grad, axis=0, keepdims=True))
+    tails = [got_ref[x, full:, :].astype(jnp.float32) for x in range(got_ref.shape[0])]
+    rows.append(sum(t[count : count + 1] + t[count + 1 : count + 2] for t in tails))
+    fill = out_ref.shape[0] - len(rows)
+    rows.append(jnp.zeros((fill, out_ref.shape[1]), jnp.float32))
+    out_ref[...] = jnp.concatenate(rows, axis=0)
+
+
+def both_kernel(a_ref, b_ref, out_ref):
+    total = a_ref[...] + b_ref[...]
+    for j in range(out_ref.shape[0]):
+        out_ref[j] = total
+
+
+def rows_kernel(index_ref, state_ref, pick_ref, lane_ref, got_ref, out_ref, own_ref):
+    n_x, _, head = got_ref.shape
+    full = pick_ref.shape[0] // n_x
+    slab = full // 2
+    states = jnp.concatenate([got_ref[x, full:, :] for x in range(n_x)], axis=0)
+    for t in range(2 * n_x):
+        grad = got_ref[t // 2, (t % 2) * slab : (t % 2 + 1) * slab, :].astype(jnp.float32)
         where = slice(t * slab, (t + 1) * slab)
         state = jnp.dot(pick_ref[where, :], states, preferred_element_type=jnp.float32)
         prev = jnp.sum(state * lane_ref[where, :].astype(jnp.float32), axis=1, keepdims=True)
         mean = jnp.sum(grad * grad, axis=1, keepdims=True) / head + epsilon
-        scale = lax.rsqrt(decay_rate * prev + (1.0 - decay_rate) * mean)
-        cols = slice(t * head, (t + 1) * head)
-        change = grad * scale * factors[t]
-        out_ref[:, cols] = (weight_ref[:, cols].astype(jnp.float32) - change).astype(out_ref.dtype)
+        out_ref[where, :] = grad * lax.rsqrt(decay_rate * prev + (1.0 - decay_rate) * mean)
 
     capacity, unit_rows = own_ref.shape
     per_piece = full // unit_rows
@@ -203,14 +196,32 @@
     for c in range(capacity):
         unit = jnp.maximum(index_ref[c], 0)
         rows = pl.ds(pl.multiple_of((unit % per_piece) * unit_rows, unit_rows), unit_rows)
-        grad = got[0][rows, :]
-        for k in range(1, N_X):
-            grad = jnp.where((my_x ^ k) == unit // per_piece, got[k][rows, :], grad)
+        grad = got_ref[0, rows, :]
+        for x in range(1, n_x):
+            grad = jnp.where(unit // per_piece == x, got_ref[x, rows, :], grad)
         grad = grad.astype(jnp.float32)
         mean = jnp.sum(grad * grad, axis=1, keepdims=True) / head + epsilon
         mean = jnp.sum(jnp.where(eye, mean, 0.0), axis=0, keepdims=True)
         new = decay_rate * state_ref[c : c + 1, :] + (1.0 - decay_rate) * mean
         own_ref[c : c + 1, :] = jnp.where(index_ref[c] >= 0, new, 0.0)
+
+
+def update_kernel(stats_ref, grad_ref, weight_ref, state_ref, out_ref, col_ref):
+    tensors, head = state_ref.shape
+    slab = weight_ref.shape[0]
+    d_model = CORES * slab * stats_ref.shape[0]
+    total = sum(stats_ref[j] for j in range(stats_ref.shape[0])) / d_model
+    for t in range(tensors):
+        col = total[t : t + 1] + epsilon
+        col_new = decay_rate * state_ref[t : t + 1, :] + (1.0 - decay_rate) * col
+        col_ref[t : t + 1, :] = col_new
+        sums = total[tensors : tensors + 1]
+        prev = sums[:, t : t + 1] + sums[:, tensors + t : tensors + t + 1]
+        average = decay_rate * prev + (1.0 - decay_rate) * jnp.mean(col, axis=1, keepdims=True)
+        factor = step_size * lax.rsqrt(col_new / average)
+        cols = slice(t * head, (t + 1) * head)
+        change = grad_ref[t * slab : (t + 1) * slab, :] * factor
+        out_ref[:, cols] = (weight_ref[:, cols].astype(jnp.float32) - change).astype(out_ref.dtype)
 
 
 def tables_kernel(row, owner_ref, state_ref, pick_ref, lane_ref, extra_ref, index_ref):
@@ -232,7 +243,7 @@
     before = jnp.dot(earlier, hot.astype(bf16), preferred_element_type=f32)
     slot = jnp.sum(before * hot, axis=1, keepdims=True).astype(jnp.int32)
 
-    seat = ((owner ^ me) & (N_X - 1)) * (seats // N_X) + owner // N_X
+    seat = (owner % N_X) * (seats // N_X) + owner // N_X
     spread = ((at((count, units), 0) // unit_rows) == at((count, units), 1)).astype(bf16)
     hot = (seat == at((units, seats), 1)).astype(bf16)
     pick_ref[...] = jnp.dot(spread, hot, preferred_element_type=f32).astype(bf16)
@@ -306,6 +317,7 @@
     blocks = slab // unit_rows
     units = tensors * blocks
 
+    same_core = [[y * CORES + c for y in range(n_y)] for c in range(CORES)]
     x_groups = [[z * N_X + x for x in range(N_X)] for z in range(n_z)]
     z_groups = [[z * N_X + x for z in range(n_z)] for x in range(N_X)]
 
@@ -357,43 +369,28 @@
 
     sent = small_kernel(sum_z_kernel, block, got, extra)
     got = lax.all_to_all(sent, "grp", 0, 0, axis_index_groups=z_groups, tiled=True)
+    sent = jax.ShapeDtypeStruct((N_X, full + state_rows, head), bf16)
+    sent = small_kernel(functools.partial(pack_kernel, share), sent, got)
+    got = lax.all_to_all(sent, "grp", 0, 0, axis_index_groups=x_groups, tiled=True)
+
+    stats = jax.ShapeDtypeStruct((2 * tensors, head), f32)
+    stats = small_kernel(functools.partial(stats_kernel, n_z, full), stats, got)
+    partner = lax.ppermute(stats, "intra", swap)
     shapes = (
-        jax.ShapeDtypeStruct((full + state_rows, head), bf16),
-        jax.ShapeDtypeStruct((N_X * intra, 8, head), f32),
-    )
-    body = functools.partial(pack_kernel, share)
-    sent, stats = small_kernel(body, shapes, got)
-    plane = N_X * intra
-    planes = [list(range(z * plane, (z + 1) * plane)) for z in range(n_z)]
-    stats = lax.all_to_all(
-        stats, ("grp", "intra"), 0, 0, axis_index_groups=planes, tiled=True
-    )
-
-    def trade(a, k):
-        pairs = [(g, g ^ k) for g in range(groups)]
-        return lax.ppermute(a, "grp", pairs)
-
-    near, wrap = trade(sent, 1), trade(sent, N_X - 1)
-    fetched = [sent, near, trade(near, N_X - 1), wrap]
-
+        jax.ShapeDtypeStruct((units * unit_rows, head), f32),
+        jax.ShapeDtypeStruct((capacity, unit_rows), f32),
+    )
+    scaled, row_moments = small_kernel(
+        rows_kernel, shapes, my_index, row_state[0, 0], pick, lane, got, scalars=1
+    )
+    sent = jax.ShapeDtypeStruct((n_y,) + stats.shape, f32)
+    sent = small_kernel(both_kernel, sent, stats, partner)
+    stats = lax.all_to_all(sent, "intra", 0, 0, axis_index_groups=same_core, tiled=True)
     shapes = (
         jax.ShapeDtypeStruct(weights.shape, weights.dtype),
-        jax.ShapeDtypeStruct((capacity, unit_rows), f32),
         jax.ShapeDtypeStruct(col_state.shape, f32),
     )
-    new_weights, row_moments, col_new = small_kernel(
-        update_kernel,
-        shapes,
-        my_index,
-        row_state[0, 0],
-        pick,
-        lane,
-        *fetched,
-        stats,
-        weights,
-        col_state,
-        scalars=1,
-    )
+    new_weights, col_new = small_kernel(update_kernel, shapes, stats, scaled, weights, col_state)
     return (new_weights, row_moments[None, None], col_new)
 
 

time: 152 us -> 153 us (level)
  the two profiles are of different devices: /device:TPU:6 before, /device:TPU:1 now
where the time goes in v6:
time: 153 us; the launch traced here: 152 us
  starting transfers between devices  57 us (37%)
  blocking collectives  50.6 us (33%)
  waiting for transfers between devices  31.5 us (21%)
  Pallas kernels  7.92 us (5%)
  local copies, waits for them, and re-layouts  2.07 us (1%)
  other arithmetic  1.94 us (1%)
    all_to_all x2, blocking collectives, on_device(): lax.all_to_all(sent, 'grp', 0, 0, axis_index_groups=z_groups, tiled=True)  31.8 us
    ppermute x7, waiting for transfers between devices, hop(): return lax.ppermute(a, 'intra', ring)  23.7 us
    ppermute x7, starting transfers between devices, hop(): return lax.ppermute(a, 'intra', ring)  17.4 us
    ppermute x1, starting transfers between devices, on_device(): got = lax.ppermute(theirs, 'intra', swap)  12.4 us
    ppermute x1, starting transfers between devices, on_device(): partner = lax.ppermute(stats, 'intra', swap)  12.1 us
    all_to_all x1, blocking collectives, on_device(): lax.all_to_all(sent, 'grp', 0, 0, axis_index_groups=x_groups, tiled=True)  9.39 us
    all_to_all x1, blocking collectives, on_device(): lax.all_to_all(own, 'grp', 0, 0, axis_index_groups=x_groups, tiled=True)  9.33 us
    ppermute x1, starting transfers between devices, on_device(): other = lax.ppermute(give, 'intra', swap)  6.6 us
  transfers between devices with their start and end apart: 12, of which 9 were waited for; matrix products, arithmetic and copies ran while one was open for 1% of the time, Pallas kernels for 2%

profile of v6, /device:TPU:1, one launch (start us, length us, event | category | flops | bytes accessed | tf_op | source)
XLA Modules:
  0.0 151.8 jit_solution(5407790323972004587)
XLA Ops:
  2.8 12.4 %collective-permute-start = (bf16[128,2048]{1,0:T(8,128)(2,1)S(1)}, bf16[128,2048]{1,0:T(8,128)(2,1)S(1)}, u32[]{:S(2)}, u32[]{:S(2)}) collective-permute-start(bf16[128,2048]{1,0:T(8,128)(2,1)S(1)} %get-tuple-element.27), channel_id=1, source_target_pairs={{0,1},{1,0},{2,3},{3,2},{4,5},{5,4},{6,7},{7,6},{8,9},{9,8},{10,11... | collective-permute-start | bytes 1572872 | tf_op jit(solution)/shard_map/ppermute | solution.py:328
  15.2 1.9 %collective-permute-start.1 = (bf16[128,1024]{1,0:T(8,128)(2,1)S(1)}, bf16[128,1024]{1,0:T(8,128)(2,1)S(1)}, u32[]{:S(2)}, u32[]{:S(2)}) collective-permute-start(bf16[128,1024]{1,0:T(8,128)(2,1)S(1)} %copy-done.2), channel_id=1, source_target_pairs={{0,1},{1,0},{2,3},{3,2},{4,5},{5,4},{6,7},{7,6},{8,9},{9,8},{10,11... | collective-permute-start | bytes 786440 | tf_op jit(solution)/shard_map/ppermute | solution.py:326
  19.1 2.1 %products.3 = (bf16[256,1024]{1,0:T(8,128)(2,1)S(1)}, bf16[256,1024]{1,0:T(8,128)(2,1)S(1)}, bf16[256,1024]{1,0:T(8,128)(2,1)S(1)}, bf16[256,1024]{1,0:T(8,128)(...) custom-call(bf16[128,2048]{1,0:T(8,128)(2,1)S(1)} %get-tuple-element.26.x_ref,, ...), custom_call_target="tpu_custom_call" | custom-call | flops 939524096 | bytes 7340032 | tf_op jit(solution)/shard_map/products/pallas_call | solution.py:69
  21.1 1.9 %collective-permute-start.6 = (bf16[256,1024]{1,0:T(8,128)(2,1)S(1)}, bf16[256,1024]{1,0:T(8,128)(2,1)S(1)}, u32[]{:S(2)}, u32[]{:S(2)}) collective-permute-start(bf16[256,1024]{1,0:T(8,128)(2,1)S(1)} %get-tuple-element.31), channel_id=1, source_target_pairs={{0,2},{1,15},{2,4},{3,1},{4,6},{5,3},{6,8},{7,5},{8,10},{9,7},{10,... | collective-permute-start | bytes 1572872 | tf_op jit(solution)/shard_map/ppermute | solution.py:341
  23.1 1.9 %collective-permute-start.2 = (bf16[256,1024]{1,0:T(8,128)(2,1)S(1)}, bf16[256,1024]{1,0:T(8,128)(2,1)S(1)}, u32[]{:S(2)}, u32[]{:S(2)}) collective-permute-start(bf16[256,1024]{1,0:T(8,128)(2,1)S(1)} %products.2.outs_0_), channel_id=1, source_target_pairs={{0,2},{1,15},{2,4},{3,1},{4,6},{5,3},{6,8},{7,5},{8,10},{9,7},{10,... | collective-permute-start | bytes 1572872 | tf_op jit(solution)/shard_map/ppermute | solution.py:341
  25.0 6.4 %collective-permute-done.6 = bf16[256,1024]{1,0:T(8,128)(2,1)S(1)} collective-permute-done((bf16[256,1024]{1,0:T(8,128)(2,1)S(1)}, bf16[256,1024]{1,0:T(8,128)(2,1)S(1)}, u32[]{:S(2)}, u32[]{:S(2)}) %collective-permute-start.6) | collective-permute-done | bytes 524320 | tf_op jit(solution)/shard_map/ppermute | solution.py:341
  31.6 2.8 %collective-permute-start.7 = (bf16[256,1024]{1,0:T(8,128)(2,1)S(1)}, bf16[256,1024]{1,0:T(8,128)(2,1)S(1)}, u32[]{:S(2)}, u32[]{:S(2)}) collective-permute-start(bf16[256,1024]{1,0:T(8,128)(2,1)S(1)} %add_convert_fusion.2), channel_id=1, source_target_pairs={{0,2},{1,15},{2,4},{3,1},{4,6},{5,3},{6,8},{7,5},{8,10},{9,7},{10,... | collective-permute-start | bytes 1572872 | tf_op jit(solution)/shard_map/ppermute | solution.py:341
  34.4 2.6 %collective-permute-done.2 = bf16[256,1024]{1,0:T(8,128)(2,1)S(1)} collective-permute-done((bf16[256,1024]{1,0:T(8,128)(2,1)S(1)}, bf16[256,1024]{1,0:T(8,128)(2,1)S(1)}, u32[]{:S(2)}, u32[]{:S(2)}) %collective-permute-start.2) | collective-permute-done | bytes 524320 | tf_op jit(solution)/shard_map/ppermute | solution.py:341
  37.2 2.8 %collective-permute-start.3 = (bf16[256,1024]{1,0:T(8,128)(2,1)S(1)}, bf16[256,1024]{1,0:T(8,128)(2,1)S(1)}, u32[]{:S(2)}, u32[]{:S(2)}) collective-permute-start(bf16[256,1024]{1,0:T(8,128)(2,1)S(1)} %add_convert_fusion.5), channel_id=1, source_target_pairs={{0,2},{1,15},{2,4},{3,1},{4,6},{5,3},{6,8},{7,5},{8,10},{9,7},{10,... | collective-permute-start | bytes 1572872 | tf_op jit(solution)/shard_map/ppermute | solution.py:341
  40.0 2.6 %collective-permute-done.7 = bf16[256,1024]{1,0:T(8,128)(2,1)S(1)} collective-permute-done((bf16[256,1024]{1,0:T(8,128)(2,1)S(1)}, bf16[256,1024]{1,0:T(8,128)(2,1)S(1)}, u32[]{:S(2)}, u32[]{:S(2)}) %collective-permute-start.7) | collective-permute-done | bytes 524320 | tf_op jit(solution)/shard_map/ppermute | solution.py:341
  42.8 2.9 %collective-permute-start.8 = (bf16[256,1024]{1,0:T(8,128)(2,1)S(1)}, bf16[256,1024]{1,0:T(8,128)(2,1)S(1)}, u32[]{:S(2)}, u32[]{:S(2)}) collective-permute-start(bf16[256,1024]{1,0:T(8,128)(2,1)S(1)} %add_convert_fusion.1), channel_id=1, source_target_pairs={{0,2},{1,15},{2,4},{3,1},{4,6},{5,3},{6,8},{7,5},{8,10},{9,7},{10,... | collective-permute-start | bytes 1572872 | tf_op jit(solution)/shard_map/ppermute | solution.py:341
  45.7 2.5 %collective-permute-done.3 = bf16[256,1024]{1,0:T(8,128)(2,1)S(1)} collective-permute-done((bf16[256,1024]{1,0:T(8,128)(2,1)S(1)}, bf16[256,1024]{1,0:T(8,128)(2,1)S(1)}, u32[]{:S(2)}, u32[]{:S(2)}) %collective-permute-start.3) | collective-permute-done | bytes 524320 | tf_op jit(solution)/shard_map/ppermute | solution.py:341
  48.4 2.9 %collective-permute-start.4 = (bf16[256,1024]{1,0:T(8,128)(2,1)S(1)}, bf16[256,1024]{1,0:T(8,128)(2,1)S(1)}, u32[]{:S(2)}, u32[]{:S(2)}) collective-permute-start(bf16[256,1024]{1,0:T(8,128)(2,1)S(1)} %add_convert_fusion.4), channel_id=1, source_target_pairs={{0,2},{1,15},{2,4},{3,1},{4,6},{5,3},{6,8},{7,5},{8,10},{9,7},{10,... | collective-permute-start | bytes 1572872 | tf_op jit(solution)/shard_map/ppermute | solution.py:341
  51.4 2.5 %collective-permute-done.8 = bf16[256,1024]{1,0:T(8,128)(2,1)S(1)} collective-permute-done((bf16[256,1024]{1,0:T(8,128)(2,1)S(1)}, bf16[256,1024]{1,0:T(8,128)(2,1)S(1)}, u32[]{:S(2)}, u32[]{:S(2)}) %collective-permute-start.8) | collective-permute-done | bytes 524320 | tf_op jit(solution)/shard_map/ppermute | solution.py:341
  54.0 6.6 %collective-permute-start.9 = (bf16[256,1024]{1,0:T(8,128)(2,1)S(1)}, bf16[256,1024]{1,0:T(8,128)(2,1)S(1)}, u32[]{:S(2)}, u32[]{:S(2)}) collective-permute-start(bf16[256,1024]{1,0:T(8,128)(2,1)S(1)} %add_convert_fusion), channel_id=1, source_target_pairs={{0,1},{1,0},{2,3},{3,2},{4,5},{5,4},{6,7},{7,6},{8,9},{9,8},{10,11... | collective-permute-start | bytes 1572872 | tf_op jit(solution)/shard_map/ppermute | solution.py:350
  61.7 2.0 %collective-permute-start.5 = (bf16[256,1024]{1,0:T(8,128)(2,1)}, bf16[256,1024]{1,0:T(8,128)(2,1)S(1)}, u32[]{:S(2)}, u32[]{:S(2)}) collective-permute-start(bf16[256,1024]{1,0:T(8,128)(2,1)} %add_convert_fusion.3), channel_id=1, source_target_pairs={{0,2},{1,15},{2,4},{3,1},{4,6},{5,3},{6,8},{7,5},{8,10},{9,7},{10,... | collective-permute-start | bytes 1572872 | tf_op jit(solution)/shard_map/ppermute | solution.py:341
  65.0 7.2 %collective-permute-done.5.a_ref = bf16[256,1024]{1,0:T(8,128)(2,1)S(1)} collective-permute-done((bf16[256,1024]{1,0:T(8,128)(2,1)}, bf16[256,1024]{1,0:T(8,128)(2,1)S(1)}, u32[]{:S(2)}, u32[]{:S(2)}) %collective-permute-start.5) | collective-permute-done | bytes 524320 | tf_op jit(solution)/shard_map/ppermute | solution.py:341
  72.4 9.3 %all_to_all.25.got_ref = bf16[4,512,128]{2,1,0:T(8,128)(2,1)S(1)} all-to-all(bf16[4,512,128]{2,1,0:T(8,128)(2,1)S(1)} %finish.1), channel_id=1, replica_groups={{0,16,32,48},{64,80,96,112},{128,144,160,176},{192,208,224,240},{256,27..., dimensions={0} | all-to-all | bytes 1048576 | tf_op jit(solution)/shard_map/all_to_all | solution.py:365
  81.8 18.8 %all_to_all.26.got_ref = bf16[12,48,128]{2,1,0:T(8,128)(2,1)S(1)} all-to-all(bf16[12,48,128]{2,1,0:T(8,128)(2,1)S(1)} %shard_map.94), channel_id=1, replica_groups={{0,64,128,192,256,320,384,448,512,576,640,704},{16,80,144,208,272,336,4..., dimensions={0} | all-to-all | bytes 294912 | tf_op jit(solution)/shard_map/all_to_all | solution.py:368
  100.7 13.0 %all_to_all.27.got_ref = bf16[12,48,128]{2,1,0:T(8,128)(2,1)S(1)} all-to-all(bf16[12,48,128]{2,1,0:T(8,128)(2,1)S(1)} %shard_map.95), channel_id=1, replica_groups={{0,64,128,192,256,320,384,448,512,576,640,704},{16,80,144,208,272,336,4..., dimensions={0} | all-to-all | bytes 294912 | tf_op jit(solution)/shard_map/all_to_all | solution.py:371
  113.7 9.4 %all_to_all.28.got_ref = bf16[4,528,128]{2,1,0:T(8,128)(2,1)S(1)} all-to-all(bf16[4,528,128]{2,1,0:T(8,128)(2,1)S(1)} %shard_map.96), channel_id=1, replica_groups={{0,16,32,48},{64,80,96,112},{128,144,160,176},{192,208,224,240},{256,27..., dimensions={0} | all-to-all | bytes 1081344 | tf_op jit(solution)/shard_map/all_to_all | solution.py:374
  123.2 12.1 %collective-permute-start.10 = (f32[16,128]{1,0:T(8,128)S(1)}, f32[16,128]{1,0:T(8,128)S(1)}, u32[]{:S(2)}, u32[]{:S(2)}) collective-permute-start(f32[16,128]{1,0:T(8,128)S(1)} %shard_map.97.a_ref), channel_id=1, source_target_pairs={{0,1},{1,0},{2,3},{3,2},{4,5},{5,4},{6,7},{7,6},{8,9},{9,8},{10,11... | collective-permute-start | bytes 24584 | tf_op jit(solution)/shard_map/ppermute | solution.py:378
  136.8 6.6 %all-to-all-start.4 = ((f32[8,16,128]{2,1,0:T(8,128)}), f32[8,16,128]{2,1,0:T(8,128)S(1)}, u32[]{:S(2)}, u32[]{:S(2)}) async-start(f32[8,16,128]{2,1,0:T(8,128)} %shard_map.98), calls=%async_computation.4 | async-start | bytes 131072 | tf_op jit(solution)/shard_map/all_to_all | solution.py:388
  145.2 5.4 %all-to-all-done.4.stats_ref = f32[8,16,128]{2,1,0:T(8,128)S(1)} async-done(((f32[8,16,128]{2,1,0:T(8,128)}), f32[8,16,128]{2,1,0:T(8,128)S(1)}, u32[]{:S(2)}, u32[]{:S(2)}) %all-to-all-start.4) | async-done | bytes 65568 | tf_op jit(solution)/shard_map/all_to_all | solution.py:388
  (37 shorter events, 12.2 us)
Async XLA Ops:
  0.6 1.2 copy-start
  1.9 0.7 copy-start.3
  2.6 12.6 %copy-start.2 = (bf16[128,1024]{1,0:T(8,128)(2,1)S(1)}, bf16[128,1024]{1,0:T(8,128)(2,1)}, u32[]{:S(2)}) copy-start(bf16[128,1024]{1,0:T(8,128)(2,1)} %c_ref.3) | copy-start | bytes 786436
  2.8 15.8 %collective-permute-start = (bf16[128,2048]{1,0:T(8,128)(2,1)S(1)}, bf16[128,2048]{1,0:T(8,128)(2,1)S(1)}, u32[]{:S(2)}, u32[]{:S(2)}) collective-permute-start(bf16[128,2048]{1,0:T(8,128)(2,1)S(1)} %get-tuple-element.27), channel_id=1, source_target_pairs={{0,1},{1,0},{2,3},{3,2},{4,5},{5,4},{6,7},{7,6},{8,9},{9,8},{10,11... | collective-permute-start | bytes 1572872 | tf_op jit(solution)/shard_map/ppermute | solution.py:328
  15.2 3.4 %collective-permute-start.1 = (bf16[128,1024]{1,0:T(8,128)(2,1)S(1)}, bf16[128,1024]{1,0:T(8,128)(2,1)S(1)}, u32[]{:S(2)}, u32[]{:S(2)}) collective-permute-start(bf16[128,1024]{1,0:T(8,128)(2,1)S(1)} %copy-done.2), channel_id=1, source_target_pairs={{0,1},{1,0},{2,3},{3,2},{4,5},{5,4},{6,7},{7,6},{8,9},{9,8},{10,11... | collective-permute-start | bytes 786440 | tf_op jit(solution)/shard_map/ppermute | solution.py:326
  21.1 10.2 %collective-permute-start.6 = (bf16[256,1024]{1,0:T(8,128)(2,1)S(1)}, bf16[256,1024]{1,0:T(8,128)(2,1)S(1)}, u32[]{:S(2)}, u32[]{:S(2)}) collective-permute-start(bf16[256,1024]{1,0:T(8,128)(2,1)S(1)} %get-tuple-element.31), channel_id=1, source_target_pairs={{0,2},{1,15},{2,4},{3,1},{4,6},{5,3},{6,8},{7,5},{8,10},{9,7},{10,... | collective-permute-start | bytes 1572872 | tf_op jit(solution)/shard_map/ppermute | solution.py:341
  23.1 13.9 %collective-permute-start.2 = (bf16[256,1024]{1,0:T(8,128)(2,1)S(1)}, bf16[256,1024]{1,0:T(8,128)(2,1)S(1)}, u32[]{:S(2)}, u32[]{:S(2)}) collective-permute-start(bf16[256,1024]{1,0:T(8,128)(2,1)S(1)} %products.2.outs_0_), channel_id=1, source_target_pairs={{0,2},{1,15},{2,4},{3,1},{4,6},{5,3},{6,8},{7,5},{8,10},{9,7},{10,... | collective-permute-start | bytes 1572872 | tf_op jit(solution)/shard_map/ppermute | solution.py:341
  31.6 11.0 %collective-permute-start.7 = (bf16[256,1024]{1,0:T(8,128)(2,1)S(1)}, bf16[256,1024]{1,0:T(8,128)(2,1)S(1)}, u32[]{:S(2)}, u32[]{:S(2)}) collective-permute-start(bf16[256,1024]{1,0:T(8,128)(2,1)S(1)} %add_convert_fusion.2), channel_id=1, source_target_pairs={{0,2},{1,15},{2,4},{3,1},{4,6},{5,3},{6,8},{7,5},{8,10},{9,7},{10,... | collective-permute-start | bytes 1572872 | tf_op jit(solution)/shard_map/ppermute | solution.py:341
  37.2 11.0 %collective-permute-start.3 = (bf16[256,1024]{1,0:T(8,128)(2,1)S(1)}, bf16[256,1024]{1,0:T(8,128)(2,1)S(1)}, u32[]{:S(2)}, u32[]{:S(2)}) collective-permute-start(bf16[256,1024]{1,0:T(8,128)(2,1)S(1)} %add_convert_fusion.5), channel_id=1, source_target_pairs={{0,2},{1,15},{2,4},{3,1},{4,6},{5,3},{6,8},{7,5},{8,10},{9,7},{10,... | collective-permute-start | bytes 1572872 | tf_op jit(solution)/shard_map/ppermute | solution.py:341
  42.8 11.0 %collective-permute-start.8 = (bf16[256,1024]{1,0:T(8,128)(2,1)S(1)}, bf16[256,1024]{1,0:T(8,128)(2,1)S(1)}, u32[]{:S(2)}, u32[]{:S(2)}) collective-permute-start(bf16[256,1024]{1,0:T(8,128)(2,1)S(1)} %add_convert_fusion.1), channel_id=1, source_target_pairs={{0,2},{1,15},{2,4},{3,1},{4,6},{5,3},{6,8},{7,5},{8,10},{9,7},{10,... | collective-permute-start | bytes 1572872 | tf_op jit(solution)/shard_map/ppermute | solution.py:341
  48.4 12.2 %collective-permute-start.4 = (bf16[256,1024]{1,0:T(8,128)(2,1)S(1)}, bf16[256,1024]{1,0:T(8,128)(2,1)S(1)}, u32[]{:S(2)}, u32[]{:S(2)}) collective-permute-start(bf16[256,1024]{1,0:T(8,128)(2,1)S(1)} %add_convert_fusion.4), channel_id=1, source_target_pairs={{0,2},{1,15},{2,4},{3,1},{4,6},{5,3},{6,8},{7,5},{8,10},{9,7},{10,... | collective-permute-start | bytes 1572872 | tf_op jit(solution)/shard_map/ppermute | solution.py:341
  54.0 10.9 %collective-permute-start.9 = (bf16[256,1024]{1,0:T(8,128)(2,1)S(1)}, bf16[256,1024]{1,0:T(8,128)(2,1)S(1)}, u32[]{:S(2)}, u32[]{:S(2)}) collective-permute-start(bf16[256,1024]{1,0:T(8,128)(2,1)S(1)} %add_convert_fusion), channel_id=1, source_target_pairs={{0,1},{1,0},{2,3},{3,2},{4,5},{5,4},{6,7},{7,6},{8,9},{9,8},{10,11... | collective-permute-start | bytes 1572872 | tf_op jit(solution)/shard_map/ppermute | solution.py:350
  60.7 3.1 %copy-start.6 = (s32[128,1]{0,1:T(1,128)S(1)}, s32[128,1]{0,1:T(1,128)}, u32[]{:S(2)}) copy-start(s32[128,1]{0,1:T(1,128)} %param.13) | copy-start | bytes 1540
  61.7 2.2 %copy-start.5 = (f32[1,1,4,16]{3,2,1,0:T(4,128)S(1)}, f32[1,1,4,16]{3,2,1,0:T(4,128)}, u32[]{:S(2)}) copy-start(f32[1,1,4,16]{3,2,1,0:T(4,128)} %param.11) | copy-start | bytes 772
  61.7 10.5 %collective-permute-start.5 = (bf16[256,1024]{1,0:T(8,128)(2,1)}, bf16[256,1024]{1,0:T(8,128)(2,1)S(1)}, u32[]{:S(2)}, u32[]{:S(2)}) collective-permute-start(bf16[256,1024]{1,0:T(8,128)(2,1)} %add_convert_fusion.3), channel_id=1, source_target_pairs={{0,2},{1,15},{2,4},{3,1},{4,6},{5,3},{6,8},{7,5},{8,10},{9,7},{10,... | collective-permute-start | bytes 1572872 | tf_op jit(solution)/shard_map/ppermute | solution.py:341
  123.2 13.0 %collective-permute-start.10 = (f32[16,128]{1,0:T(8,128)S(1)}, f32[16,128]{1,0:T(8,128)S(1)}, u32[]{:S(2)}, u32[]{:S(2)}) collective-permute-start(f32[16,128]{1,0:T(8,128)S(1)} %shard_map.97.a_ref), channel_id=1, source_target_pairs={{0,1},{1,0},{2,3},{3,2},{4,5},{5,4},{6,7},{7,6},{8,9},{9,8},{10,11... | collective-permute-start | bytes 24584 | tf_op jit(solution)/shard_map/ppermute | solution.py:378
  136.8 13.8 %all-to-all-start.4 = ((f32[8,16,128]{2,1,0:T(8,128)}), f32[8,16,128]{2,1,0:T(8,128)S(1)}, u32[]{:S(2)}, u32[]{:S(2)}) async-start(f32[8,16,128]{2,1,0:T(8,128)} %shard_map.98), calls=%async_computation.4 | async-start | bytes 131072 | tf_op jit(solution)/shard_map/all_to_all | solution.py:388
  143.4 7.2 %copy-start.1 = (bf16[256,1024]{1,0:T(8,128)(2,1)S(1)}, bf16[256,1024]{1,0:T(8,128)(2,1)}, u32[]{:S(2)}) copy-start(bf16[256,1024]{1,0:T(8,128)(2,1)} %weight_ref.1) | copy-start | bytes 1572868
  143.4 7.2 %copy-start.4 = (f32[8,128]{1,0:T(8,128)S(1)}, f32[8,128]{1,0:T(8,128)}, u32[]{:S(2)}) copy-start(f32[8,128]{1,0:T(8,128)} %state_ref.1) | copy-start | bytes 12292

commit v7 on v6

--- a/solution.py
+++ b/solution.py
@@ -16,7 +16,7 @@
 CORES = 2
 
 
-def arrange_kernel(slab, x_ref, gain_ref, mine_ref, theirs_ref):
+def arrange_kernel(slab, x_ref, gain_ref, cot_ref, mine_ref, theirs_ref):
     me = lax.axis_index("intra")
     my_y, my_core = me // CORES, me % CORES
     half = x_ref.shape[1] // (CORES * slab)
@@ -30,55 +30,58 @@
             block = x_ref[:, pl.ds(column, slab)].astype(jnp.float32)
             scaled = block * gain_ref[:, pl.ds(column, slab)]
             out[:, u * slab : (u + 1) * slab] = scaled.astype(out.dtype)
-
-
-def arrange(x, gain, slab):
+    theirs_ref[:, half * slab :] = cot_ref[...]
+
+
+def arrange(x, gain, cot, slab):
     tokens, d_model = x.shape
-    half = jax.ShapeDtypeStruct((tokens, d_model // CORES), x.dtype)
+    half = d_model // CORES
     vmem = pl.BlockSpec(memory_space=pltpu.VMEM)
     return pl.pallas_call(
         functools.partial(arrange_kernel, slab),
-        out_shape=(half, half),
-        in_specs=[vmem, vmem],
+        out_shape=(
+            jax.ShapeDtypeStruct((tokens, half), x.dtype),
+            jax.ShapeDtypeStruct((tokens, half + cot.shape[1]), x.dtype),
+        ),
+        in_specs=[vmem, vmem, vmem],
         out_specs=(vmem, vmem),
         cost_estimate=pl.CostEstimate(
             flops=tokens * d_model, bytes_accessed=4 * tokens * d_model, transcendentals=0
         ),
         compiler_params=pltpu.CompilerParams(vmem_limit_bytes=12 << 20),
         name="arrange",
-    )(x, gain)
-
-
-def products_kernel(slab, begin, after, x_ref, xg_ref, c_ref, cg_ref, *outs):
+    )(x, gain, cot)
+
+
+def products_kernel(slab, pieces, after, x_ref, got_ref, c_ref, *outs):
     dims = (((0,), (0,)), ((), ()))
-    for u, out in enumerate(outs[after:], begin):
+    rows = x_ref.shape[1]
+    for u, out in zip(pieces, outs[after:]):
         cols = slice(u * slab, (u + 1) * slab)
         total = lax.dot_general(
             x_ref[:, cols], c_ref[...], dims, preferred_element_type=jnp.float32
         ) + lax.dot_general(
-            xg_ref[:, cols], cg_ref[...], dims, preferred_element_type=jnp.float32
+            got_ref[:, cols], got_ref[:, rows:], dims, preferred_element_type=jnp.float32
         )
         out[...] = total.astype(out.dtype)
 
 
-def products(mine, got, cot, cot_got, slab, begin, end, *after):
-    tokens, _ = mine.shape
+def products(mine, got, cot, slab, pieces, *after):
+    tokens = mine.shape[0]
     width = cot.shape[1]
-    count = end - begin
+    size = len(pieces) * slab * width
     vmem = pl.BlockSpec(memory_space=pltpu.VMEM)
     return pl.pallas_call(
-        functools.partial(products_kernel, slab, begin, len(after)),
-        out_shape=tuple(jax.ShapeDtypeStruct((slab, width), cot.dtype) for _ in range(count)),
-        in_specs=[vmem] * 4 + [pl.BlockSpec(memory_space=pl.ANY)] * len(after),
-        out_specs=tuple([vmem] * count),
+        functools.partial(products_kernel, slab, pieces, len(after)),
+        out_shape=tuple(jax.ShapeDtypeStruct((slab, width), cot.dtype) for _ in pieces),
+        in_specs=[vmem] * 3 + [pl.BlockSpec(memory_space=pl.ANY)] * len(after),
+        out_specs=tuple([vmem] * len(pieces)),
         cost_estimate=pl.CostEstimate(
-            flops=4 * tokens * count * slab * width,
-            bytes_accessed=4 * count * slab * width,
-            transcendentals=0,
+            flops=4 * tokens * size, bytes_accessed=4 * size, transcendentals=0
         ),
         compiler_params=pltpu.CompilerParams(vmem_limit_bytes=16 << 20),
         name="products",
-    )(mine, got, cot, cot_got, *after)
+    )(mine, got, cot, *after)
 
 
 def finish_kernel(a_ref, b_ref, out_ref):
@@ -323,12 +326,14 @@
 
 
     swap = [(i, i ^ 1) for i in range(intra)]
-    cot_got = lax.ppermute(cotangent, "intra", swap)
-    mine, theirs = arrange(normed, norm_gain[None, :], slab)
-    got = lax.ppermute(theirs, "intra", swap)
-    inputs = (mine, got, cotangent, cot_got, slab)
-    parts = products(*inputs, 0, 1)
-    parts = parts + products(*inputs, 1, mine.shape[1] // slab, parts[0])
+    mine, theirs = arrange(normed, norm_gain[None, :], cotangent, slab)
+    inputs = (mine, lax.ppermute(theirs, "intra", swap), cotangent, slab)
+    n_pieces = mine.shape[1] // slab
+    early = (0, 2)
+    late = tuple(u for u in range(n_pieces) if u not in early)
+    made = products(*inputs, early)
+    made = made + products(*inputs, late, made[0])
+    parts = [made[(early + late).index(u)] for u in range(n_pieces)]
 
     ring = [
         (y * CORES + c, ((y + 1 - 2 * c) % n_y) * CORES + c) for y in range(n_y) for c in range(CORES)

time: 153 us -> 144 us (0.941)
  waiting for transfers between devices: 31.5 us -> 25.6 us
  starting transfers between devices: 57 us -> 53.3 us
    ppermute x7, waiting for transfers between devices: 23.7 us -> 17 us  [hop(): return lax.ppermute(a, 'intra', ring)]
    ppermute x1, starting transfers between devices: 12.1 us -> 9.01 us  [on_device(): partner = lax.ppermute(stats, 'intra', swap)]
    ppermute x2 -> x1, starting transfers between devices: 14.3 us -> 12.4 us  [on_device(): inputs = (mine, lax.ppermute(theirs, 'intra', swap), cotangent, slab)]
  transfers between devices with their start and end apart: 12 -> 11, of which waited for: 9 -> 10; matrix products, arithmetic and copies ran while one was open for 1% -> 1% of each run, Pallas kernels for 2% -> 3%
where the time goes in v7:
time: 144 us; the launch traced here: 143 us
  starting transfers between devices  53.3 us (37%)
  blocking collectives  50.3 us (35%)
  waiting for transfers between devices  25.6 us (18%)
  Pallas kernels  7.92 us (6%)
  local copies, waits for them, and re-layouts  3.02 us (2%)
  other arithmetic  1.93 us (1%)
    all_to_all x2, blocking collectives, on_device(): lax.all_to_all(sent, 'grp', 0, 0, axis_index_groups=z_groups, tiled=True)  31.3 us
    ppermute x7, starting transfers between devices, hop(): return lax.ppermute(a, 'intra', ring)  18.4 us
    ppermute x7, waiting for transfers between devices, hop(): return lax.ppermute(a, 'intra', ring)  17 us
    ppermute x1, starting transfers between devices, on_device(): inputs = (mine, lax.ppermute(theirs, 'intra', swap), cotangent, slab)  12.4 us
    all_to_all x1, blocking collectives, on_device(): lax.all_to_all(own, 'grp', 0, 0, axis_index_groups=x_groups, tiled=True)  9.56 us
    all_to_all x1, blocking collectives, on_device(): lax.all_to_all(sent, 'grp', 0, 0, axis_index_groups=x_groups, tiled=True)  9.39 us
    ppermute x1, starting transfers between devices, on_device(): partner = lax.ppermute(stats, 'intra', swap)  9.01 us
    ppermute x1, starting transfers between devices, on_device(): other = lax.ppermute(give, 'intra', swap)  6.97 us
  transfers between devices with their start and end apart: 11, of which 10 were waited for; matrix products, arithmetic and copies ran while one was open for 1% of the time, Pallas kernels for 3%

profile of v7, /device:TPU:1, one launch (start us, length us, event | category | flops | bytes accessed | tf_op | source)
XLA Modules:
  0.0 142.9 jit_solution(13452743286211233518)
XLA Ops:
  3.7 12.4 %collective-permute-start = (bf16[128,3072]{1,0:T(8,128)(2,1)S(1)}, bf16[128,3072]{1,0:T(8,128)(2,1)S(1)}, u32[]{:S(2)}, u32[]{:S(2)}) collective-permute-start(bf16[128,3072]{1,0:T(8,128)(2,1)S(1)} %get-tuple-element.28), channel_id=1, source_target_pairs={{0,1},{1,0},{2,3},{3,2},{4,5},{5,4},{6,7},{7,6},{8,9},{9,8},{10,11... | collective-permute-start | bytes 2359304 | tf_op jit(solution)/shard_map/ppermute | solution.py:330
  16.1 1.9 %collective-permute-done.got_ref = bf16[128,3072]{1,0:T(8,128)(2,1)S(1)} collective-permute-done((bf16[128,3072]{1,0:T(8,128)(2,1)S(1)}, bf16[128,3072]{1,0:T(8,128)(2,1)S(1)}, u32[]{:S(2)}, u32[]{:S(2)}) %collective-permute-start) | collective-permute-done | bytes 786464 | tf_op jit(solution)/shard_map/ppermute | solution.py:330
  18.7 1.9 %collective-permute-start.1 = (bf16[256,1024]{1,0:T(8,128)(2,1)S(1)}, bf16[256,1024]{1,0:T(8,128)(2,1)S(1)}, u32[]{:S(2)}, u32[]{:S(2)}) collective-permute-start(bf16[256,1024]{1,0:T(8,128)(2,1)S(1)} %get-tuple-element.29.outs_0_), channel_id=1, source_target_pairs={{0,2},{1,15},{2,4},{3,1},{4,6},{5,3},{6,8},{7,5},{8,10},{9,7},{10,... | collective-permute-start | bytes 1572872 | tf_op jit(solution)/shard_map/ppermute | solution.py:346
  20.7 1.9 %collective-permute-start.5 = (bf16[256,1024]{1,0:T(8,128)(2,1)S(1)}, bf16[256,1024]{1,0:T(8,128)(2,1)S(1)}, u32[]{:S(2)}, u32[]{:S(2)}) collective-permute-start(bf16[256,1024]{1,0:T(8,128)(2,1)S(1)} %get-tuple-element.33), channel_id=1, source_target_pairs={{0,2},{1,15},{2,4},{3,1},{4,6},{5,3},{6,8},{7,5},{8,10},{9,7},{10,... | collective-permute-start | bytes 1572872 | tf_op jit(solution)/shard_map/ppermute | solution.py:346
  22.6 1.8 %products.3 = (bf16[256,1024]{1,0:T(8,128)(2,1)S(1)}, bf16[256,1024]{1,0:T(8,128)(2,1)S(1)}, bf16[256,1024]{1,0:T(8,128)(2,1)S(1)}, bf16[256,1024]{1,0:T(8,128)(...) custom-call(bf16[128,2048]{1,0:T(8,128)(2,1)S(1)} %get-tuple-element.27.x_ref, ...), custom_call_target="tpu_custom_call" | custom-call | flops 805306368 | bytes 6291456 | tf_op jit(solution)/shard_map/products/pallas_call | solution.py:74
  24.4 4.5 %collective-permute-done.1 = bf16[256,1024]{1,0:T(8,128)(2,1)S(1)} collective-permute-done((bf16[256,1024]{1,0:T(8,128)(2,1)S(1)}, bf16[256,1024]{1,0:T(8,128)(2,1)S(1)}, u32[]{:S(2)}, u32[]{:S(2)}) %collective-permute-start.1) | collective-permute-done | bytes 524320 | tf_op jit(solution)/shard_map/ppermute | solution.py:346
  29.1 2.8 %collective-permute-start.2 = (bf16[256,1024]{1,0:T(8,128)(2,1)S(1)}, bf16[256,1024]{1,0:T(8,128)(2,1)S(1)}, u32[]{:S(2)}, u32[]{:S(2)}) collective-permute-start(bf16[256,1024]{1,0:T(8,128)(2,1)S(1)} %add_convert_fusion.5), channel_id=1, source_target_pairs={{0,2},{1,15},{2,4},{3,1},{4,6},{5,3},{6,8},{7,5},{8,10},{9,7},{10,... | collective-permute-start | bytes 1572872 | tf_op jit(solution)/shard_map/ppermute | solution.py:346
  32.0 2.6 %collective-permute-done.5 = bf16[256,1024]{1,0:T(8,128)(2,1)S(1)} collective-permute-done((bf16[256,1024]{1,0:T(8,128)(2,1)S(1)}, bf16[256,1024]{1,0:T(8,128)(2,1)S(1)}, u32[]{:S(2)}, u32[]{:S(2)}) %collective-permute-start.5) | collective-permute-done | bytes 524320 | tf_op jit(solution)/shard_map/ppermute | solution.py:346
  34.8 2.8 %collective-permute-start.6 = (bf16[256,1024]{1,0:T(8,128)(2,1)S(1)}, bf16[256,1024]{1,0:T(8,128)(2,1)S(1)}, u32[]{:S(2)}, u32[]{:S(2)}) collective-permute-start(bf16[256,1024]{1,0:T(8,128)(2,1)S(1)} %add_convert_fusion.2), channel_id=1, source_target_pairs={{0,2},{1,15},{2,4},{3,1},{4,6},{5,3},{6,8},{7,5},{8,10},{9,7},{10,... | collective-permute-start | bytes 1572872 | tf_op jit(solution)/shard_map/ppermute | solution.py:346
  37.6 2.6 %collective-permute-done.2 = bf16[256,1024]{1,0:T(8,128)(2,1)S(1)} collective-permute-done((bf16[256,1024]{1,0:T(8,128)(2,1)S(1)}, bf16[256,1024]{1,0:T(8,128)(2,1)S(1)}, u32[]{:S(2)}, u32[]{:S(2)}) %collective-permute-start.2) | collective-permute-done | bytes 524320 | tf_op jit(solution)/shard_map/ppermute | solution.py:346
  40.4 2.9 %collective-permute-start.3 = (bf16[256,1024]{1,0:T(8,128)(2,1)S(1)}, bf16[256,1024]{1,0:T(8,128)(2,1)S(1)}, u32[]{:S(2)}, u32[]{:S(2)}) collective-permute-start(bf16[256,1024]{1,0:T(8,128)(2,1)S(1)} %add_convert_fusion.4), channel_id=1, source_target_pairs={{0,2},{1,15},{2,4},{3,1},{4,6},{5,3},{6,8},{7,5},{8,10},{9,7},{10,... | collective-permute-start | bytes 1572872 | tf_op jit(solution)/shard_map/ppermute | solution.py:346
  43.3 2.5 %collective-permute-done.6 = bf16[256,1024]{1,0:T(8,128)(2,1)S(1)} collective-permute-done((bf16[256,1024]{1,0:T(8,128)(2,1)S(1)}, bf16[256,1024]{1,0:T(8,128)(2,1)S(1)}, u32[]{:S(2)}, u32[]{:S(2)}) %collective-permute-start.6) | collective-permute-done | bytes 524320 | tf_op jit(solution)/shard_map/ppermute | solution.py:346
  46.0 2.9 %collective-permute-start.7 = (bf16[256,1024]{1,0:T(8,128)(2,1)S(1)}, bf16[256,1024]{1,0:T(8,128)(2,1)S(1)}, u32[]{:S(2)}, u32[]{:S(2)}) collective-permute-start(bf16[256,1024]{1,0:T(8,128)(2,1)S(1)} %add_convert_fusion.1), channel_id=1, source_target_pairs={{0,2},{1,15},{2,4},{3,1},{4,6},{5,3},{6,8},{7,5},{8,10},{9,7},{10,... | collective-permute-start | bytes 1572872 | tf_op jit(solution)/shard_map/ppermute | solution.py:346
  48.9 2.5 %collective-permute-done.3 = bf16[256,1024]{1,0:T(8,128)(2,1)S(1)} collective-permute-done((bf16[256,1024]{1,0:T(8,128)(2,1)S(1)}, bf16[256,1024]{1,0:T(8,128)(2,1)S(1)}, u32[]{:S(2)}, u32[]{:S(2)}) %collective-permute-start.3) | collective-permute-done | bytes 524320 | tf_op jit(solution)/shard_map/ppermute | solution.py:346
  51.6 3.0 %collective-permute-start.4 = (bf16[256,1024]{1,0:T(8,128)(2,1)S(1)}, bf16[256,1024]{1,0:T(8,128)(2,1)S(1)}, u32[]{:S(2)}, u32[]{:S(2)}) collective-permute-start(bf16[256,1024]{1,0:T(8,128)(2,1)S(1)} %add_convert_fusion.3), channel_id=1, source_target_pairs={{0,2},{1,15},{2,4},{3,1},{4,6},{5,3},{6,8},{7,5},{8,10},{9,7},{10,... | collective-permute-start | bytes 1572872 | tf_op jit(solution)/shard_map/ppermute | solution.py:346
  54.7 2.4 %collective-permute-done.7 = bf16[256,1024]{1,0:T(8,128)(2,1)S(1)} collective-permute-done((bf16[256,1024]{1,0:T(8,128)(2,1)S(1)}, bf16[256,1024]{1,0:T(8,128)(2,1)S(1)}, u32[]{:S(2)}, u32[]{:S(2)}) %collective-permute-start.7) | collective-permute-done | bytes 524320 | tf_op jit(solution)/shard_map/ppermute | solution.py:346
  58.0 7.0 %collective-permute-start.8 = (bf16[256,1024]{1,0:T(8,128)(2,1)}, bf16[256,1024]{1,0:T(8,128)(2,1)S(1)}, u32[]{:S(2)}, u32[]{:S(2)}) collective-permute-start(bf16[256,1024]{1,0:T(8,128)(2,1)} %add_convert_fusion), channel_id=1, source_target_pairs={{0,1},{1,0},{2,3},{3,2},{4,5},{5,4},{6,7},{7,6},{8,9},{9,8},{10,11... | collective-permute-start | bytes 1572872 | tf_op jit(solution)/shard_map/ppermute | solution.py:355
  66.9 9.6 %all_to_all.25.got_ref = bf16[4,512,128]{2,1,0:T(8,128)(2,1)S(1)} all-to-all(bf16[4,512,128]{2,1,0:T(8,128)(2,1)S(1)} %finish.1), channel_id=1, replica_groups={{0,16,32,48},{64,80,96,112},{128,144,160,176},{192,208,224,240},{256,27..., dimensions={0} | all-to-all | bytes 1048576 | tf_op jit(solution)/shard_map/all_to_all | solution.py:370
  76.5 17.9 %all_to_all.26.got_ref = bf16[12,48,128]{2,1,0:T(8,128)(2,1)S(1)} all-to-all(bf16[12,48,128]{2,1,0:T(8,128)(2,1)S(1)} %shard_map.94), channel_id=1, replica_groups={{0,64,128,192,256,320,384,448,512,576,640,704},{16,80,144,208,272,336,4..., dimensions={0} | all-to-all | bytes 294912 | tf_op jit(solution)/shard_map/all_to_all | solution.py:373
  94.5 13.4 %all_to_all.27.got_ref = bf16[12,48,128]{2,1,0:T(8,128)(2,1)S(1)} all-to-all(bf16[12,48,128]{2,1,0:T(8,128)(2,1)S(1)} %shard_map.95), channel_id=1, replica_groups={{0,64,128,192,256,320,384,448,512,576,640,704},{16,80,144,208,272,336,4..., dimensions={0} | all-to-all | bytes 294912 | tf_op jit(solution)/shard_map/all_to_all | solution.py:376
  107.9 9.4 %all_to_all.28.got_ref = bf16[4,528,128]{2,1,0:T(8,128)(2,1)S(1)} all-to-all(bf16[4,528,128]{2,1,0:T(8,128)(2,1)S(1)} %shard_map.96), channel_id=1, replica_groups={{0,16,32,48},{64,80,96,112},{128,144,160,176},{192,208,224,240},{256,27..., dimensions={0} | all-to-all | bytes 1081344 | tf_op jit(solution)/shard_map/all_to_all | solution.py:379
  117.4 9.0 %collective-permute-start.9 = (f32[16,128]{1,0:T(8,128)S(1)}, f32[16,128]{1,0:T(8,128)S(1)}, u32[]{:S(2)}, u32[]{:S(2)}) collective-permute-start(f32[16,128]{1,0:T(8,128)S(1)} %shard_map.97.a_ref), channel_id=1, source_target_pairs={{0,1},{1,0},{2,3},{3,2},{4,5},{5,4},{6,7},{7,6},{8,9},{9,8},{10,11... | collective-permute-start | bytes 24584 | tf_op jit(solution)/shard_map/ppermute | solution.py:383
  127.9 6.6 %all-to-all-start.4 = ((f32[8,16,128]{2,1,0:T(8,128)}), f32[8,16,128]{2,1,0:T(8,128)S(1)}, u32[]{:S(2)}, u32[]{:S(2)}) async-start(f32[8,16,128]{2,1,0:T(8,128)} %shard_map.98), calls=%async_computation.4 | async-start | bytes 131072 | tf_op jit(solution)/shard_map/all_to_all | solution.py:393
  136.3 5.4 %all-to-all-done.4.stats_ref = f32[8,16,128]{2,1,0:T(8,128)S(1)} async-done(((f32[8,16,128]{2,1,0:T(8,128)}), f32[8,16,128]{2,1,0:T(8,128)S(1)}, u32[]{:S(2)}, u32[]{:S(2)}) %all-to-all-start.4) | async-done | bytes 65568 | tf_op jit(solution)/shard_map/all_to_all | solution.py:393
  (37 shorter events, 12.3 us)
Async XLA Ops:
  0.6 1.2 copy-start
  1.9 0.9 copy-start.1
  2.8 0.7 copy-start.4
  3.5 14.5 %copy-start.2 = (bf16[128,1024]{1,0:T(8,128)(2,1)S(1)}, bf16[128,1024]{1,0:T(8,128)(2,1)}, u32[]{:S(2)}) copy-start(bf16[128,1024]{1,0:T(8,128)(2,1)} %c_ref.3) | copy-start | bytes 786436
  3.7 14.3 %collective-permute-start = (bf16[128,3072]{1,0:T(8,128)(2,1)S(1)}, bf16[128,3072]{1,0:T(8,128)(2,1)S(1)}, u32[]{:S(2)}, u32[]{:S(2)}) collective-permute-start(bf16[128,3072]{1,0:T(8,128)(2,1)S(1)} %get-tuple-element.28), channel_id=1, source_target_pairs={{0,1},{1,0},{2,3},{3,2},{4,5},{5,4},{6,7},{7,6},{8,9},{9,8},{10,11... | collective-permute-start | bytes 2359304 | tf_op jit(solution)/shard_map/ppermute | solution.py:330
  18.7 10.2 %collective-permute-start.1 = (bf16[256,1024]{1,0:T(8,128)(2,1)S(1)}, bf16[256,1024]{1,0:T(8,128)(2,1)S(1)}, u32[]{:S(2)}, u32[]{:S(2)}) collective-permute-start(bf16[256,1024]{1,0:T(8,128)(2,1)S(1)} %get-tuple-element.29.outs_0_), channel_id=1, source_target_pairs={{0,2},{1,15},{2,4},{3,1},{4,6},{5,3},{6,8},{7,5},{8,10},{9,7},{10,... | collective-permute-start | bytes 1572872 | tf_op jit(solution)/shard_map/ppermute | solution.py:346
  20.7 13.9 %collective-permute-start.5 = (bf16[256,1024]{1,0:T(8,128)(2,1)S(1)}, bf16[256,1024]{1,0:T(8,128)(2,1)S(1)}, u32[]{:S(2)}, u32[]{:S(2)}) collective-permute-start(bf16[256,1024]{1,0:T(8,128)(2,1)S(1)} %get-tuple-element.33), channel_id=1, source_target_pairs={{0,2},{1,15},{2,4},{3,1},{4,6},{5,3},{6,8},{7,5},{8,10},{9,7},{10,... | collective-permute-start | bytes 1572872 | tf_op jit(solution)/shard_map/ppermute | solution.py:346
  29.1 11.0 %collective-permute-start.2 = (bf16[256,1024]{1,0:T(8,128)(2,1)S(1)}, bf16[256,1024]{1,0:T(8,128)(2,1)S(1)}, u32[]{:S(2)}, u32[]{:S(2)}) collective-permute-start(bf16[256,1024]{1,0:T(8,128)(2,1)S(1)} %add_convert_fusion.5), channel_id=1, source_target_pairs={{0,2},{1,15},{2,4},{3,1},{4,6},{5,3},{6,8},{7,5},{8,10},{9,7},{10,... | collective-permute-start | bytes 1572872 | tf_op jit(solution)/shard_map/ppermute | solution.py:346
  34.8 11.0 %collective-permute-start.6 = (bf16[256,1024]{1,0:T(8,128)(2,1)S(1)}, bf16[256,1024]{1,0:T(8,128)(2,1)S(1)}, u32[]{:S(2)}, u32[]{:S(2)}) collective-permute-start(bf16[256,1024]{1,0:T(8,128)(2,1)S(1)} %add_convert_fusion.2), channel_id=1, source_target_pairs={{0,2},{1,15},{2,4},{3,1},{4,6},{5,3},{6,8},{7,5},{8,10},{9,7},{10,... | collective-permute-start | bytes 1572872 | tf_op jit(solution)/shard_map/ppermute | solution.py:346
  40.4 11.0 %collective-permute-start.3 = (bf16[256,1024]{1,0:T(8,128)(2,1)S(1)}, bf16[256,1024]{1,0:T(8,128)(2,1)S(1)}, u32[]{:S(2)}, u32[]{:S(2)}) collective-permute-start(bf16[256,1024]{1,0:T(8,128)(2,1)S(1)} %add_convert_fusion.4), channel_id=1, source_target_pairs={{0,2},{1,15},{2,4},{3,1},{4,6},{5,3},{6,8},{7,5},{8,10},{9,7},{10,... | collective-permute-start | bytes 1572872 | tf_op jit(solution)/shard_map/ppermute | solution.py:346
  46.0 11.0 %collective-permute-start.7 = (bf16[256,1024]{1,0:T(8,128)(2,1)S(1)}, bf16[256,1024]{1,0:T(8,128)(2,1)S(1)}, u32[]{:S(2)}, u32[]{:S(2)}) collective-permute-start(bf16[256,1024]{1,0:T(8,128)(2,1)S(1)} %add_convert_fusion.1), channel_id=1, source_target_pairs={{0,2},{1,15},{2,4},{3,1},{4,6},{5,3},{6,8},{7,5},{8,10},{9,7},{10,... | collective-permute-start | bytes 1572872 | tf_op jit(solution)/shard_map/ppermute | solution.py:346
  51.6 14.6 %collective-permute-start.4 = (bf16[256,1024]{1,0:T(8,128)(2,1)S(1)}, bf16[256,1024]{1,0:T(8,128)(2,1)S(1)}, u32[]{:S(2)}, u32[]{:S(2)}) collective-permute-start(bf16[256,1024]{1,0:T(8,128)(2,1)S(1)} %add_convert_fusion.3), channel_id=1, source_target_pairs={{0,2},{1,15},{2,4},{3,1},{4,6},{5,3},{6,8},{7,5},{8,10},{9,7},{10,... | collective-permute-start | bytes 1572872 | tf_op jit(solution)/shard_map/ppermute | solution.py:346
  57.0 8.0 %copy-start.7 = (s32[128,1]{0,1:T(1,128)S(1)}, s32[128,1]{0,1:T(1,128)}, u32[]{:S(2)}) copy-start(s32[128,1]{0,1:T(1,128)} %param.13) | copy-start | bytes 1540
  58.0 7.1 %copy-start.6 = (f32[1,1,4,16]{3,2,1,0:T(4,128)S(1)}, f32[1,1,4,16]{3,2,1,0:T(4,128)}, u32[]{:S(2)}) copy-start(f32[1,1,4,16]{3,2,1,0:T(4,128)} %param.11) | copy-start | bytes 772
  58.0 8.7 %collective-permute-start.8 = (bf16[256,1024]{1,0:T(8,128)(2,1)}, bf16[256,1024]{1,0:T(8,128)(2,1)S(1)}, u32[]{:S(2)}, u32[]{:S(2)}) collective-permute-start(bf16[256,1024]{1,0:T(8,128)(2,1)} %add_convert_fusion), channel_id=1, source_target_pairs={{0,1},{1,0},{2,3},{3,2},{4,5},{5,4},{6,7},{7,6},{8,9},{9,8},{10,11... | collective-permute-start | bytes 1572872 | tf_op jit(solution)/shard_map/ppermute | solution.py:355
  117.4 9.8 %collective-permute-start.9 = (f32[16,128]{1,0:T(8,128)S(1)}, f32[16,128]{1,0:T(8,128)S(1)}, u32[]{:S(2)}, u32[]{:S(2)}) collective-permute-start(f32[16,128]{1,0:T(8,128)S(1)} %shard_map.97.a_ref), channel_id=1, source_target_pairs={{0,1},{1,0},{2,3},{3,2},{4,5},{5,4},{6,7},{7,6},{8,9},{9,8},{10,11... | collective-permute-start | bytes 24584 | tf_op jit(solution)/shard_map/ppermute | solution.py:383
  127.9 13.8 %all-to-all-start.4 = ((f32[8,16,128]{2,1,0:T(8,128)}), f32[8,16,128]{2,1,0:T(8,128)S(1)}, u32[]{:S(2)}, u32[]{:S(2)}) async-start(f32[8,16,128]{2,1,0:T(8,128)} %shard_map.98), calls=%async_computation.4 | async-start | bytes 131072 | tf_op jit(solution)/shard_map/all_to_all | solution.py:393
  134.5 7.2 %copy-start.3 = (bf16[256,1024]{1,0:T(8,128)(2,1)S(1)}, bf16[256,1024]{1,0:T(8,128)(2,1)}, u32[]{:S(2)}) copy-start(bf16[256,1024]{1,0:T(8,128)(2,1)} %weight_ref.1) | copy-start | bytes 1572868
  134.5 7.2 %copy-start.5 = (f32[8,128]{1,0:T(8,128)S(1)}, f32[8,128]{1,0:T(8,128)}, u32[]{:S(2)}) copy-start(f32[8,128]{1,0:T(8,128)} %state_ref.1) | copy-start | bytes 12292

commit v8 on v7

--- a/solution.py
+++ b/solution.py
@@ -16,41 +16,76 @@
 CORES = 2
 
 
-def arrange_kernel(slab, x_ref, gain_ref, cot_ref, mine_ref, theirs_ref):
+def scale_pieces(slab, other, x_ref, gain_ref, out_ref):
     me = lax.axis_index("intra")
     my_y, my_core = me // CORES, me % CORES
     half = x_ref.shape[1] // (CORES * slab)
     n_y = 2 * half // CORES
     ahead = [n_y] + [2 * k + h for k in range(n_y // 2 - 1, 0, -1) for h in (0, 1)] + [1]
     behind = [n_y + 1] + [2 * k + h for k in range(n_y // 2 + 1, n_y) for h in (1, 0)] + [0]
-    for out, up, down in ((theirs_ref, behind, ahead), (mine_ref, ahead, behind)):
-        for u in range(half):
-            piece = lax.rem(jnp.where(my_core == 0, up[u], down[u]) + 2 * my_y, 2 * half)
-            column = pl.multiple_of(piece * slab, slab)
-            block = x_ref[:, pl.ds(column, slab)].astype(jnp.float32)
-            scaled = block * gain_ref[:, pl.ds(column, slab)]
-            out[:, u * slab : (u + 1) * slab] = scaled.astype(out.dtype)
-    theirs_ref[:, half * slab :] = cot_ref[...]
-
-
-def arrange(x, gain, cot, slab):
+    up, down = (behind, ahead) if other else (ahead, behind)
+    for u in range(half):
+        piece = lax.rem(jnp.where(my_core == 0, up[u], down[u]) + 2 * my_y, 2 * half)
+        column = pl.multiple_of(piece * slab, slab)
+        block = x_ref[:, pl.ds(column, slab)].astype(jnp.float32)
+        scaled = block * gain_ref[:, pl.ds(column, slab)]
+        out_ref[:, u * slab : (u + 1) * slab] = scaled.astype(out_ref.dtype)
+
+
+def theirs_kernel(slab, x_hbm, gain_hbm, cot_hbm, out_ref, x_ref, gain_ref, cot_ref, sems):
+    loads = [
+        pltpu.make_async_copy(source, target, sems.at[n])
+        for n, (source, target) in enumerate(
+            ((x_hbm, x_ref), (gain_hbm, gain_ref), (cot_hbm, cot_ref))
+        )
+    ]
+    for load in loads:
+        load.start()
+    for load in loads:
+        load.wait()
+    scale_pieces(slab, True, x_ref, gain_ref, out_ref)
+    out_ref[:, x_ref.shape[1] // CORES :] = cot_ref[...]
+
+
+def theirs_of(x, gain, cot, slab):
     tokens, d_model = x.shape
-    half = d_model // CORES
-    vmem = pl.BlockSpec(memory_space=pltpu.VMEM)
-    return pl.pallas_call(
-        functools.partial(arrange_kernel, slab),
-        out_shape=(
-            jax.ShapeDtypeStruct((tokens, half), x.dtype),
-            jax.ShapeDtypeStruct((tokens, half + cot.shape[1]), x.dtype),
-        ),
-        in_specs=[vmem, vmem, vmem],
-        out_specs=(vmem, vmem),
+    return pl.pallas_call(
+        functools.partial(theirs_kernel, slab),
+        out_shape=jax.ShapeDtypeStruct((tokens, d_model // CORES + cot.shape[1]), x.dtype),
+        in_specs=[pl.BlockSpec(memory_space=pltpu.HBM)] * 3,
+        out_specs=pl.BlockSpec(memory_space=pltpu.VMEM),
+        scratch_shapes=[
+            pltpu.VMEM(x.shape, x.dtype),
+            pltpu.VMEM(gain.shape, gain.dtype),
+            pltpu.VMEM(cot.shape, cot.dtype),
+            pltpu.SemaphoreType.DMA((3,)),
+        ],
         cost_estimate=pl.CostEstimate(
             flops=tokens * d_model, bytes_accessed=4 * tokens * d_model, transcendentals=0
         ),
+        compiler_params=pltpu.CompilerParams(vmem_limit_bytes=67000000),
+        name="theirs",
+    )(x, gain, cot)
+
+
+def mine_kernel(slab, x_ref, gain_ref, after_ref, out_ref):
+    scale_pieces(slab, False, x_ref, gain_ref, out_ref)
+
+
+def mine_of(x, gain, slab, after):
+    tokens, d_model = x.shape
+    vmem = pl.BlockSpec(memory_space=pltpu.VMEM)
+    return pl.pallas_call(
+        functools.partial(mine_kernel, slab),
+        out_shape=jax.ShapeDtypeStruct((tokens, d_model // CORES), x.dtype),
+        in_specs=[vmem, vmem, pl.BlockSpec(memory_space=pl.ANY)],
+        out_specs=vmem,
+        cost_estimate=pl.CostEstimate(
+            flops=tokens * d_model, bytes_accessed=2 * tokens * d_model, transcendentals=0
+        ),
         compiler_params=pltpu.CompilerParams(vmem_limit_bytes=12 << 20),
-        name="arrange",
-    )(x, gain, cot)
+        name="mine",
+    )(x, gain, after)
 
 
 def products_kernel(slab, pieces, after, x_ref, got_ref, c_ref, *outs):
@@ -326,7 +361,9 @@
 
 
     swap = [(i, i ^ 1) for i in range(intra)]
-    mine, theirs = arrange(normed, norm_gain[None, :], cotangent, slab)
+    gain = norm_gain[None, :]
+    theirs = theirs_of(normed, gain, cotangent, slab)
+    mine = mine_of(normed, gain, slab, theirs)
     inputs = (mine, lax.ppermute(theirs, "intra", swap), cotangent, slab)
     n_pieces = mine.shape[1] // slab
     early = (0, 2)

time: 144 us -> 144 us (level)
  Pallas kernels: 7.92 us -> 10.1 us
  waiting for transfers between devices: 25.6 us -> 23.7 us
    pallas_call x1 -> x2, Pallas kernels: 0.18 us -> 2.38 us  [the longest x1 2.29 us: theirs_of(): pl.pallas_call(functools.partial(theirs_kernel, slab), out_shape=jax.Shap...]
    ppermute x1, waiting for transfers between devices: 1.89 us -> 0.01 us  [on_device(): inputs = (mine, lax.ppermute(theirs, 'intra', swap), cotangent, slab)]
  transfers between devices with their start and end apart: 11 -> 11, of which waited for: 10 -> 9; matrix products, arithmetic and copies ran while one was open for 1% -> 1% of each run, Pallas kernels for 3% -> 3%
where the time goes in v8:
time: 144 us; the launch traced here: 143 us
  starting transfers between devices  53 us (37%)
  blocking collectives  50.2 us (35%)
  waiting for transfers between devices  23.7 us (16%)
  Pallas kernels  10.1 us (7%)
  local copies, waits for them, and re-layouts  3.33 us (2%)
  other arithmetic  1.93 us (1%)
    all_to_all x2, blocking collectives, on_device(): lax.all_to_all(sent, 'grp', 0, 0, axis_index_groups=z_groups, tiled=True)  31.3 us
    ppermute x7, starting transfers between devices, hop(): return lax.ppermute(a, 'intra', ring)  18.4 us
    ppermute x7, waiting for transfers between devices, hop(): return lax.ppermute(a, 'intra', ring)  17 us
    ppermute x1, starting transfers between devices, on_device(): inputs = (mine, lax.ppermute(theirs, 'intra', swap), cotangent, slab)  12.4 us
    all_to_all x1, blocking collectives, on_device(): lax.all_to_all(own, 'grp', 0, 0, axis_index_groups=x_groups, tiled=True)  9.56 us
    all_to_all x1, blocking collectives, on_device(): lax.all_to_all(sent, 'grp', 0, 0, axis_index_groups=x_groups, tiled=True)  9.39 us
    ppermute x1, starting transfers between devices, on_device(): partner = lax.ppermute(stats, 'intra', swap)  9.01 us
    ppermute x1, starting transfers between devices, on_device(): other = lax.ppermute(give, 'intra', swap)  6.61 us
  transfers between devices with their start and end apart: 11, of which 9 were waited for; matrix products, arithmetic and copies ran while one was open for 1% of the time, Pallas kernels for 3%

profile of v8, /device:TPU:1, one launch (start us, length us, event | category | flops | bytes accessed | tf_op | source)
XLA Modules:
  0.0 143.2 jit_solution(13706830717656157332)
XLA Ops:
  0.6 2.3 %theirs.1.after_ref = bf16[128,3072]{1,0:T(8,128)(2,1)} custom-call(bf16[128,4096]{1,0:T(8,128)(2,1)} %x_ref.1, f32[1,4096]{1,0:T(1,128)} %bitcast.3, bf16[128,1024]{1,0:T(8,128)(2,1)} %c_ref.3), custom_call_target="tpu_custom_call" | custom-call | flops 524288 | bytes 2097152 | tf_op jit(solution)/shard_map/theirs/pallas_call | solution.py:52
  2.9 12.4 %collective-permute-start = (bf16[128,3072]{1,0:T(8,128)(2,1)}, bf16[128,3072]{1,0:T(8,128)(2,1)S(1)}, u32[]{:S(2)}, u32[]{:S(2)}) collective-permute-start(bf16[128,3072]{1,0:T(8,128)(2,1)} %theirs.1.after_ref), channel_id=1, source_target_pairs={{0,1},{1,0},{2,3},{3,2},{4,5},{5,4},{6,7},{7,6},{8,9},{9,8},{10,11... | collective-permute-start | bytes 2359304 | tf_op jit(solution)/shard_map/ppermute | solution.py:367
  19.4 1.9 %collective-permute-start.1 = (bf16[256,1024]{1,0:T(8,128)(2,1)S(1)}, bf16[256,1024]{1,0:T(8,128)(2,1)S(1)}, u32[]{:S(2)}, u32[]{:S(2)}) collective-permute-start(bf16[256,1024]{1,0:T(8,128)(2,1)S(1)} %get-tuple-element.25.outs_0_), channel_id=1, source_target_pairs={{0,2},{1,15},{2,4},{3,1},{4,6},{5,3},{6,8},{7,5},{8,10},{9,7},{10,... | collective-permute-start | bytes 1572872 | tf_op jit(solution)/shard_map/ppermute | solution.py:383
  21.3 1.9 %collective-permute-start.5 = (bf16[256,1024]{1,0:T(8,128)(2,1)S(1)}, bf16[256,1024]{1,0:T(8,128)(2,1)S(1)}, u32[]{:S(2)}, u32[]{:S(2)}) collective-permute-start(bf16[256,1024]{1,0:T(8,128)(2,1)S(1)} %get-tuple-element.29), channel_id=1, source_target_pairs={{0,2},{1,15},{2,4},{3,1},{4,6},{5,3},{6,8},{7,5},{8,10},{9,7},{10,... | collective-permute-start | bytes 1572872 | tf_op jit(solution)/shard_map/ppermute | solution.py:383
  23.2 1.8 %products.3 = (bf16[256,1024]{1,0:T(8,128)(2,1)S(1)}, bf16[256,1024]{1,0:T(8,128)(2,1)S(1)}, bf16[256,1024]{1,0:T(8,128)(2,1)S(1)}, bf16[256,1024]{1,0:T(8,128)(...) custom-call(bf16[128,2048]{1,0:T(8,128)(2,1)S(1)} %mine.1.x_ref, ...), custom_call_target="tpu_custom_call" | custom-call | flops 805306368 | bytes 6291456 | tf_op jit(solution)/shard_map/products/pallas_call | solution.py:109
  25.1 4.5 %collective-permute-done.1 = bf16[256,1024]{1,0:T(8,128)(2,1)S(1)} collective-permute-done((bf16[256,1024]{1,0:T(8,128)(2,1)S(1)}, bf16[256,1024]{1,0:T(8,128)(2,1)S(1)}, u32[]{:S(2)}, u32[]{:S(2)}) %collective-permute-start.1) | collective-permute-done | bytes 524320 | tf_op jit(solution)/shard_map/ppermute | solution.py:383
  29.8 2.8 %collective-permute-start.2 = (bf16[256,1024]{1,0:T(8,128)(2,1)S(1)}, bf16[256,1024]{1,0:T(8,128)(2,1)S(1)}, u32[]{:S(2)}, u32[]{:S(2)}) collective-permute-start(bf16[256,1024]{1,0:T(8,128)(2,1)S(1)} %add_convert_fusion.5), channel_id=1, source_target_pairs={{0,2},{1,15},{2,4},{3,1},{4,6},{5,3},{6,8},{7,5},{8,10},{9,7},{10,... | collective-permute-start | bytes 1572872 | tf_op jit(solution)/shard_map/ppermute | solution.py:383
  32.6 2.6 %collective-permute-done.5 = bf16[256,1024]{1,0:T(8,128)(2,1)S(1)} collective-permute-done((bf16[256,1024]{1,0:T(8,128)(2,1)S(1)}, bf16[256,1024]{1,0:T(8,128)(2,1)S(1)}, u32[]{:S(2)}, u32[]{:S(2)}) %collective-permute-start.5) | collective-permute-done | bytes 524320 | tf_op jit(solution)/shard_map/ppermute | solution.py:383
  35.4 2.8 %collective-permute-start.6 = (bf16[256,1024]{1,0:T(8,128)(2,1)S(1)}, bf16[256,1024]{1,0:T(8,128)(2,1)S(1)}, u32[]{:S(2)}, u32[]{:S(2)}) collective-permute-start(bf16[256,1024]{1,0:T(8,128)(2,1)S(1)} %add_convert_fusion.2), channel_id=1, source_target_pairs={{0,2},{1,15},{2,4},{3,1},{4,6},{5,3},{6,8},{7,5},{8,10},{9,7},{10,... | collective-permute-start | bytes 1572872 | tf_op jit(solution)/shard_map/ppermute | solution.py:383
  38.3 2.6 %collective-permute-done.2 = bf16[256,1024]{1,0:T(8,128)(2,1)S(1)} collective-permute-done((bf16[256,1024]{1,0:T(8,128)(2,1)S(1)}, bf16[256,1024]{1,0:T(8,128)(2,1)S(1)}, u32[]{:S(2)}, u32[]{:S(2)}) %collective-permute-start.2) | collective-permute-done | bytes 524320 | tf_op jit(solution)/shard_map/ppermute | solution.py:383
  41.0 2.9 %collective-permute-start.3 = (bf16[256,1024]{1,0:T(8,128)(2,1)S(1)}, bf16[256,1024]{1,0:T(8,128)(2,1)S(1)}, u32[]{:S(2)}, u32[]{:S(2)}) collective-permute-start(bf16[256,1024]{1,0:T(8,128)(2,1)S(1)} %add_convert_fusion.4), channel_id=1, source_target_pairs={{0,2},{1,15},{2,4},{3,1},{4,6},{5,3},{6,8},{7,5},{8,10},{9,7},{10,... | collective-permute-start | bytes 1572872 | tf_op jit(solution)/shard_map/ppermute | solution.py:383
  44.0 2.5 %collective-permute-done.6 = bf16[256,1024]{1,0:T(8,128)(2,1)S(1)} collective-permute-done((bf16[256,1024]{1,0:T(8,128)(2,1)S(1)}, bf16[256,1024]{1,0:T(8,128)(2,1)S(1)}, u32[]{:S(2)}, u32[]{:S(2)}) %collective-permute-start.6) | collective-permute-done | bytes 524320 | tf_op jit(solution)/shard_map/ppermute | solution.py:383
  46.7 2.9 %collective-permute-start.7 = (bf16[256,1024]{1,0:T(8,128)(2,1)S(1)}, bf16[256,1024]{1,0:T(8,128)(2,1)S(1)}, u32[]{:S(2)}, u32[]{:S(2)}) collective-permute-start(bf16[256,1024]{1,0:T(8,128)(2,1)S(1)} %add_convert_fusion.1), channel_id=1, source_target_pairs={{0,2},{1,15},{2,4},{3,1},{4,6},{5,3},{6,8},{7,5},{8,10},{9,7},{10,... | collective-permute-start | bytes 1572872 | tf_op jit(solution)/shard_map/ppermute | solution.py:383
  49.6 2.5 %collective-permute-done.3 = bf16[256,1024]{1,0:T(8,128)(2,1)S(1)} collective-permute-done((bf16[256,1024]{1,0:T(8,128)(2,1)S(1)}, bf16[256,1024]{1,0:T(8,128)(2,1)S(1)}, u32[]{:S(2)}, u32[]{:S(2)}) %collective-permute-start.3) | collective-permute-done | bytes 524320 | tf_op jit(solution)/shard_map/ppermute | solution.py:383
  52.3 3.0 %collective-permute-start.4 = (bf16[256,1024]{1,0:T(8,128)(2,1)S(1)}, bf16[256,1024]{1,0:T(8,128)(2,1)S(1)}, u32[]{:S(2)}, u32[]{:S(2)}) collective-permute-start(bf16[256,1024]{1,0:T(8,128)(2,1)S(1)} %add_convert_fusion.3), channel_id=1, source_target_pairs={{0,2},{1,15},{2,4},{3,1},{4,6},{5,3},{6,8},{7,5},{8,10},{9,7},{10,... | collective-permute-start | bytes 1572872 | tf_op jit(solution)/shard_map/ppermute | solution.py:383
  55.3 2.4 %collective-permute-done.7 = bf16[256,1024]{1,0:T(8,128)(2,1)S(1)} collective-permute-done((bf16[256,1024]{1,0:T(8,128)(2,1)S(1)}, bf16[256,1024]{1,0:T(8,128)(2,1)S(1)}, u32[]{:S(2)}, u32[]{:S(2)}) %collective-permute-start.7) | collective-permute-done | bytes 524320 | tf_op jit(solution)/shard_map/ppermute | solution.py:383
  58.7 6.6 %collective-permute-start.8 = (bf16[256,1024]{1,0:T(8,128)(2,1)}, bf16[256,1024]{1,0:T(8,128)(2,1)S(1)}, u32[]{:S(2)}, u32[]{:S(2)}) collective-permute-start(bf16[256,1024]{1,0:T(8,128)(2,1)} %add_convert_fusion), channel_id=1, source_target_pairs={{0,1},{1,0},{2,3},{3,2},{4,5},{5,4},{6,7},{7,6},{8,9},{9,8},{10,11... | collective-permute-start | bytes 1572872 | tf_op jit(solution)/shard_map/ppermute | solution.py:392
  67.2 9.6 %all_to_all.25.got_ref = bf16[4,512,128]{2,1,0:T(8,128)(2,1)S(1)} all-to-all(bf16[4,512,128]{2,1,0:T(8,128)(2,1)S(1)} %finish.1), channel_id=1, replica_groups={{0,16,32,48},{64,80,96,112},{128,144,160,176},{192,208,224,240},{256,27..., dimensions={0} | all-to-all | bytes 1048576 | tf_op jit(solution)/shard_map/all_to_all | solution.py:407
  76.8 17.9 %all_to_all.26.got_ref = bf16[12,48,128]{2,1,0:T(8,128)(2,1)S(1)} all-to-all(bf16[12,48,128]{2,1,0:T(8,128)(2,1)S(1)} %shard_map.94), channel_id=1, replica_groups={{0,64,128,192,256,320,384,448,512,576,640,704},{16,80,144,208,272,336,4..., dimensions={0} | all-to-all | bytes 294912 | tf_op jit(solution)/shard_map/all_to_all | solution.py:410
  94.7 13.4 %all_to_all.27.got_ref = bf16[12,48,128]{2,1,0:T(8,128)(2,1)S(1)} all-to-all(bf16[12,48,128]{2,1,0:T(8,128)(2,1)S(1)} %shard_map.95), channel_id=1, replica_groups={{0,64,128,192,256,320,384,448,512,576,640,704},{16,80,144,208,272,336,4..., dimensions={0} | all-to-all | bytes 294912 | tf_op jit(solution)/shard_map/all_to_all | solution.py:413
  108.2 9.4 %all_to_all.28.got_ref = bf16[4,528,128]{2,1,0:T(8,128)(2,1)S(1)} all-to-all(bf16[4,528,128]{2,1,0:T(8,128)(2,1)S(1)} %shard_map.96), channel_id=1, replica_groups={{0,16,32,48},{64,80,96,112},{128,144,160,176},{192,208,224,240},{256,27..., dimensions={0} | all-to-all | bytes 1081344 | tf_op jit(solution)/shard_map/all_to_all | solution.py:416
  117.7 9.0 %collective-permute-start.9 = (f32[16,128]{1,0:T(8,128)S(1)}, f32[16,128]{1,0:T(8,128)S(1)}, u32[]{:S(2)}, u32[]{:S(2)}) collective-permute-start(f32[16,128]{1,0:T(8,128)S(1)} %shard_map.97.a_ref), channel_id=1, source_target_pairs={{0,1},{1,0},{2,3},{3,2},{4,5},{5,4},{6,7},{7,6},{8,9},{9,8},{10,11... | collective-permute-start | bytes 24584 | tf_op jit(solution)/shard_map/ppermute | solution.py:420
  128.2 6.6 %all-to-all-start.4 = ((f32[8,16,128]{2,1,0:T(8,128)}), f32[8,16,128]{2,1,0:T(8,128)S(1)}, u32[]{:S(2)}, u32[]{:S(2)}) async-start(f32[8,16,128]{2,1,0:T(8,128)} %shard_map.98), calls=%async_computation.4 | async-start | bytes 131072 | tf_op jit(solution)/shard_map/all_to_all | solution.py:430
  136.6 5.4 %all-to-all-done.4.stats_ref = f32[8,16,128]{2,1,0:T(8,128)S(1)} async-done(((f32[8,16,128]{2,1,0:T(8,128)}), f32[8,16,128]{2,1,0:T(8,128)S(1)}, u32[]{:S(2)}, u32[]{:S(2)}) %all-to-all-start.4) | async-done | bytes 65568 | tf_op jit(solution)/shard_map/all_to_all | solution.py:430
  (38 shorter events, 12.6 us)
Async XLA Ops:
  0.6 14.7 %copy-start.4 = (f32[4096]{0:T(1024)S(1)}, f32[4096]{0:T(1024)}, u32[]{:S(2)}) copy-start(f32[4096]{0:T(1024)} %param.9) | copy-start | bytes 49156
  2.9 14.9 %collective-permute-start = (bf16[128,3072]{1,0:T(8,128)(2,1)}, bf16[128,3072]{1,0:T(8,128)(2,1)S(1)}, u32[]{:S(2)}, u32[]{:S(2)}) collective-permute-start(bf16[128,3072]{1,0:T(8,128)(2,1)} %theirs.1.after_ref), channel_id=1, source_target_pairs={{0,1},{1,0},{2,3},{3,2},{4,5},{5,4},{6,7},{7,6},{8,9},{9,8},{10,11... | collective-permute-start | bytes 2359304 | tf_op jit(solution)/shard_map/ppermute | solution.py:367
  15.3 1.2 copy-start
  16.6 1.1 copy-start.1
  17.7 0.9 copy-start.2
  19.4 10.2 %collective-permute-start.1 = (bf16[256,1024]{1,0:T(8,128)(2,1)S(1)}, bf16[256,1024]{1,0:T(8,128)(2,1)S(1)}, u32[]{:S(2)}, u32[]{:S(2)}) collective-permute-start(bf16[256,1024]{1,0:T(8,128)(2,1)S(1)} %get-tuple-element.25.outs_0_), channel_id=1, source_target_pairs={{0,2},{1,15},{2,4},{3,1},{4,6},{5,3},{6,8},{7,5},{8,10},{9,7},{10,... | collective-permute-start | bytes 1572872 | tf_op jit(solution)/shard_map/ppermute | solution.py:383
  21.3 13.9 %collective-permute-start.5 = (bf16[256,1024]{1,0:T(8,128)(2,1)S(1)}, bf16[256,1024]{1,0:T(8,128)(2,1)S(1)}, u32[]{:S(2)}, u32[]{:S(2)}) collective-permute-start(bf16[256,1024]{1,0:T(8,128)(2,1)S(1)} %get-tuple-element.29), channel_id=1, source_target_pairs={{0,2},{1,15},{2,4},{3,1},{4,6},{5,3},{6,8},{7,5},{8,10},{9,7},{10,... | collective-permute-start | bytes 1572872 | tf_op jit(solution)/shard_map/ppermute | solution.py:383
  29.8 11.0 %collective-permute-start.2 = (bf16[256,1024]{1,0:T(8,128)(2,1)S(1)}, bf16[256,1024]{1,0:T(8,128)(2,1)S(1)}, u32[]{:S(2)}, u32[]{:S(2)}) collective-permute-start(bf16[256,1024]{1,0:T(8,128)(2,1)S(1)} %add_convert_fusion.5), channel_id=1, source_target_pairs={{0,2},{1,15},{2,4},{3,1},{4,6},{5,3},{6,8},{7,5},{8,10},{9,7},{10,... | collective-permute-start | bytes 1572872 | tf_op jit(solution)/shard_map/ppermute | solution.py:383
  35.4 11.0 %collective-permute-start.6 = (bf16[256,1024]{1,0:T(8,128)(2,1)S(1)}, bf16[256,1024]{1,0:T(8,128)(2,1)S(1)}, u32[]{:S(2)}, u32[]{:S(2)}) collective-permute-start(bf16[256,1024]{1,0:T(8,128)(2,1)S(1)} %add_convert_fusion.2), channel_id=1, source_target_pairs={{0,2},{1,15},{2,4},{3,1},{4,6},{5,3},{6,8},{7,5},{8,10},{9,7},{10,... | collective-permute-start | bytes 1572872 | tf_op jit(solution)/shard_map/ppermute | solution.py:383
  41.0 11.0 %collective-permute-start.3 = (bf16[256,1024]{1,0:T(8,128)(2,1)S(1)}, bf16[256,1024]{1,0:T(8,128)(2,1)S(1)}, u32[]{:S(2)}, u32[]{:S(2)}) collective-permute-start(bf16[256,1024]{1,0:T(8,128)(2,1)S(1)} %add_convert_fusion.4), channel_id=1, source_target_pairs={{0,2},{1,15},{2,4},{3,1},{4,6},{5,3},{6,8},{7,5},{8,10},{9,7},{10,... | collective-permute-start | bytes 1572872 | tf_op jit(solution)/shard_map/ppermute | solution.py:383
  46.7 11.0 %collective-permute-start.7 = (bf16[256,1024]{1,0:T(8,128)(2,1)S(1)}, bf16[256,1024]{1,0:T(8,128)(2,1)S(1)}, u32[]{:S(2)}, u32[]{:S(2)}) collective-permute-start(bf16[256,1024]{1,0:T(8,128)(2,1)S(1)} %add_convert_fusion.1), channel_id=1, source_target_pairs={{0,2},{1,15},{2,4},{3,1},{4,6},{5,3},{6,8},{7,5},{8,10},{9,7},{10,... | collective-permute-start | bytes 1572872 | tf_op jit(solution)/shard_map/ppermute | solution.py:383
  52.3 14.3 %collective-permute-start.4 = (bf16[256,1024]{1,0:T(8,128)(2,1)S(1)}, bf16[256,1024]{1,0:T(8,128)(2,1)S(1)}, u32[]{:S(2)}, u32[]{:S(2)}) collective-permute-start(bf16[256,1024]{1,0:T(8,128)(2,1)S(1)} %add_convert_fusion.3), channel_id=1, source_target_pairs={{0,2},{1,15},{2,4},{3,1},{4,6},{5,3},{6,8},{7,5},{8,10},{9,7},{10,... | collective-permute-start | bytes 1572872 | tf_op jit(solution)/shard_map/ppermute | solution.py:383
  57.7 7.6 %copy-start.7 = (s32[128,1]{0,1:T(1,128)S(1)}, s32[128,1]{0,1:T(1,128)}, u32[]{:S(2)}) copy-start(s32[128,1]{0,1:T(1,128)} %param.13) | copy-start | bytes 1540
  58.7 6.7 %copy-start.6 = (f32[1,1,4,16]{3,2,1,0:T(4,128)S(1)}, f32[1,1,4,16]{3,2,1,0:T(4,128)}, u32[]{:S(2)}) copy-start(f32[1,1,4,16]{3,2,1,0:T(4,128)} %param.11) | copy-start | bytes 772
  58.7 8.3 %collective-permute-start.8 = (bf16[256,1024]{1,0:T(8,128)(2,1)}, bf16[256,1024]{1,0:T(8,128)(2,1)S(1)}, u32[]{:S(2)}, u32[]{:S(2)}) collective-permute-start(bf16[256,1024]{1,0:T(8,128)(2,1)} %add_convert_fusion), channel_id=1, source_target_pairs={{0,1},{1,0},{2,3},{3,2},{4,5},{5,4},{6,7},{7,6},{8,9},{9,8},{10,11... | collective-permute-start | bytes 1572872 | tf_op jit(solution)/shard_map/ppermute | solution.py:392
  117.7 9.8 %collective-permute-start.9 = (f32[16,128]{1,0:T(8,128)S(1)}, f32[16,128]{1,0:T(8,128)S(1)}, u32[]{:S(2)}, u32[]{:S(2)}) collective-permute-start(f32[16,128]{1,0:T(8,128)S(1)} %shard_map.97.a_ref), channel_id=1, source_target_pairs={{0,1},{1,0},{2,3},{3,2},{4,5},{5,4},{6,7},{7,6},{8,9},{9,8},{10,11... | collective-permute-start | bytes 24584 | tf_op jit(solution)/shard_map/ppermute | solution.py:420
  128.2 13.8 %all-to-all-start.4 = ((f32[8,16,128]{2,1,0:T(8,128)}), f32[8,16,128]{2,1,0:T(8,128)S(1)}, u32[]{:S(2)}, u32[]{:S(2)}) async-start(f32[8,16,128]{2,1,0:T(8,128)} %shard_map.98), calls=%async_computation.4 | async-start | bytes 131072 | tf_op jit(solution)/shard_map/all_to_all | solution.py:430
  134.8 7.2 %copy-start.3 = (bf16[256,1024]{1,0:T(8,128)(2,1)S(1)}, bf16[256,1024]{1,0:T(8,128)(2,1)}, u32[]{:S(2)}) copy-start(bf16[256,1024]{1,0:T(8,128)(2,1)} %weight_ref.1) | copy-start | bytes 1572868
  134.8 7.2 %copy-start.5 = (f32[8,128]{1,0:T(8,128)S(1)}, f32[8,128]{1,0:T(8,128)}, u32[]{:S(2)}) copy-start(f32[8,128]{1,0:T(8,128)} %state_ref.1) | copy-start | bytes 12292
